TPU v7x, 256 devices: a whole 4x4x8 slice. The times are simulated.
256 devices in a mesh: chan: 64 (over z, y, core), stn: 4 (over x).
Axes of the slice: x: 4, y: 4, z: 8, core: 2. Of those that a mesh axis runs over, the one named last changes fastest.
Arguments:
- visibilities: bfloat16 [2, 256, 512, 512], P(None, 'chan', 'stn'), may hold values from -140 to 140
- calibrator: float32 [256], P('chan'), may hold values from 20 to 40
- catalog: float32 [5, 65536], P(None, 'chan'), may hold values from -2 to 2, as said below
- assignment: int32 [65536, 1], replicated, may hold values from 0 to 63; in each aligned block of 1024 rows (0 to 1023, 1024 to 2047, ...) at most 32 rows name the same one
- stations: float32 [2, 512], replicated, may hold values from -150 to 150
- input_order: int32 [512], replicated, may hold values from 0 to 511, each once
- station_flags: int32 [512], replicated, may hold values 0 or 1
Outputs:
- gains: float32 [2, 256, 512], P(None, 'chan', 'stn')
- residual: bfloat16 [2, 256, 512, 512], P(None, 'chan', 'stn')
- changes: float32 [3, 256], P(None, 'chan')
Inputs may be any that keep to these rules, and one draw needn't show every extreme that they name: `assignment`: of the 1024 sources on one index of chan, at most 32 belong to any one channel block. `catalog`: rows l and m lie within -0.1 to 0.1, flux within 0.02 to 0.5, spectral index within -1.2 to 0.2, curvature within -2 to 2.
All inputs are finite; a program needn't handle non-finite values.
Results may differ from a plain program's by a relative error of at most 0.0039.
Values sent between devices are 32-bit elements; how exact they have to be, the bound alone decides.
No kernel may reach another device: no remote copies, remote signals or barrier semaphores. Data moves between devices by JAX's collectives and lax.ppermute only.
A program may use at most 64 MiB of HBM per device.

v0:
```python
import jax
import jax.numpy as jnp
from jax import lax
from jax.sharding import PartitionSpec as P

ITERS = 3


def predict(components, placed, frequency, bright_centre, row_start, row_count):
    phase_angle = (
        2.0
        * jnp.pi
        * frequency
        * (
            components[0][:, None] * placed[0][None, :]
            + components[1][:, None] * placed[1][None, :]
        )
    )
    cosine = jnp.cos(phase_angle)
    sine_part = jnp.sin(phase_angle)
    log_freq = jnp.log(frequency)
    brightness = components[2] * jnp.exp(log_freq * (components[3] + components[4] * log_freq))
    right_side = jnp.concatenate(
        [brightness[:, None] * cosine, brightness[:, None] * sine_part], axis=0
    ).astype(jnp.bfloat16)
    cos_rows = lax.dynamic_slice_in_dim(cosine, row_start, row_count, 1).astype(jnp.bfloat16)
    sin_rows = lax.dynamic_slice_in_dim(sine_part, row_start, row_count, 1).astype(jnp.bfloat16)
    left_side = jnp.concatenate(
        [
            jnp.concatenate([cos_rows, sin_rows], axis=0),
            jnp.concatenate([sin_rows, -cos_rows], axis=0),
        ],
        axis=1,
    )
    model_full = lax.dot_general(
        left_side, right_side, (((0,), (0,)), ((), ())), preferred_element_type=jnp.float32
    )
    return (model_full[:row_count] + bright_centre, model_full[row_count:])


def per_device(visibilities, calibrator, catalog, assignment, stations, input_order, station_flags):
    chan_count = lax.axis_size("chan")
    chan_index = lax.axis_index("chan")
    stn_index = lax.axis_index("stn")
    local_chans = visibilities.shape[1]
    row_count = visibilities.shape[2]
    station_count = visibilities.shape[3]
    source_dev = catalog.shape[1]
    capacity = 2 * source_dev // chan_count
    flat_assign = assignment[:, 0]
    source_ids = jnp.arange(source_dev, dtype=jnp.int32)
    whole_catalog = lax.all_gather(catalog, "chan", axis=1, tiled=True)
    in_block = (flat_assign == chan_index).astype(jnp.float32).reshape(chan_count, source_dev)
    upper_tri = (source_ids[:, None] <= source_ids[None, :]).astype(jnp.float32)
    running = jnp.dot(
        in_block, upper_tri, precision=lax.Precision.HIGHEST, preferred_element_type=jnp.float32
    )
    slot_ids = jnp.arange(capacity, dtype=jnp.float32)
    selector = in_block[:, :, None] * (running[:, :, None] - 1.0 == slot_ids[None, None, :]).astype(
        jnp.float32
    )
    block_rows = whole_catalog.reshape(5, chan_count, source_dev)
    components = jnp.einsum(
        "fos,osr->for", block_rows, selector, precision=lax.Precision.HIGHEST
    ).reshape(5, chan_count * capacity)
    station_ids = jnp.arange(station_count, dtype=jnp.int32)
    order_hot = (input_order[:, None] == station_ids[None, :]).astype(jnp.float32)
    placed = jnp.dot(
        stations, order_hot.T, precision=lax.Precision.HIGHEST, preferred_element_type=jnp.float32
    )
    station_ok = jnp.dot(
        order_hot,
        station_flags.astype(jnp.float32),
        precision=lax.Precision.HIGHEST,
        preferred_element_type=jnp.float32,
    )
    row_start = stn_index * row_count
    channel_ids = chan_index * local_chans + jnp.arange(local_chans, dtype=jnp.int32)
    frequency = 1.0 + 0.5 * channel_ids.astype(jnp.float32) / (local_chans * chan_count)

    def one_channel(inputs):
        return predict(components, placed, inputs[0], inputs[1], row_start, row_count)

    model_real, model_imag = lax.map(one_channel, (frequency, calibrator))
    column_ids = jnp.arange(station_count, dtype=jnp.int32)
    row_ids = row_start + jnp.arange(row_count, dtype=jnp.int32)
    row_ok = lax.dynamic_slice_in_dim(station_ok, row_start, row_count)
    pair_weight = (
        row_ok[:, None]
        * station_ok[None, :]
        * (row_ids[:, None] != column_ids[None, :]).astype(jnp.float32)
    )
    vis_real = visibilities[0].astype(jnp.float32)
    vis_imag = visibilities[1].astype(jnp.float32)
    full_real = jnp.ones((local_chans, station_count), jnp.float32)
    full_imag = jnp.zeros((local_chans, station_count), jnp.float32)
    local_real = jnp.ones((local_chans, row_count), jnp.float32)
    local_imag = jnp.zeros((local_chans, row_count), jnp.float32)
    history = []
    for iteration in range(ITERS):
        weight_real = full_real[:, None, :] * model_real + full_imag[:, None, :] * model_imag
        weight_imag = full_real[:, None, :] * model_imag - full_imag[:, None, :] * model_real
        top_real = jnp.sum(pair_weight * (weight_real * vis_real + weight_imag * vis_imag), axis=2)
        top_imag = jnp.sum(pair_weight * (weight_real * vis_imag - weight_imag * vis_real), axis=2)
        bottom = (
            jnp.sum(pair_weight * (weight_real * weight_real + weight_imag * weight_imag), axis=2)
            + 1e-06
            + (1.0 - row_ok)
        )
        new_real = top_real / bottom
        new_imag = top_imag / bottom
        if iteration % 2 == 1:
            new_real = 0.5 * (new_real + local_real)
            new_imag = 0.5 * (new_imag + local_imag)
        gathered = lax.all_gather(jnp.stack([new_real, new_imag]), "stn", axis=2, tiled=True)
        part_moved = jnp.sum((new_real - local_real) ** 2 + (new_imag - local_imag) ** 2, axis=1)
        part_total = jnp.sum(new_real * new_real + new_imag * new_imag, axis=1)
        norm_moved, norm_total = lax.psum((part_moved, part_total), "stn")
        history.append(norm_moved / (norm_total + 1e-06))
        local_real = new_real
        local_imag = new_imag
        full_real = gathered[0]
        full_imag = gathered[1]
    pair_real = (
        local_real[:, :, None] * full_real[:, None, :]
        + local_imag[:, :, None] * full_imag[:, None, :]
    )
    pair_imag = (
        local_imag[:, :, None] * full_real[:, None, :]
        - local_real[:, :, None] * full_imag[:, None, :]
    )
    res_real = pair_weight * (vis_real - (pair_real * model_real - pair_imag * model_imag))
    res_imag = pair_weight * (vis_imag - (pair_real * model_imag + pair_imag * model_real))
    gains = jnp.stack([local_real, local_imag])
    residual = jnp.stack([res_real, res_imag]).astype(jnp.bfloat16)
    return (gains, residual, jnp.stack(history))


def solution(mesh):
    placed = (P(None, "chan", "stn", None), P("chan"), P(None, "chan"), P(), P(), P(), P())
    return jax.shard_map(
        per_device,
        mesh=mesh,
        in_specs=placed,
        out_specs=(P(None, "chan", "stn"), P(None, "chan", "stn", None), P(None, "chan")),
        check_vma=False,
    )
```

profile of v0, /device:TPU:2, one launch (start us, length us, event | category | flops | bytes accessed | tf_op | source)
XLA Modules:
  0.0 306.4 jit_solution(12277074474041384659)
XLA Ops:
  7.2 0.0 copy-start
  7.2 0.0 copy-start.3
  7.2 0.0 all-gather.2.cloned.1.call-start
  7.2 0.7 all-gather.2.cloned.1.call-update
  7.9 1.7 compare_reduce_fusion
  9.6 0.1 eq.45
  9.8 0.7 convert_element_type.43
  10.5 1.3 fusion.49
  11.8 0.1 broadcast_subtract_fusion
  11.9 0.4 fusion.23
  12.3 0.0 copy-done
  12.3 0.0 copy-done.3
  12.3 0.6 convolution_bitcast_fusion
  12.9 0.1 multiply_select_fusion
  13.0 78.3 %all-gather.2.cloned.1.call-done = f32[5,65536]{1,0:T(8,128)} async-done(((f32[5,1024]{1,0:T(8,128)}), f32[5,65536]{1,0:T(8,128)}) %all-gather.2.cloned.1.call-update) | async-done | bytes 1310736 | tf_op jit(solution)/shard_map/all_gather | solution.py:52
  91.3 9.2 %fusion.24 = f32[5,64,32]{2,0,1:T(8,128)S(1)} fusion(f32[5,64,1024]{2,0,1:T(8,128)} %bitcast.139, f32[64,1024]{1,0:T(8,128)S(1)} %convert_element_type.45, f32[64,1024]{1,0:T(8,128)S(1)} %fusion.23), kind=kOutput, calls=%fused_computation.48 | convolution fusion | flops 130023424 | bytes 1875968 | tf_op jit(solution)/shard_map/fos,osr->for/dot_general | solution.py:63
  100.6 0.1 reshape.431
  100.7 0.1 broadcast.348
  100.9 0.1 broadcast.348.clone
  101.0 0.2 copy-done.4
  101.2 151.7 %while.14 = (s32[]{:T(128)}, f32[4,128,512]{2,1,0:T(8,128)S(1)}, f32[4,128,512]{2,1,0:T(8,128)S(1)}, f32[4]{0:T(128)S(1)}, f32[5,2048]{1,0:T(8,128)S(1)}, /*inde...) while((s32[]{:T(128)}, f32[4,128,512]{2,1,0:T(8,128)S(1)}, ...), condition=%wide.region_1.2_spmd, body=%wide.region_0.1_spmd.sunk | while | flops 1106059264 | bytes 18473128 | solution.py:84
  101.2 0.6 dynamic_slice.31
  103.2 16.3 %fusion.81 = (bf16[2048,512]{1,0:T(8,128)(2,1)S(1)}, bf16[2048,512]{1,0:T(8,128)(2,1)S(1)}) fusion(f32[512]{0:T(512)S(1)} %bitcast.134, f32[2048]{0:T(1024)S(1)} %bitcast.129, f32[512]{0:T(512)S(1)} %bitcast.132, f32[2048]{0:T(1024)S(1)} %bitcast.127, f32[]{:T(128)} %bitcast.125), kind=kLoop, calls=%fused_computation.7.clone.2 | loop fusion | flops 6291456 | bytes 4214788 | tf_op jit(solution)/shard_map/while/body/eval_jaxpr/sin | solution.py:20
  119.5 0.3 fusion.82
  119.8 16.8 %multiply_convert_fusion.3 = (bf16[2048,512]{1,0:T(8,128)(2,1)S(1)}, bf16[2048,512]{1,0:T(8,128)(2,1)S(1)}) fusion(f32[2048]{0:T(1024)S(1)} %bitcast.131, f32[512]{0:T(512)S(1)} %bitcast.135, f32[2048]{0:T(1024)S(1)} %bitcast.130, f32[512]{0:T(512)S(1)} %bitcast.133, f32[2048]{0:T(1024)S(1)} %bitcast.128, f32[]{:T(128)} %bitcast.125), kind=kLoop, calls=%fused_computation.5.clone.1 | loop fusion | flops 8388608 | bytes 4222980 | tf_op jit(solution)/shard_map/convert
  136.6 1.3 fusion.83
  137.9 0.6 dynamic_slice.32
  138.5 0.7 fusion.84
  139.2 0.6 dynamic_slice.31
  141.2 16.3 %fusion.81 = (bf16[2048,512]{1,0:T(8,128)(2,1)S(1)}, bf16[2048,512]{1,0:T(8,128)(2,1)S(1)}) fusion(f32[512]{0:T(512)S(1)} %bitcast.134, f32[2048]{0:T(1024)S(1)} %bitcast.129, f32[512]{0:T(512)S(1)} %bitcast.132, f32[2048]{0:T(1024)S(1)} %bitcast.127, f32[]{:T(128)} %bitcast.125), kind=kLoop, calls=%fused_computation.7.clone.2 | loop fusion | flops 6291456 | bytes 4214788 | tf_op jit(solution)/shard_map/while/body/eval_jaxpr/sin | solution.py:20
  157.4 0.3 fusion.82
  157.7 16.8 %multiply_convert_fusion.3 = (bf16[2048,512]{1,0:T(8,128)(2,1)S(1)}, bf16[2048,512]{1,0:T(8,128)(2,1)S(1)}) fusion(f32[2048]{0:T(1024)S(1)} %bitcast.131, f32[512]{0:T(512)S(1)} %bitcast.135, f32[2048]{0:T(1024)S(1)} %bitcast.130, f32[512]{0:T(512)S(1)} %bitcast.133, f32[2048]{0:T(1024)S(1)} %bitcast.128, f32[]{:T(128)} %bitcast.125), kind=kLoop, calls=%fused_computation.5.clone.1 | loop fusion | flops 8388608 | bytes 4222980 | tf_op jit(solution)/shard_map/convert
  174.5 1.3 fusion.83
  175.8 0.6 dynamic_slice.32
  176.4 0.7 fusion.84
  177.1 0.6 dynamic_slice.31
  179.1 16.3 %fusion.81 = (bf16[2048,512]{1,0:T(8,128)(2,1)S(1)}, bf16[2048,512]{1,0:T(8,128)(2,1)S(1)}) fusion(f32[512]{0:T(512)S(1)} %bitcast.134, f32[2048]{0:T(1024)S(1)} %bitcast.129, f32[512]{0:T(512)S(1)} %bitcast.132, f32[2048]{0:T(1024)S(1)} %bitcast.127, f32[]{:T(128)} %bitcast.125), kind=kLoop, calls=%fused_computation.7.clone.2 | loop fusion | flops 6291456 | bytes 4214788 | tf_op jit(solution)/shard_map/while/body/eval_jaxpr/sin | solution.py:20
  195.4 0.3 fusion.82
  195.6 16.8 %multiply_convert_fusion.3 = (bf16[2048,512]{1,0:T(8,128)(2,1)S(1)}, bf16[2048,512]{1,0:T(8,128)(2,1)S(1)}) fusion(f32[2048]{0:T(1024)S(1)} %bitcast.131, f32[512]{0:T(512)S(1)} %bitcast.135, f32[2048]{0:T(1024)S(1)} %bitcast.130, f32[512]{0:T(512)S(1)} %bitcast.133, f32[2048]{0:T(1024)S(1)} %bitcast.128, f32[]{:T(128)} %bitcast.125), kind=kLoop, calls=%fused_computation.5.clone.1 | loop fusion | flops 8388608 | bytes 4222980 | tf_op jit(solution)/shard_map/convert
  212.5 1.3 fusion.83
  213.7 0.6 dynamic_slice.32
  214.3 0.7 fusion.84
  215.0 0.6 dynamic_slice.31
  217.0 16.3 %fusion.81 = (bf16[2048,512]{1,0:T(8,128)(2,1)S(1)}, bf16[2048,512]{1,0:T(8,128)(2,1)S(1)}) fusion(f32[512]{0:T(512)S(1)} %bitcast.134, f32[2048]{0:T(1024)S(1)} %bitcast.129, f32[512]{0:T(512)S(1)} %bitcast.132, f32[2048]{0:T(1024)S(1)} %bitcast.127, f32[]{:T(128)} %bitcast.125), kind=kLoop, calls=%fused_computation.7.clone.2 | loop fusion | flops 6291456 | bytes 4214788 | tf_op jit(solution)/shard_map/while/body/eval_jaxpr/sin | solution.py:20
  233.3 0.3 fusion.82
  233.6 16.8 %multiply_convert_fusion.3 = (bf16[2048,512]{1,0:T(8,128)(2,1)S(1)}, bf16[2048,512]{1,0:T(8,128)(2,1)S(1)}) fusion(f32[2048]{0:T(1024)S(1)} %bitcast.131, f32[512]{0:T(512)S(1)} %bitcast.135, f32[2048]{0:T(1024)S(1)} %bitcast.130, f32[512]{0:T(512)S(1)} %bitcast.133, f32[2048]{0:T(1024)S(1)} %bitcast.128, f32[]{:T(128)} %bitcast.125), kind=kLoop, calls=%fused_computation.5.clone.1 | loop fusion | flops 8388608 | bytes 4222980 | tf_op jit(solution)/shard_map/convert
  250.4 1.3 fusion.83
  251.6 0.6 dynamic_slice.32
  252.2 0.7 fusion.84
  252.9 1.2 fusion.29
  254.2 10.7 %all_gather.13 = f32[2,4,512]{2,1,0:T(4,128)S(1)} all-gather(f32[2,4,128]{2,1,0:T(4,128)S(1)} %pad_maximum_fusion.1), channel_id=1, replica_groups=mesh['chan'=64,'stn'=4] {'stn'}, dimensions={2}, use_global_device_ids=true | all-gather | bytes 20480 | tf_op jit(solution)/shard_map/all_gather | solution.py:115
  264.9 0.3 multiply_add_fusion.2
  265.2 1.0 fusion.35
  266.2 10.1 %all_gather.14 = f32[2,4,512]{2,1,0:T(4,128)S(1)} all-gather(f32[2,4,128]{2,1,0:T(4,128)S(1)} %pad_maximum_fusion.2), channel_id=1, replica_groups=mesh['chan'=64,'stn'=4] {'stn'}, dimensions={2}, use_global_device_ids=true | all-gather | bytes 20480 | tf_op jit(solution)/shard_map/all_gather | solution.py:115
  276.4 0.3 multiply_add_fusion.1
  276.7 1.0 fusion.41
  277.7 0.0 copy-start.2
  277.7 10.1 %all_gather.15 = f32[2,4,512]{2,1,0:T(4,128)S(1)} all-gather(f32[2,4,128]{2,1,0:T(4,128)S(1)} %pad_maximum_fusion.3), channel_id=1, replica_groups=mesh['chan'=64,'stn'=4] {'stn'}, dimensions={2}, use_global_device_ids=true | all-gather | bytes 20480 | tf_op jit(solution)/shard_map/all_gather | solution.py:115
  287.8 0.2 add_reduce_fusion.4
  288.0 9.2 %all-reduce = (f32[4]{0:T(128)S(1)}, f32[4]{0:T(128)S(1)}, f32[4]{0:T(128)S(1)}, f32[4]{0:T(128)S(1)}, f32[4]{0:T(128)S(1)}, /*index=5*/f32[4]{0:T(128)S(1)}) all-reduce(f32[4]{0:T(128)S(1)} %get-tuple-element.114, f32[4]{0:T(128)S(1)} %get-tuple-element.115, ...), channel_id=1, replica_groups=mesh['chan'=64,'stn'=4] {'stn'}, use_global_device_ids=true, to_apply=%region_20.21 | all-reduce | flops 24 | bytes 192 | tf_op jit(solution)/shard_map/psum | solution.py:118
  297.2 0.7 fusion.52
  297.9 0.0 copy-done.2
  297.9 1.1 pad_maximum_fusion
  299.0 0.6 pad_maximum_fusion.4
  (27 shorter events, 0.4 us)
Async XLA Ops:
  7.2 5.1 %copy-start = (f32[2,512]{1,0:T(2,128)S(1)}, f32[2,512]{1,0:T(2,128)}, u32[]{:S(2)}) copy-start(f32[2,512]{1,0:T(2,128)} %param.13) | copy-start | bytes 12292
  7.2 5.1 %copy-start.3 = (s32[512]{0:T(512)S(1)}, s32[512]{0:T(512)}, u32[]{:S(2)}) copy-start(s32[512]{0:T(512)} %param.14) | copy-start | bytes 6148
  7.2 84.2 %all-gather.2.cloned.1.call-start = ((), (), s32[]{:S(2)}) async-start(), calls=%async_computation | async-start | bytes 2129920 | tf_op jit(solution)/shard_map/all_gather | solution.py:52
  100.6 0.7 copy-start.4
  101.2 151.7 %copy-start.1 = (bf16[2,4,128,512]{3,2,1,0:T(8,128)(2,1)S(1)}, bf16[2,4,128,512]{3,2,1,0:T(8,128)(2,1)}, u32[]{:S(2)}) copy-start(bf16[2,4,128,512]{3,2,1,0:T(8,128)(2,1)} %param.9) | copy-start | bytes 3145732
  277.7 20.3 %copy-start.2 = (f32[2,4,128]{2,1,0:T(4,128)}, f32[2,4,128]{2,1,0:T(4,128)S(1)}, u32[]{:S(2)}) copy-start(f32[2,4,128]{2,1,0:T(4,128)S(1)} %pad_maximum_fusion.3) | copy-start | bytes 12292
Sparse Core Ops, SparseCore 0:
  10.8 80.5 all-gather.1
where the time goes:
time: 307 us; the launch traced here: 306 us
  other arithmetic  145 us (47%)
  waiting for transfers between devices  79 us (26%)
  blocking collectives  40.1 us (13%)
  matrix products  16.6 us (5%)
  between operations  14.2 us (5%)
  loops' own time  5.61 us (2%)
  local copies, waits for them, and re-layouts  5.47 us (2%)
    all_gather x1, waiting for transfers between devices, per_device(): whole_catalog = lax.all_gather(catalog, 'chan', axis=1, tiled=True)  78.3 us
    another operation x4, other arithmetic  67.2 us
    sin x4, other arithmetic, predict(): sine_part = jnp.sin(phase_angle)  65.2 us
    all_gather x3, blocking collectives, per_device(): lax.all_gather(jnp.stack([new_real, new_imag]), 'stn', axis=2, tiled=True)  30.9 us
    dot_general x1, matrix products, per_device(): jnp.einsum('fos,osr->for', block_rows, selector, precision=lax.Precision....  9.22 us
    psum x1, blocking collectives, per_device(): norm_moved, norm_total = lax.psum((part_moved, part_total), 'stn')  9.19 us
  transfers between devices with their start and end apart: 1, of which 1 were waited for; matrix products, arithmetic and copies ran while one was open for 2% of the time, Pallas kernels for 0%

commit v1 on v0

v1 whole, which is shorter than its diff:
```python
import jax
import jax.numpy as jnp
from jax import lax
from jax.experimental import pallas as pl
from jax.experimental.pallas import tpu as pltpu
from jax.sharding import PartitionSpec as P

ITERS = 3
CAP = 32
VMEM = pltpu.VMEM
F32 = jnp.float32
BF16 = jnp.bfloat16
NT = (((1,), (1,)), ((), ()))

SIN_HALF = (3.141582005383235, -5.167142124470761, 2.541892570102862, -0.5546189642693115)
COS_HALF = (
    0.999999953374577,
    -4.934792843915727,
    4.05841155956257,
    -1.3318775116821093,
    0.2196907395767838,
)
SIN_STEP = (1.9999932214850844, -0.33258196069982343)
COS_STEP = (1.9999999959214183, -0.9999979659209961, 0.08318303377955542)
ROUND = 12582912.0


def horner(coefficients, x):
    total = coefficients[-1]
    for c in coefficients[-2::-1]:
        total = total * x + c
    return total


def split3(x):
    high = x.astype(BF16).astype(F32)
    rest = x - high
    middle = rest.astype(BF16).astype(F32)
    return high, middle, rest - middle


def spread_kernel(vis_ref, *out_refs):
    k = lax.axis_index("stn")
    for s in range(4):
        out_refs[s][...] = vis_ref[:, lax.rem(k + s, 4)].astype(F32)


def route_kernel(assign_ref, cat_ref, st_ref, order_ref, flag_ref, send_ref, xb_ref, yb_ref, ok_ref, own, sem):
    c = lax.axis_index("chan")
    copy = pltpu.make_async_copy(assign_ref.at[pl.ds(pl.multiple_of(c * 8, 8), 8)], own, sem)
    copy.start()
    n = order_ref.shape[1]
    hot = (lax.broadcasted_iota(jnp.int32, (n, n), 0) == order_ref[...]).astype(F32).astype(BF16)
    high, middle, low = split3(st_ref[...])
    rows = jnp.concatenate([high, middle, low, flag_ref[...].astype(F32), jnp.zeros((9, n), F32)], axis=0)
    placed = jnp.dot(rows.astype(BF16), hot, preferred_element_type=F32)
    middle_nu = 1.0 + (4.0 * c.astype(F32) + 1.5) * (1.0 / 512.0)
    x = (placed[0:1] + placed[2:3] + placed[4:5]) * middle_nu
    y = (placed[1:2] + placed[3:4] + placed[5:6]) * middle_nu
    ok_ref[...] = jnp.broadcast_to(placed[6:7], ok_ref.shape)
    for b in range(n // 128):
        cols = slice(128 * b, 128 * b + 128)
        xb_ref[cols] = jnp.broadcast_to(x[:, cols], (128, 128)).T
        yb_ref[cols] = jnp.broadcast_to(y[:, cols], (128, 128)).T
    copy.wait()
    blocks = lax.broadcasted_iota(jnp.int32, (64, 128), 0)
    hits = [(blocks == own[t : t + 1]).astype(F32) for t in range(8)]
    stacked = jnp.concatenate(hits, axis=0).astype(BF16)
    upper = lax.broadcasted_iota(jnp.int32, (128, 128), 0) <= lax.broadcasted_iota(jnp.int32, (128, 128), 1)
    running = jnp.dot(stacked, upper.astype(F32).astype(BF16), preferred_element_type=F32)
    totals = jnp.dot(stacked, jnp.ones((128, 128), BF16), preferred_element_type=F32)
    before = jnp.full((64, 128), -1.0, F32)
    slot = lax.broadcasted_iota(jnp.int32, (CAP, 128), 0).astype(F32)
    pieces = split3(cat_ref[...])
    left, right = [], []
    for t in range(8):
        part = slice(64 * t, 64 * t + 64)
        rank = jnp.sum(hits[t] * (running[part] + before), axis=0, keepdims=True)
        before = before + totals[part]
        chosen = slot == rank
        hit = hits[t].astype(BF16)
        for piece in pieces:
            left.append(hit)
            here = piece[:, 128 * t : 128 * t + 128]
            right.append(
                jnp.concatenate([jnp.where(chosen, here[f : f + 1], 0.0) for f in range(5)], axis=0).astype(BF16)
            )
    sent = lax.dot_general(
        jnp.concatenate(left, axis=1), jnp.concatenate(right, axis=1), NT, preferred_element_type=F32
    )
    send_ref[:, 0, :] = sent


def phasor_kernel(comp_ref, xb_ref, yb_ref, right_ref, left_ref, model_ref, wide, mine):
    width = comp_ref.shape[1]
    c = lax.axis_index("chan")
    k = lax.axis_index("stn")
    rows = mine.shape[0]
    quarter = rows // 4
    base = 1.0 + 4.0 * c.astype(F32) * (1.0 / 512.0)
    middle_nu = 1.0 + (4.0 * c.astype(F32) + 1.5) * (1.0 / 512.0)
    step = jnp.full((1, 128), 2.0 * jnp.pi / 1024.0, F32) / middle_nu
    wide[0] = jnp.broadcast_to(comp_ref[0:1], (16, width))
    wide[1] = jnp.broadcast_to(comp_ref[1:2], (16, width))
    for ch in range(4):
        log_nu = jnp.log(jnp.full((1, width), 1.0, F32) * (base + ch / 512.0))
        bright = comp_ref[2:3] * jnp.exp(log_nu * (comp_ref[3:4] + comp_ref[4:5] * log_nu))
        wide[2 + ch] = jnp.broadcast_to(bright, (16, width))

    def block(r0, l0, channel):
        x = xb_ref[pl.ds(r0, 16)]
        y = yb_ref[pl.ds(r0, 16)]
        for j in range(width // 128):
            at = slice(128 * j, 128 * j + 128)
            turns = wide[0, :, at] * x + wide[1, :, at] * y
            r = turns - ((turns + ROUND) - ROUND)
            t = r * r
            s = r * horner(SIN_HALF, t)
            h = horner(COS_HALF, t)
            half_cos = 0.5 - s * s
            half_sin = s * h
            e = turns * step
            e2 = e * e
            s2 = e * horner(SIN_STEP, e2)
            c2 = horner(COS_STEP, e2)
            twice = c2 * c2 - 2.0
            cc, ss = half_cos * c2, half_sin * s2
            sc, cs = half_sin * c2, half_cos * s2
            cos1, cos2 = cc + ss, cc - ss
            sin1, sin2 = sc - cs, sc + cs
            cosine = (twice * cos1 - cos2, cos1, cos2, twice * cos2 - cos1)
            sine = (twice * sin1 - sin2, sin1, sin2, twice * sin2 - sin1)
            for ch in range(4):
                bright = wide[2 + ch, :, at]
                right_ref[ch, pl.ds(r0, 16), at] = (bright * cosine[ch]).astype(BF16)
                right_ref[ch, pl.ds(r0, 16), slice(width + 128 * j, width + 128 * j + 128)] = (
                    bright * sine[ch]
                ).astype(BF16)
            for first, value in ((0, cosine), (width, sine)):
                put = slice(first + 128 * j, first + 128 * j + 128)
                mine[pl.ds(r0, 16), put] = value[channel].astype(BF16)
                if l0 is not None:
                    for ch in range(4):
                        left_ref[ch, pl.ds(l0, 16), put] = value[ch].astype(BF16)
            put = slice(2 * width + 128 * j, 2 * width + 128 * j + 128)
            mine[pl.ds(r0, 16), put] = (-cosine[channel]).astype(BF16)
            if l0 is not None:
                for ch in range(4):
                    left_ref[ch, pl.ds(l0, 16), put] = (-cosine[ch]).astype(BF16)

    def run(channel):
        def own_rows(i, _):
            block(channel * quarter + 16 * i, 16 * i, channel)
            return 0

        def other_rows(first):
            def body(i, _):
                block(first + 16 * i, None, channel)
                return 0

            return body

        lax.fori_loop(0, quarter // 16, own_rows, 0)
        if channel > 0:
            lax.fori_loop(0, channel * quarter // 16, other_rows(0), 0)
        if channel < 3:
            lax.fori_loop(0, (3 - channel) * quarter // 16, other_rows((channel + 1) * quarter), 0)

    for channel in range(4):
        pl.when(k == channel)(lambda channel=channel: run(channel))

    product = lax.dot_general(
        jnp.concatenate([mine[:, : 2 * width], mine[:, width:]], axis=0),
        right_ref[k],
        NT,
        preferred_element_type=F32,
    )

    @pl.when(pl.program_id(0) == 0)
    def _():
        model_ref[...] = product

    @pl.when(pl.program_id(0) != 0)
    def _():
        model_ref[...] += product


def model_kernel(right_ref, left_ref, model_ref):
    steps = 4
    rw = right_ref.shape[2] // steps
    width = rw // 2
    lefts = []
    for q in range(steps):
        lefts.append(
            jnp.concatenate(
                [
                    left_ref[0, :, 3 * width * q : 3 * width * q + 2 * width],
                    left_ref[0, :, 3 * width * q + width : 3 * width * q + 3 * width],
                ],
                axis=0,
            )
        )
    model_ref[0] = lax.dot_general(
        jnp.concatenate(lefts, axis=1), right_ref[0], NT, preferred_element_type=F32
    )


def solve_kernel(model_ref, v0, v1, v2, v3, ok_ref, cal_ref, out_ref, a_re, a_im, b_ab, wide, part):
    k = lax.axis_index("stn")
    n = v0.shape[2]
    quarter = n // 4
    bright = cal_ref[k]
    ok = ok_ref[0:1]
    columns = lax.broadcasted_iota(jnp.int32, (8, n), 1)
    sub = lax.broadcasted_iota(jnp.int32, (8, n), 0)

    def fold(x):
        return (x[:, :128] + x[:, 128:256]) + (x[:, 256:384] + x[:, 384:])

    def set_up(s, v):
        first = lax.rem(k + 4 - s, 4) * quarter

        def body(i, _):
            local = pl.multiple_of(8 * i, 8)
            r0 = pl.multiple_of(first + 8 * i, 8)
            mr = model_ref[pl.ds(r0, 8)] + bright
            mi = model_ref[pl.ds(n + r0, 8)]
            off = columns != sub + r0
            mr = jnp.where(off, mr, 0.0)
            mi = jnp.where(off, mi, 0.0)
            vr = v[0, pl.ds(local, 8)]
            vi = v[1, pl.ds(local, 8)]
            ar = mr * vr + mi * vi
            ai = mr * vi - mi * vr
            b = mr * mr + mi * mi
            a_re[pl.ds(r0, 8)] = ar
            a_im[pl.ds(r0, 8)] = ai
            b_ab[pl.ds(r0, 8)] = b
            g = wide[0]
            part[0, pl.ds(r0, 8)] = fold(ar * g)
            part[1, pl.ds(r0, 8)] = fold(ai * g)
            part[2, pl.ds(r0, 8)] = fold(b * g)
            return 0

        lax.fori_loop(0, quarter // 8, body, 0)

    def sums():
        gr, gi, gg = wide[0], wide[1], wide[2]

        def body(i, _):
            r0 = pl.multiple_of(8 * i, 8)
            ar, ai = a_re[pl.ds(r0, 8)], a_im[pl.ds(r0, 8)]
            part[0, pl.ds(r0, 8)] = fold(ar * gr - ai * gi)
            part[1, pl.ds(r0, 8)] = fold(ar * gi + ai * gr)
            part[2, pl.ds(r0, 8)] = fold(b_ab[pl.ds(r0, 8)] * gg)
            return 0

        lax.fori_loop(0, n // 8, body, 0)

    def total(q):
        return jnp.concatenate(
            [jnp.sum(part[q, 128 * b : 128 * b + 128].T, axis=0, keepdims=True) for b in range(n // 128)], axis=1
        )

    g_re, g_im = jnp.ones((1, n), F32), jnp.zeros((1, n), F32)
    out_ref[...] = jnp.zeros_like(out_ref)
    for iteration in range(ITERS):
        wide[0] = jnp.broadcast_to(ok * g_re, (8, n))
        wide[1] = jnp.broadcast_to(ok * g_im, (8, n))
        wide[2] = jnp.broadcast_to(ok * (g_re * g_re + g_im * g_im), (8, n))
        if iteration == 0:
            for s, v in enumerate((v0, v1, v2, v3)):
                set_up(s, v)
        else:
            sums()
        below = total(2) * ok + 1e-6 + (1.0 - ok)
        new_re = total(0) * ok / below
        new_im = total(1) * ok / below
        if iteration % 2 == 1:
            new_re = 0.5 * (new_re + g_re)
            new_im = 0.5 * (new_im + g_im)
        moved = jnp.sum((new_re - g_re) ** 2 + (new_im - g_im) ** 2, axis=1, keepdims=True)
        size = jnp.sum(new_re * new_re + new_im * new_im, axis=1, keepdims=True)
        out_ref[2 + iteration : 3 + iteration] = jnp.broadcast_to(moved / (size + 1e-6), (1, n))
        g_re, g_im = new_re, new_im
    out_ref[0:1] = g_re
    out_ref[1:2] = g_im


def residual_kernel(model_ref, vis_ref, g0, g1, g2, g3, ok_ref, cal_ref, gains_ref, res_ref, change_ref, table):
    k = lax.axis_index("stn")
    ch = pl.program_id(0)
    n = vis_ref.shape[3]
    quarter = n // 4
    lanes = pl.ds(pl.multiple_of(k * quarter, 128), quarter)

    @pl.when(ch == 0)
    def _():
        for s, g in enumerate((g0, g1, g2, g3)):
            table[lax.rem(k + 4 - s, 4)] = g[...]
        lane = lax.broadcasted_iota(jnp.int32, (ITERS, 4), 1)
        history = jnp.zeros((ITERS, 4), F32)
        for q in range(4):
            gains_ref[0, q : q + 1] = table[q, 0:1, lanes]
            gains_ref[1, q : q + 1] = table[q, 1:2, lanes]
            history = jnp.where(lane == q, table[q, 2 : 2 + ITERS, 0:4], history)
        change_ref[...] = history

    bright = cal_ref[ch]

    def column(row):
        return jnp.broadcast_to(row, (128, 128)).T

    gi_re = column(table[ch, 0:1, lanes])
    gi_im = column(table[ch, 1:2, lanes])
    ui = column(ok_ref[0:1, lanes])
    columns = lax.broadcasted_iota(jnp.int32, (16, 128), 1)
    sub = lax.broadcasted_iota(jnp.int32, (16, 128), 0)
    gj_re = [jnp.broadcast_to(table[ch, 0:1, 128 * b : 128 * b + 128], (16, 128)) for b in range(4)]
    gj_im = [jnp.broadcast_to(table[ch, 1:2, 128 * b : 128 * b + 128], (16, 128)) for b in range(4)]
    uj = [jnp.broadcast_to(ok_ref[0:1, 128 * b : 128 * b + 128], (16, 128)) for b in range(4)]
    for i in range(quarter // 16):
        rows = slice(16 * i, 16 * i + 16)
        a_re, a_im, a_ok = gi_re[rows], gi_im[rows], ui[rows]
        for b in range(4):
            at = slice(128 * b, 128 * b + 128)
            off = columns + 128 * b != sub + (k * quarter + 16 * i)
            e = jnp.where(off, a_ok * uj[b], 0.0)
            p_re = a_re * gj_re[b] + a_im * gj_im[b]
            p_im = a_im * gj_re[b] - a_re * gj_im[b]
            mr = model_ref[0, rows, at] + bright
            mi = model_ref[0, slice(quarter + 16 * i, quarter + 16 * i + 16), at]
            vr = vis_ref[0, 0, rows, at].astype(F32)
            vi = vis_ref[1, 0, rows, at].astype(F32)
            res_ref[0, 0, rows, at] = (e * (vr - (p_re * mr - p_im * mi))).astype(BF16)
            res_ref[1, 0, rows, at] = (e * (vi - (p_re * mi + p_im * mr))).astype(BF16)


def per_device(visibilities, calibrator, catalog, assignment, stations, input_order, station_flags):
    rows, n = visibilities.shape[2], visibilities.shape[3]
    sources = 64 * CAP
    width = 512
    chunks = sources // width
    whole = pl.BlockSpec(memory_space=VMEM)
    smem = pl.BlockSpec(memory_space=pltpu.SMEM)
    small = pltpu.CompilerParams(vmem_limit_bytes=24 << 20)

    def shape(*dims, dtype=F32):
        return jax.ShapeDtypeStruct(dims, dtype)

    def ring(s):
        return [(i, (i + s) % 4) for i in range(4)]

    spread = pl.pallas_call(
        spread_kernel,
        out_shape=[shape(2, rows, n)] * 4,
        in_specs=[whole],
        out_specs=[whole] * 4,
        compiler_params=small,
        name="spread",
    )(visibilities)
    tiles = [spread[0]] + [lax.ppermute(spread[s], "stn", ring(s)) for s in (1, 2, 3)]

    send, xb, yb, ok = pl.pallas_call(
        route_kernel,
        out_shape=[shape(64, 1, 5 * CAP), shape(n, 128), shape(n, 128), shape(8, n)],
        in_specs=[pl.BlockSpec(memory_space=pl.ANY)] + [whole] * 4,
        out_specs=[whole] * 4,
        scratch_shapes=[VMEM((8, 128), jnp.int32), pltpu.SemaphoreType.DMA],
        compiler_params=small,
        name="route",
    )(
        assignment.reshape(-1, 128),
        catalog,
        stations,
        input_order.reshape(1, n),
        station_flags.reshape(1, n),
    )
    received = lax.all_to_all(send, "chan", 0, 0)
    components = received.reshape(64, 5, CAP).transpose(1, 0, 2).reshape(5, sources)

    right, left, model_own = pl.pallas_call(
        phasor_kernel,
        grid=(chunks,),
        out_shape=[
            shape(4, n, 2 * sources, dtype=BF16),
            shape(4, rows, 3 * sources, dtype=BF16),
            shape(2 * n, n),
        ],
        in_specs=[
            pl.BlockSpec((5, width), lambda q: (0, q)),
            pl.BlockSpec((n, 128), lambda q: (0, 0)),
            pl.BlockSpec((n, 128), lambda q: (0, 0)),
        ],
        out_specs=[
            pl.BlockSpec((4, n, 2 * width), lambda q: (0, 0, q)),
            pl.BlockSpec((4, rows, 3 * width), lambda q: (0, 0, q)),
            pl.BlockSpec((2 * n, n), lambda q: (0, 0)),
        ],
        scratch_shapes=[VMEM((6, 16, width), F32), VMEM((n, 3 * width), BF16)],
        compiler_params=pltpu.CompilerParams(vmem_limit_bytes=32 << 20),
        cost_estimate=pl.CostEstimate(flops=10 << 30, bytes_accessed=21 << 20, transcendentals=0),
        name="phasor",
    )(components, xb, yb)

    solved = pl.pallas_call(
        solve_kernel,
        out_shape=shape(8, n),
        in_specs=[whole] * 6 + [smem],
        out_specs=whole,
        scratch_shapes=[VMEM((n, n), F32)] * 3 + [VMEM((3, 8, n), F32), VMEM((3, n, 128), F32)],
        compiler_params=small,
        name="solve",
    )(model_own, *tiles, ok, calibrator)
    tables = [solved] + [lax.ppermute(solved, "stn", ring(s)) for s in (1, 2, 3)]

    model = pl.pallas_call(
        model_kernel,
        grid=(4,),
        out_shape=shape(4, 2 * rows, n),
        in_specs=[
            pl.BlockSpec((1, n, 2 * sources), lambda q: (q, 0, 0)),
            pl.BlockSpec((1, rows, 3 * sources), lambda q: (q, 0, 0)),
        ],
        out_specs=pl.BlockSpec((1, 2 * rows, n), lambda q: (q, 0, 0)),
        compiler_params=pltpu.CompilerParams(vmem_limit_bytes=32 << 20),
        cost_estimate=pl.CostEstimate(flops=5 << 30, bytes_accessed=21 << 20, transcendentals=0),
        name="model",
    )(right, left)

    row = pl.BlockSpec((8, n), lambda q: (0, 0))
    gains, residual, changes = pl.pallas_call(
        residual_kernel,
        grid=(4,),
        out_shape=[shape(2, 4, rows), shape(2, 4, rows, n, dtype=BF16), shape(ITERS, 4)],
        in_specs=[
            pl.BlockSpec((1, 2 * rows, n), lambda q: (q, 0, 0)),
            pl.BlockSpec((2, 1, rows, n), lambda q: (0, q, 0, 0)),
            row,
            row,
            row,
            row,
            row,
            smem,
        ],
        out_specs=[
            pl.BlockSpec((2, 4, rows), lambda q: (0, 0, 0)),
            pl.BlockSpec((2, 1, rows, n), lambda q: (0, q, 0, 0)),
            pl.BlockSpec((ITERS, 4), lambda q: (0, 0)),
        ],
        scratch_shapes=[VMEM((4, 8, n), F32)],
        compiler_params=small,
        name="residual",
    )(model, visibilities, *tables, ok, calibrator)
    return (gains, residual, changes)


def solution(mesh):
    placed = (P(None, "chan", "stn", None), P("chan"), P(None, "chan"), P(), P(), P(), P())
    return jax.shard_map(
        per_device,
        mesh=mesh,
        in_specs=placed,
        out_specs=(P(None, "chan", "stn"), P(None, "chan", "stn", None), P(None, "chan")),
        check_vma=False,
    )
```

time: 307 us -> 75.4 us (0.25)
  the two profiles are of different devices: /device:TPU:2 before, /device:TPU:1 now
where the time goes in v1:
time: 75.4 us; the launch traced here: 74.9 us
  Pallas kernels  38.8 us (51%)
  starting transfers between devices  22.9 us (30%)
  local copies, waits for them, and re-layouts  9.37 us (12%)
  waiting for transfers between devices  3.1 us (4%)
    pallas_call x1, Pallas kernels, per_device(): pl.pallas_call(phasor_kernel, grid=(chunks,), out_shape=[shape(4, n, 2 *...  20.5 us
    all_to_all x1, starting transfers between devices, per_device(): received = lax.all_to_all(send, 'chan', 0, 0)  13.3 us
    pallas_call x1, Pallas kernels, per_device(): pl.pallas_call(model_kernel, grid=(4,), out_shape=shape(4, 2 * rows, n),...  8.6 us
    unnamed x20, local copies, waits for them, and re-layouts  6.61 us
    ppermute x3, starting transfers between devices, per_device(): lax.ppermute(spread[s], 'stn', ring(s))  4.81 us
    ppermute x3, starting transfers between devices, per_device(): lax.ppermute(solved, 'stn', ring(s))  4.71 us
    pallas_call x1, Pallas kernels, per_device(): pl.pallas_call(solve_kernel, out_shape=shape(8, n), in_specs=[whole] * 6...  3.99 us
    all_to_all x1, waiting for transfers between devices, per_device(): received = lax.all_to_all(send, 'chan', 0, 0)  3.08 us
  transfers between devices with their start and end apart: 7, of which 1 were waited for; matrix products, arithmetic and copies ran while one was open for 4% of the time, Pallas kernels for 40%

profile of v1, /device:TPU:1, one launch (start us, length us, event | category | flops | bytes accessed | tf_op | source)
XLA Modules:
  0.0 74.9 jit_solution(8977535358489861865)
XLA Ops:
  0.6 0.0 copy-start.2
  0.6 0.9 %copy-done.2 = s32[65536,1]{0,1:T(1,128)S(1)} copy-done((s32[65536,1]{0,1:T(1,128)S(1)}, s32[65536,1]{0,1:T(1,128)}, u32[]{:S(2)}) %copy-start.2) | copy-done | bytes 262168
  1.6 0.0 copy-start.3
  1.6 0.8 %copy-done.3 = f32[5,1024]{1,0:T(8,128)S(1)} copy-done((f32[5,1024]{1,0:T(8,128)S(1)}, f32[5,1024]{1,0:T(8,128)}, u32[]{:S(2)}) %copy-start.3) | copy-done | bytes 20504
  2.3 0.0 copy-start.4
  2.3 0.7 copy-done.4
  3.0 0.0 copy-start.5
  3.0 0.7 copy-done.5
  3.7 0.0 copy-start.6
  3.7 0.7 copy-done.6
  4.4 1.8 %route.1 = (f32[64,1,160]{2,1,0:T(1,128)}, f32[512,128]{1,0:T(8,128)S(1)}, f32[512,128]{1,0:T(8,128)S(1)}, f32[8,512]{1,0:T(8,128)S(1)}) custom-call(s32[512,128]{1,0:T(8,128)S(1)} %bitcast.6, f32[5,1024]{1,0:T(8,128)S(1)} %copy-done.3, f32[2,512]{1,0:T(2,128)S(1)} %copy-done.4, s32[1,512]{1,0:T(1,128)S(1)} %bitcast.7, s32[1,512]{1,0:T(1,128)S(1)} %bitcast.8), custom_call_target="tpu_custom_call" | custom-call | tf_op jit(solution)/shard_map/route/pallas_call | solution.py:364
  6.2 0.0 copy-start.8
  6.2 0.7 copy-done.8
  6.9 13.3 %all-to-all-start = ((f32[64,1,160]{2,1,0:T(1,128)}), f32[64,1,160]{2,1,0:T(1,128)}, u32[]{:S(2)}, u32[]{:S(2)}) async-start(f32[64,1,160]{2,1,0:T(1,128)} %get-tuple-element.14), calls=%async_computation | async-start | bytes 131072 | tf_op jit(solution)/shard_map/all_to_all | solution.py:379
  20.2 0.0 copy-start
  20.3 1.2 %copy-done = bf16[2,4,128,512]{3,2,1,0:T(8,128)(2,1)S(1)} copy-done((bf16[2,4,128,512]{3,2,1,0:T(8,128)(2,1)S(1)}, bf16[2,4,128,512]{3,2,1,0:T(8,128)(2,1)}, u32[]{:S(2)}) %copy-start) | copy-done | bytes 1048600
  21.5 0.9 %spread.1 = (f32[2,128,512]{2,1,0:T(8,128)S(1)}, f32[2,128,512]{2,1,0:T(8,128)}, f32[2,128,512]{2,1,0:T(8,128)S(1)}, f32[2,128,512]{2,1,0:T(8,128)S(1)}) custom-call(bf16[2,4,128,512]{3,2,1,0:T(8,128)(2,1)S(1)} %copy-done), custom_call_target="tpu_custom_call" | custom-call | tf_op jit(solution)/shard_map/spread/pallas_call | solution.py:354
  22.4 1.2 %collective-permute-start = (f32[2,128,512]{2,1,0:T(8,128)}, f32[2,128,512]{2,1,0:T(8,128)S(1)}, u32[]{:S(2)}, u32[]{:S(2)}) collective-permute-start(f32[2,128,512]{2,1,0:T(8,128)} %get-tuple-element.21), channel_id=1, source_target_pairs={{0,1},{1,2},{2,3},{3,0},{4,5},{5,6},{6,7},{7,4},{8,9},{9,10},{10,1... | collective-permute-start | bytes 1572872 | tf_op jit(solution)/shard_map/ppermute | solution.py:362
  23.6 2.5 %collective-permute-start.1 = (f32[2,128,512]{2,1,0:T(8,128)S(1)}, f32[2,128,512]{2,1,0:T(8,128)S(1)}, u32[]{:S(2)}, u32[]{:S(2)}) collective-permute-start(f32[2,128,512]{2,1,0:T(8,128)S(1)} %get-tuple-element.22), channel_id=1, source_target_pairs={{0,2},{1,3},{2,0},{3,1},{4,6},{5,7},{6,4},{7,5},{8,10},{9,11},{10,... | collective-permute-start | bytes 1572872 | tf_op jit(solution)/shard_map/ppermute | solution.py:362
  26.0 1.2 %collective-permute-start.2 = (f32[2,128,512]{2,1,0:T(8,128)S(1)}, f32[2,128,512]{2,1,0:T(8,128)S(1)}, u32[]{:S(2)}, u32[]{:S(2)}) collective-permute-start(f32[2,128,512]{2,1,0:T(8,128)S(1)} %get-tuple-element.23), channel_id=1, source_target_pairs={{0,3},{1,0},{2,1},{3,2},{4,7},{5,4},{6,5},{7,6},{8,11},{9,8},{10,9... | collective-permute-start | bytes 1572872 | tf_op jit(solution)/shard_map/ppermute | solution.py:362
  27.2 3.1 %all-to-all-done = f32[64,1,160]{2,1,0:T(1,128)} async-done(((f32[64,1,160]{2,1,0:T(1,128)}), f32[64,1,160]{2,1,0:T(1,128)}, u32[]{:S(2)}, u32[]{:S(2)}) %all-to-all-start) | async-done | bytes 40992 | tf_op jit(solution)/shard_map/all_to_all | solution.py:379
  30.2 0.9 %copy.11 = f32[64,1,160]{0,2,1:T(8,128)S(1)} copy(f32[64,1,160]{2,1,0:T(1,128)} %all-to-all-done) | data formatting | bytes 81920 | tf_op jit(solution)/shard_map/all_to_all | solution.py:379
  31.2 0.8 %copy.12 = f32[5,64,32]{2,1,0:T(8,128)} copy(f32[5,64,32]{1,2,0:T(8,128)S(1)} %bitcast.9) | data formatting | bytes 81920 | tf_op jit(solution)/shard_map/transpose | solution.py:380
  32.0 1.0 %reshape.25.comp_ref = f32[5,2048]{1,0:T(8,128)S(1)} reshape(f32[5,64,32]{2,1,0:T(8,128)} %copy.12) | data formatting | bytes 81920 | tf_op jit(solution)/shard_map/reshape | solution.py:380
  33.0 0.0 copy-start.9
  33.0 0.9 %copy-done.9 = f32[512,128]{1,0:T(8,128)S(1)} copy-done((f32[512,128]{1,0:T(8,128)S(1)}, f32[512,128]{1,0:T(8,128)}, u32[]{:S(2)}) %copy-start.9) | copy-done | bytes 262168
  34.0 0.0 copy-start.7
  34.0 20.5 %phasor.1 = (bf16[4,512,4096]{2,1,0:T(8,128)(2,1)}, bf16[4,128,6144]{2,1,0:T(8,128)(2,1)S(1)}, f32[1024,512]{1,0:T(8,128)S(1)}) custom-call(f32[5,2048]{1,0:T(8,128)S(1)} %reshape.25.comp_ref, f32[512,128]{1,0:T(8,128)S(1)} %get-tuple-element.15.xb_ref, f32[512,128]{1,0:T(8,128)S(1)} %copy-done.9), custom_call_target="tpu_custom_call" | custom-call | flops 10737418240 | bytes 22020096 | tf_op jit(solution)/shard_map/phasor/pallas_call | solution.py:382
  54.5 0.0 collective-permute-done.v1
  54.5 0.0 collective-permute-done.1.v2
  54.5 0.0 collective-permute-done.2.v3
  54.5 0.0 copy-done.7
  54.5 4.0 %solve.1.g0 = f32[8,512]{1,0:T(8,128)S(1)} custom-call(f32[1024,512]{1,0:T(8,128)S(1)} %get-tuple-element.19.model_ref, f32[2,128,512]{2,1,0:T(8,128)S(1)} %get-tuple-element.20.v0, f32[2,128,512]{2,1,0:T(8,128)S(1)} %collective-permute-done.v1, f32[2,128,512]{2,1,0:T(8,128)S(1)} %collective-permute-done.1.v2, f32[2,128,512]{2,1,0:T(8,128)S(1)} %collective-permute-done.2.v3, ...), custom_call_target="tpu_custom_call" | custom-call | tf_op jit(solution)/shard_map/solve/pallas_call | solution.py:406
  58.5 1.1 %collective-permute-start.3 = (f32[8,512]{1,0:T(8,128)S(1)}, f32[8,512]{1,0:T(8,128)S(1)}, u32[]{:S(2)}, u32[]{:S(2)}) collective-permute-start(f32[8,512]{1,0:T(8,128)S(1)} %solve.1.g0), channel_id=1, source_target_pairs={{0,1},{1,2},{2,3},{3,0},{4,5},{5,6},{6,7},{7,4},{8,9},{9,10},{10,1... | collective-permute-start | bytes 49160 | tf_op jit(solution)/shard_map/ppermute | solution.py:415
  59.6 2.3 %collective-permute-start.4 = (f32[8,512]{1,0:T(8,128)S(1)}, f32[8,512]{1,0:T(8,128)S(1)}, u32[]{:S(2)}, u32[]{:S(2)}) collective-permute-start(f32[8,512]{1,0:T(8,128)S(1)} %solve.1.g0), channel_id=1, source_target_pairs={{0,2},{1,3},{2,0},{3,1},{4,6},{5,7},{6,4},{7,5},{8,10},{9,11},{10,... | collective-permute-start | bytes 49160 | tf_op jit(solution)/shard_map/ppermute | solution.py:415
  61.9 1.3 %collective-permute-start.5 = (f32[8,512]{1,0:T(8,128)S(1)}, f32[8,512]{1,0:T(8,128)S(1)}, u32[]{:S(2)}, u32[]{:S(2)}) collective-permute-start(f32[8,512]{1,0:T(8,128)S(1)} %solve.1.g0), channel_id=1, source_target_pairs={{0,3},{1,0},{2,1},{3,2},{4,7},{5,4},{6,5},{7,6},{8,11},{9,8},{10,9... | collective-permute-start | bytes 49160 | tf_op jit(solution)/shard_map/ppermute | solution.py:415
  63.2 0.0 copy-start.1
  63.2 8.6 %model.1.model_ref = f32[4,256,512]{2,1,0:T(8,128)S(1)} custom-call(bf16[4,512,4096]{2,1,0:T(8,128)(2,1)} %get-tuple-element.17.right_ref, bf16[4,128,6144]{2,1,0:T(8,128)(2,1)S(1)} %get-tuple-element.18.left_ref), custom_call_target="tpu_custom_call" | custom-call | flops 5368709120 | bytes 22020096 | tf_op jit(solution)/shard_map/model/pallas_call | solution.py:417
  71.8 0.0 collective-permute-done.3.g1
  71.8 0.0 collective-permute-done.4.g2
  71.9 0.0 collective-permute-done.5.g3
  71.9 0.0 copy-done.1
  71.9 3.0 %residual.1 = (f32[2,4,128]{2,1,0:T(4,128)}, bf16[2,4,128,512]{3,2,1,0:T(8,128)(2,1)}, f32[3,4]{1,0:T(4,128)}) custom-call(f32[4,256,512]{2,1,0:T(8,128)S(1)} %model.1.model_ref, bf16[2,4,128,512]{3,2,1,0:T(8,128)(2,1)S(1)} %copy-done.1, f32[8,512]{1,0:T(8,128)S(1)} %solve.1.g0, f32[8,512]{1,0:T(8,128)S(1)} %collective-permute-done.3.g1, ...), custom_call_target="tpu_custom_call" | custom-call | tf_op jit(solution)/shard_map/residual/pallas_call | solution.py:432
Async XLA Ops:
  0.6 1.0 %copy-start.2 = (s32[65536,1]{0,1:T(1,128)S(1)}, s32[65536,1]{0,1:T(1,128)}, u32[]{:S(2)}) copy-start(s32[65536,1]{0,1:T(1,128)} %param.10) | copy-start | bytes 786436
  1.6 0.8 %copy-start.3 = (f32[5,1024]{1,0:T(8,128)S(1)}, f32[5,1024]{1,0:T(8,128)}, u32[]{:S(2)}) copy-start(f32[5,1024]{1,0:T(8,128)} %cat_ref.1) | copy-start | bytes 61444
  2.3 0.7 copy-start.4
  3.0 0.7 copy-start.5
  3.7 0.7 copy-start.6
  6.2 0.7 copy-start.8
  6.9 23.3 %all-to-all-start = ((f32[64,1,160]{2,1,0:T(1,128)}), f32[64,1,160]{2,1,0:T(1,128)}, u32[]{:S(2)}, u32[]{:S(2)}) async-start(f32[64,1,160]{2,1,0:T(1,128)} %get-tuple-element.14), calls=%async_computation | async-start | bytes 131072 | tf_op jit(solution)/shard_map/all_to_all | solution.py:379
  20.2 1.2 %copy-start = (bf16[2,4,128,512]{3,2,1,0:T(8,128)(2,1)S(1)}, bf16[2,4,128,512]{3,2,1,0:T(8,128)(2,1)}, u32[]{:S(2)}) copy-start(bf16[2,4,128,512]{3,2,1,0:T(8,128)(2,1)} %vis_ref.3) | copy-start | bytes 3145732
  22.4 32.2 %collective-permute-start = (f32[2,128,512]{2,1,0:T(8,128)}, f32[2,128,512]{2,1,0:T(8,128)S(1)}, u32[]{:S(2)}, u32[]{:S(2)}) collective-permute-start(f32[2,128,512]{2,1,0:T(8,128)} %get-tuple-element.21), channel_id=1, source_target_pairs={{0,1},{1,2},{2,3},{3,0},{4,5},{5,6},{6,7},{7,4},{8,9},{9,10},{10,1... | collective-permute-start | bytes 1572872 | tf_op jit(solution)/shard_map/ppermute | solution.py:362
  23.6 30.9 %collective-permute-start.1 = (f32[2,128,512]{2,1,0:T(8,128)S(1)}, f32[2,128,512]{2,1,0:T(8,128)S(1)}, u32[]{:S(2)}, u32[]{:S(2)}) collective-permute-start(f32[2,128,512]{2,1,0:T(8,128)S(1)} %get-tuple-element.22), channel_id=1, source_target_pairs={{0,2},{1,3},{2,0},{3,1},{4,6},{5,7},{6,4},{7,5},{8,10},{9,11},{10,... | collective-permute-start | bytes 1572872 | tf_op jit(solution)/shard_map/ppermute | solution.py:362
  26.0 28.5 %collective-permute-start.2 = (f32[2,128,512]{2,1,0:T(8,128)S(1)}, f32[2,128,512]{2,1,0:T(8,128)S(1)}, u32[]{:S(2)}, u32[]{:S(2)}) collective-permute-start(f32[2,128,512]{2,1,0:T(8,128)S(1)} %get-tuple-element.23), channel_id=1, source_target_pairs={{0,3},{1,0},{2,1},{3,2},{4,7},{5,4},{6,5},{7,6},{8,11},{9,8},{10,9... | collective-permute-start | bytes 1572872 | tf_op jit(solution)/shard_map/ppermute | solution.py:362
  33.0 1.0 %copy-start.9 = (f32[512,128]{1,0:T(8,128)S(1)}, f32[512,128]{1,0:T(8,128)}, u32[]{:S(2)}) copy-start(f32[512,128]{1,0:T(8,128)} %copy-done.8) | copy-start | bytes 786436
  34.0 20.6 %copy-start.7 = (f32[4]{0:T(128)S(1)}, f32[4]{0:T(128)}, u32[]{:S(2)}) copy-start(f32[4]{0:T(128)} %cal_ref.3) | copy-start | bytes 52
  58.5 13.3 %collective-permute-start.3 = (f32[8,512]{1,0:T(8,128)S(1)}, f32[8,512]{1,0:T(8,128)S(1)}, u32[]{:S(2)}, u32[]{:S(2)}) collective-permute-start(f32[8,512]{1,0:T(8,128)S(1)} %solve.1.g0), channel_id=1, source_target_pairs={{0,1},{1,2},{2,3},{3,0},{4,5},{5,6},{6,7},{7,4},{8,9},{9,10},{10,1... | collective-permute-start | bytes 49160 | tf_op jit(solution)/shard_map/ppermute | solution.py:415
  59.6 12.2 %collective-permute-start.4 = (f32[8,512]{1,0:T(8,128)S(1)}, f32[8,512]{1,0:T(8,128)S(1)}, u32[]{:S(2)}, u32[]{:S(2)}) collective-permute-start(f32[8,512]{1,0:T(8,128)S(1)} %solve.1.g0), channel_id=1, source_target_pairs={{0,2},{1,3},{2,0},{3,1},{4,6},{5,7},{6,4},{7,5},{8,10},{9,11},{10,... | collective-permute-start | bytes 49160 | tf_op jit(solution)/shard_map/ppermute | solution.py:415
  61.9 9.9 %collective-permute-start.5 = (f32[8,512]{1,0:T(8,128)S(1)}, f32[8,512]{1,0:T(8,128)S(1)}, u32[]{:S(2)}, u32[]{:S(2)}) collective-permute-start(f32[8,512]{1,0:T(8,128)S(1)} %solve.1.g0), channel_id=1, source_target_pairs={{0,3},{1,0},{2,1},{3,2},{4,7},{5,4},{6,5},{7,6},{8,11},{9,8},{10,9... | collective-permute-start | bytes 49160 | tf_op jit(solution)/shard_map/ppermute | solution.py:415
  63.2 8.6 %copy-start.1 = (bf16[2,4,128,512]{3,2,1,0:T(8,128)(2,1)S(1)}, bf16[2,4,128,512]{3,2,1,0:T(8,128)(2,1)}, u32[]{:S(2)}) copy-start(bf16[2,4,128,512]{3,2,1,0:T(8,128)(2,1)} %vis_ref.3) | copy-start | bytes 3145732

commit v2 on v1

--- a/solution.py
+++ b/solution.py
@@ -45,24 +45,36 @@
         out_refs[s][...] = vis_ref[:, lax.rem(k + s, 4)].astype(F32)
 
 
-def route_kernel(assign_ref, cat_ref, st_ref, order_ref, flag_ref, send_ref, xb_ref, yb_ref, ok_ref, own, sem):
+def route_kernel(assign_hbm, cat_hbm, st_hbm, order_hbm, flag_hbm, send_ref, place_ref, own, cat, st, order, flag, sem):
     c = lax.axis_index("chan")
-    copy = pltpu.make_async_copy(assign_ref.at[pl.ds(pl.multiple_of(c * 8, 8), 8)], own, sem)
-    copy.start()
-    n = order_ref.shape[1]
-    hot = (lax.broadcasted_iota(jnp.int32, (n, n), 0) == order_ref[...]).astype(F32).astype(BF16)
-    high, middle, low = split3(st_ref[...])
-    rows = jnp.concatenate([high, middle, low, flag_ref[...].astype(F32), jnp.zeros((9, n), F32)], axis=0)
+    copies = [
+        pltpu.make_async_copy(source, target, sem.at[i])
+        for i, (source, target) in enumerate(
+            (
+                (st_hbm, st),
+                (order_hbm, order),
+                (flag_hbm, flag),
+                (assign_hbm.at[pl.ds(pl.multiple_of(c * 8, 8), 8)], own),
+                (cat_hbm, cat),
+            )
+        )
+    ]
+    for copy in copies:
+        copy.start()
+    n = order.shape[1]
+    for copy in copies[:3]:
+        copy.wait()
+    hot = (lax.broadcasted_iota(jnp.int32, (n, n), 0) == order[...]).astype(F32).astype(BF16)
+    high, middle, low = split3(st[...])
+    rows = jnp.concatenate([high, middle, low, flag[...].astype(F32), jnp.zeros((9, n), F32)], axis=0)
     placed = jnp.dot(rows.astype(BF16), hot, preferred_element_type=F32)
     middle_nu = 1.0 + (4.0 * c.astype(F32) + 1.5) * (1.0 / 512.0)
-    x = (placed[0:1] + placed[2:3] + placed[4:5]) * middle_nu
-    y = (placed[1:2] + placed[3:4] + placed[5:6]) * middle_nu
-    ok_ref[...] = jnp.broadcast_to(placed[6:7], ok_ref.shape)
-    for b in range(n // 128):
-        cols = slice(128 * b, 128 * b + 128)
-        xb_ref[cols] = jnp.broadcast_to(x[:, cols], (128, 128)).T
-        yb_ref[cols] = jnp.broadcast_to(y[:, cols], (128, 128)).T
-    copy.wait()
+    place_ref[...] = jnp.zeros_like(place_ref)
+    place_ref[0:1] = placed[6:7]
+    place_ref[1:2] = (placed[0:1] + placed[2:3] + placed[4:5]) * middle_nu
+    place_ref[2:3] = (placed[1:2] + placed[3:4] + placed[5:6]) * middle_nu
+    for copy in copies[3:]:
+        copy.wait()
     blocks = lax.broadcasted_iota(jnp.int32, (64, 128), 0)
     hits = [(blocks == own[t : t + 1]).astype(F32) for t in range(8)]
     stacked = jnp.concatenate(hits, axis=0).astype(BF16)
@@ -71,7 +83,7 @@
     totals = jnp.dot(stacked, jnp.ones((128, 128), BF16), preferred_element_type=F32)
     before = jnp.full((64, 128), -1.0, F32)
     slot = lax.broadcasted_iota(jnp.int32, (CAP, 128), 0).astype(F32)
-    pieces = split3(cat_ref[...])
+    pieces = split3(cat[...])
     left, right = [], []
     for t in range(8):
         part = slice(64 * t, 64 * t + 64)
@@ -91,117 +103,143 @@
     send_ref[:, 0, :] = sent
 
 
-def phasor_kernel(comp_ref, xb_ref, yb_ref, right_ref, left_ref, model_ref, wide, mine):
-    width = comp_ref.shape[1]
+def phasor_kernel(recv_ref, place_ref, right_out, left_out, model_ref, parts, spots, rights, lefts, wides, sems):
     c = lax.axis_index("chan")
     k = lax.axis_index("stn")
-    rows = mine.shape[0]
-    quarter = rows // 4
+    g = pl.program_id(0)
+    n = model_ref.shape[1]
+    quarter = n // 4
+    width = 256
+    tiles = width // 128
     base = 1.0 + 4.0 * c.astype(F32) * (1.0 / 512.0)
     middle_nu = 1.0 + (4.0 * c.astype(F32) + 1.5) * (1.0 / 512.0)
-    step = jnp.full((1, 128), 2.0 * jnp.pi / 1024.0, F32) / middle_nu
-    wide[0] = jnp.broadcast_to(comp_ref[0:1], (16, width))
-    wide[1] = jnp.broadcast_to(comp_ref[1:2], (16, width))
-    for ch in range(4):
-        log_nu = jnp.log(jnp.full((1, width), 1.0, F32) * (base + ch / 512.0))
-        bright = comp_ref[2:3] * jnp.exp(log_nu * (comp_ref[3:4] + comp_ref[4:5] * log_nu))
-        wide[2 + ch] = jnp.broadcast_to(bright, (16, width))
-
-    def block(r0, l0, channel):
-        x = xb_ref[pl.ds(r0, 16)]
-        y = yb_ref[pl.ds(r0, 16)]
-        for j in range(width // 128):
-            at = slice(128 * j, 128 * j + 128)
-            turns = wide[0, :, at] * x + wide[1, :, at] * y
-            r = turns - ((turns + ROUND) - ROUND)
-            t = r * r
-            s = r * horner(SIN_HALF, t)
-            h = horner(COS_HALF, t)
-            half_cos = 0.5 - s * s
-            half_sin = s * h
-            e = turns * step
-            e2 = e * e
-            s2 = e * horner(SIN_STEP, e2)
-            c2 = horner(COS_STEP, e2)
-            twice = c2 * c2 - 2.0
-            cc, ss = half_cos * c2, half_sin * s2
-            sc, cs = half_sin * c2, half_cos * s2
-            cos1, cos2 = cc + ss, cc - ss
-            sin1, sin2 = sc - cs, sc + cs
-            cosine = (twice * cos1 - cos2, cos1, cos2, twice * cos2 - cos1)
-            sine = (twice * sin1 - sin2, sin1, sin2, twice * sin2 - sin1)
-            for ch in range(4):
-                bright = wide[2 + ch, :, at]
-                right_ref[ch, pl.ds(r0, 16), at] = (bright * cosine[ch]).astype(BF16)
-                right_ref[ch, pl.ds(r0, 16), slice(width + 128 * j, width + 128 * j + 128)] = (
-                    bright * sine[ch]
-                ).astype(BF16)
-            for first, value in ((0, cosine), (width, sine)):
-                put = slice(first + 128 * j, first + 128 * j + 128)
-                mine[pl.ds(r0, 16), put] = value[channel].astype(BF16)
-                if l0 is not None:
-                    for ch in range(4):
-                        left_ref[ch, pl.ds(l0, 16), put] = value[ch].astype(BF16)
-            put = slice(2 * width + 128 * j, 2 * width + 128 * j + 128)
-            mine[pl.ds(r0, 16), put] = (-cosine[channel]).astype(BF16)
-            if l0 is not None:
-                for ch in range(4):
-                    left_ref[ch, pl.ds(l0, 16), put] = (-cosine[ch]).astype(BF16)
-
-    def run(channel):
-        def own_rows(i, _):
-            block(channel * quarter + 16 * i, 16 * i, channel)
-            return 0
-
-        def other_rows(first):
-            def body(i, _):
-                block(first + 16 * i, None, channel)
-                return 0
-
-            return body
-
-        lax.fori_loop(0, quarter // 16, own_rows, 0)
-        if channel > 0:
-            lax.fori_loop(0, channel * quarter // 16, other_rows(0), 0)
-        if channel < 3:
-            lax.fori_loop(0, (3 - channel) * quarter // 16, other_rows((channel + 1) * quarter), 0)
-
-    for channel in range(4):
-        pl.when(k == channel)(lambda channel=channel: run(channel))
-
-    product = lax.dot_general(
-        jnp.concatenate([mine[:, : 2 * width], mine[:, width:]], axis=0),
-        right_ref[k],
-        NT,
-        preferred_element_type=F32,
-    )
-
-    @pl.when(pl.program_id(0) == 0)
+    step = jnp.full((8, width), 2.0 * jnp.pi / 1024.0, F32) / middle_nu
+
+    @pl.when(g == 0)
     def _():
-        model_ref[...] = product
-
-    @pl.when(pl.program_id(0) != 0)
+        got = recv_ref[:, 0, :]
+        got = jnp.concatenate([got, jnp.zeros((64, 256 - got.shape[1]), F32)], axis=1)
+        got = jnp.concatenate([got, jnp.zeros((64, 256), F32)], axis=0).T
+        lane = lax.broadcasted_iota(jnp.int32, (16, 128), 1)
+        rows = []
+        for f in range(5):
+            low, high = got[32 * f : 32 * f + 16], got[32 * f + 16 : 32 * f + 32]
+            rows.append(jnp.where(lane < 64, low, pltpu.roll(high, 64, 1)))
+        parts[0] = rows[0]
+        parts[1] = rows[1]
+        for ch in range(4):
+            log_nu = jnp.log(jnp.full((16, 128), 1.0, F32) * (base + ch / 512.0))
+            parts[2 + ch] = rows[2] * jnp.exp(log_nu * (rows[3] + rows[4] * log_nu))
+        for axis in range(2):
+            for b in range(n // 128):
+                row = place_ref[1 + axis : 2 + axis, 128 * b : 128 * b + 128]
+                spots[axis, 128 * b : 128 * b + 128] = jnp.broadcast_to(row, (128, 128)).T
+
+    def out_copies(chunk, buffer):
+        return (
+            pltpu.make_async_copy(rights[buffer], right_out.at[chunk], sems.at[2 * buffer]),
+            pltpu.make_async_copy(
+                lefts[buffer].at[:, pl.ds(pl.multiple_of(k * quarter, quarter), quarter)],
+                left_out.at[chunk],
+                sems.at[2 * buffer + 1],
+            ),
+        )
+
+    def phases(buffer, r0):
+        right, left, wide = rights[buffer], lefts[buffer], wides[buffer]
+        rows = slice(r0, r0 + 8)
+        x = jnp.concatenate([spots[0, rows]] * tiles, axis=1)
+        y = jnp.concatenate([spots[1, rows]] * tiles, axis=1)
+        turns = wide[0] * x + wide[1] * y
+        r = turns - ((turns + ROUND) - ROUND)
+        t = r * r
+        s = r * horner(SIN_HALF, t)
+        h = horner(COS_HALF, t)
+        half_cos = 0.5 - s * s
+        half_sin = s * h
+        e = turns * step
+        e2 = e * e
+        s2 = e * horner(SIN_STEP, e2)
+        c2 = horner(COS_STEP, e2)
+        twice = c2 * c2 - 2.0
+        cc, ss = half_cos * c2, half_sin * s2
+        sc, cs = half_sin * c2, half_cos * s2
+        cos1, cos2 = cc + ss, cc - ss
+        sin1, sin2 = sc - cs, sc + cs
+        for ch, cosine, sine in (
+            (1, cos1, sin1),
+            (2, cos2, sin2),
+            (0, twice * cos1 - cos2, twice * sin1 - sin2),
+            (3, twice * cos2 - cos1, twice * sin2 - sin1),
+        ):
+            bright = wide[2 + ch]
+            right[ch, rows, :width] = (bright * cosine).astype(BF16)
+            right[ch, rows, width:] = (bright * sine).astype(BF16)
+            left[ch, rows, :width] = cosine.astype(BF16)
+            left[ch, rows, width:] = sine.astype(BF16)
+
+    def product(buffer, imag, half):
+        left, right = lefts[buffer], rights[buffer]
+        if imag:
+            lhs = jnp.concatenate([left[k, :, width:], -left[k, :, :width]], axis=1)
+        else:
+            lhs = left[k]
+        return lax.dot_general(
+            lhs, right[k, half * n // 2 : (half + 1) * n // 2], NT, preferred_element_type=F32
+        )
+
+    def accumulate(buffer, imag, half, fresh):
+        out = product(buffer, imag, half)
+        rows, cols = slice(imag * n, imag * n + n), slice(half * n // 2, (half + 1) * n // 2)
+        if fresh is None:
+            model_ref[rows, cols] += out
+        else:
+            model_ref[rows, cols] = jnp.where(fresh, 0.0, model_ref[rows, cols]) + out
+
+    for sub in range(2):
+        chunk = 2 * g + sub
+        other = 1 - sub
+
+        @pl.when(g > 0)
+        def _():
+            for copy in out_copies(chunk - 2, sub):
+                copy.wait()
+
+        for f in range(6):
+            for j in range(tiles):
+                row = parts[f, pl.ds(tiles * chunk + j, 1)]
+                wides[sub][f, :, 128 * j : 128 * j + 128] = jnp.broadcast_to(row, (8, 128))
+        for piece in range(4):
+            accumulate(other, piece // 2, piece % 2, chunk <= 1)
+            for i in range(quarter // 8):
+                phases(sub, piece * quarter + 8 * i)
+        for copy in out_copies(chunk, sub):
+            copy.start()
+
+    @pl.when(g == pl.num_programs(0) - 1)
     def _():
-        model_ref[...] += product
+        for piece in range(4):
+            accumulate(1, piece // 2, piece % 2, None)
+        for sub in range(2):
+            for copy in out_copies(2 * g + sub, sub):
+                copy.wait()
 
 
 def model_kernel(right_ref, left_ref, model_ref):
-    steps = 4
-    rw = right_ref.shape[2] // steps
-    width = rw // 2
+    chunks, half = left_ref.shape[0], left_ref.shape[3] // 2
     lefts = []
-    for q in range(steps):
+    for q in range(chunks):
+        cosine, sine = left_ref[q, 0, :, :half], left_ref[q, 0, :, half:]
         lefts.append(
             jnp.concatenate(
-                [
-                    left_ref[0, :, 3 * width * q : 3 * width * q + 2 * width],
-                    left_ref[0, :, 3 * width * q + width : 3 * width * q + 3 * width],
-                ],
-                axis=0,
+                [jnp.concatenate([cosine, sine], axis=1), jnp.concatenate([sine, -cosine], axis=1)], axis=0
             )
         )
     model_ref[0] = lax.dot_general(
-        jnp.concatenate(lefts, axis=1), right_ref[0], NT, preferred_element_type=F32
+        jnp.concatenate(lefts, axis=1),
+        jnp.concatenate([right_ref[q, 0] for q in range(chunks)], axis=1),
+        NT,
+        preferred_element_type=F32,
     )
 
 
@@ -339,10 +377,10 @@
 def per_device(visibilities, calibrator, catalog, assignment, stations, input_order, station_flags):
     rows, n = visibilities.shape[2], visibilities.shape[3]
     sources = 64 * CAP
-    width = 512
-    chunks = sources // width
+    chunks = sources // 256
     whole = pl.BlockSpec(memory_space=VMEM)
     smem = pl.BlockSpec(memory_space=pltpu.SMEM)
+    hbm = pl.BlockSpec(memory_space=pltpu.HBM)
     small = pltpu.CompilerParams(vmem_limit_bytes=24 << 20)
 
     def shape(*dims, dtype=F32):
@@ -351,22 +389,19 @@
     def ring(s):
         return [(i, (i + s) % 4) for i in range(4)]
 
-    spread = pl.pallas_call(
-        spread_kernel,
-        out_shape=[shape(2, rows, n)] * 4,
-        in_specs=[whole],
-        out_specs=[whole] * 4,
-        compiler_params=small,
-        name="spread",
-    )(visibilities)
-    tiles = [spread[0]] + [lax.ppermute(spread[s], "stn", ring(s)) for s in (1, 2, 3)]
-
-    send, xb, yb, ok = pl.pallas_call(
+    send, place = pl.pallas_call(
         route_kernel,
-        out_shape=[shape(64, 1, 5 * CAP), shape(n, 128), shape(n, 128), shape(8, n)],
-        in_specs=[pl.BlockSpec(memory_space=pl.ANY)] + [whole] * 4,
-        out_specs=[whole] * 4,
-        scratch_shapes=[VMEM((8, 128), jnp.int32), pltpu.SemaphoreType.DMA],
+        out_shape=[shape(64, 1, 5 * CAP), shape(8, n)],
+        in_specs=[hbm] * 5,
+        out_specs=[whole] * 2,
+        scratch_shapes=[
+            VMEM((8, 128), jnp.int32),
+            VMEM(catalog.shape, F32),
+            VMEM(stations.shape, F32),
+            VMEM((1, n), jnp.int32),
+            VMEM((1, n), jnp.int32),
+            pltpu.SemaphoreType.DMA((5,)),
+        ],
         compiler_params=small,
         name="route",
     )(
@@ -377,31 +412,42 @@
         station_flags.reshape(1, n),
     )
     received = lax.all_to_all(send, "chan", 0, 0)
-    components = received.reshape(64, 5, CAP).transpose(1, 0, 2).reshape(5, sources)
+
+    spread = pl.pallas_call(
+        spread_kernel,
+        out_shape=[shape(2, rows, n)] * 4,
+        in_specs=[whole],
+        out_specs=[whole] * 4,
+        compiler_params=small,
+        name="spread",
+    )(visibilities)
+    tiles = [spread[0]] + [lax.ppermute(spread[s], "stn", ring(s)) for s in (1, 2, 3)]
 
     right, left, model_own = pl.pallas_call(
         phasor_kernel,
-        grid=(chunks,),
+        grid=(chunks // 2,),
         out_shape=[
-            shape(4, n, 2 * sources, dtype=BF16),
-            shape(4, rows, 3 * sources, dtype=BF16),
+            shape(chunks, 4, n, 512, dtype=BF16),
+            shape(chunks, 4, rows, 512, dtype=BF16),
             shape(2 * n, n),
         ],
         in_specs=[
-            pl.BlockSpec((5, width), lambda q: (0, q)),
-            pl.BlockSpec((n, 128), lambda q: (0, 0)),
-            pl.BlockSpec((n, 128), lambda q: (0, 0)),
-        ],
-        out_specs=[
-            pl.BlockSpec((4, n, 2 * width), lambda q: (0, 0, q)),
-            pl.BlockSpec((4, rows, 3 * width), lambda q: (0, 0, q)),
-            pl.BlockSpec((2 * n, n), lambda q: (0, 0)),
-        ],
-        scratch_shapes=[VMEM((6, 16, width), F32), VMEM((n, 3 * width), BF16)],
+            pl.BlockSpec((64, 1, 5 * CAP), lambda g: (0, 0, 0)),
+            pl.BlockSpec((8, n), lambda g: (0, 0)),
+        ],
+        out_specs=[hbm, hbm, pl.BlockSpec((2 * n, n), lambda g: (0, 0))],
+        scratch_shapes=[
+            VMEM((6, 16, 128), F32),
+            VMEM((2, n, 128), F32),
+            [VMEM((4, n, 512), BF16)] * 2,
+            [VMEM((4, n, 512), BF16)] * 2,
+            [VMEM((6, 8, 256), F32)] * 2,
+            pltpu.SemaphoreType.DMA((4,)),
+        ],
         compiler_params=pltpu.CompilerParams(vmem_limit_bytes=32 << 20),
         cost_estimate=pl.CostEstimate(flops=10 << 30, bytes_accessed=21 << 20, transcendentals=0),
         name="phasor",
-    )(components, xb, yb)
+    )(received, place)
 
     solved = pl.pallas_call(
         solve_kernel,
@@ -411,7 +457,7 @@
         scratch_shapes=[VMEM((n, n), F32)] * 3 + [VMEM((3, 8, n), F32), VMEM((3, n, 128), F32)],
         compiler_params=small,
         name="solve",
-    )(model_own, *tiles, ok, calibrator)
+    )(model_own, *tiles, place, calibrator)
     tables = [solved] + [lax.ppermute(solved, "stn", ring(s)) for s in (1, 2, 3)]
 
     model = pl.pallas_call(
@@ -419,8 +465,8 @@
         grid=(4,),
         out_shape=shape(4, 2 * rows, n),
         in_specs=[
-            pl.BlockSpec((1, n, 2 * sources), lambda q: (q, 0, 0)),
-            pl.BlockSpec((1, rows, 3 * sources), lambda q: (q, 0, 0)),
+            pl.BlockSpec((chunks, 1, n, 512), lambda q: (0, q, 0, 0)),
+            pl.BlockSpec((chunks, 1, rows, 512), lambda q: (0, q, 0, 0)),
         ],
         out_specs=pl.BlockSpec((1, 2 * rows, n), lambda q: (q, 0, 0)),
         compiler_params=pltpu.CompilerParams(vmem_limit_bytes=32 << 20),
@@ -451,7 +497,7 @@
         scratch_shapes=[VMEM((4, 8, n), F32)],
         compiler_params=small,
         name="residual",
-    )(model, visibilities, *tables, ok, calibrator)
+    )(model, visibilities, *tables, place, calibrator)
     return (gains, residual, changes)
 
 

time: 75.4 us -> 69 us (0.915); the launches traced: 74.9 us -> 67.7 us
  local copies, waits for them, and re-layouts: 9.37 us -> 4.98 us
  Pallas kernels: 38.8 us -> 35.3 us
  waiting for transfers between devices: 3.1 us -> 4.69 us
  starting transfers between devices: 22.9 us -> 22 us
    pallas_call x2, Pallas kernels: 22.3 us -> 18.8 us  [the longest x1 17.2 us: per_device(): pl.pallas_call(phasor_kernel, grid=(chunks // 2,), out_shape=[shape(chunk...]
    unnamed x20 -> x16, local copies, waits for them, and re-layouts: 6.61 us -> 4.98 us
    ppermute x3, waiting for transfers between devices: 0.01 us -> 1.52 us  [per_device(): lax.ppermute(spread[s], 'stn', ring(s))]
    reshape x1 -> x0, local copies, waits for them, and re-layouts: 1.03 us -> none  [per_device(): received.reshape(64, 5, CAP).transpose(1, 0, 2).reshape(5, sources)]
    all_to_all x1 -> x0, local copies, waits for them, and re-layouts: 0.93 us -> none  [per_device(): received = lax.all_to_all(send, 'chan', 0, 0)]
    transpose x1 -> x0, local copies, waits for them, and re-layouts: 0.79 us -> none  [per_device(): received.reshape(64, 5, CAP).transpose(1, 0, 2).reshape(5, sources)]
  transfers between devices with their start and end apart: 7 -> 7, of which waited for: 1 -> 2; matrix products, arithmetic and copies ran while one was open for 4% -> 0% of each run, Pallas kernels for 40% -> 39%
where the time goes in v2:
time: 69 us; the launch traced here: 67.7 us
  Pallas kernels  35.3 us (51%)
  starting transfers between devices  22 us (32%)
  local copies, waits for them, and re-layouts  4.98 us (7%)
  waiting for transfers between devices  4.69 us (7%)
  between operations  0.73 us (1%)
    pallas_call x1, Pallas kernels, per_device(): pl.pallas_call(phasor_kernel, grid=(chunks // 2,), out_shape=[shape(chunk...  17.2 us
    all_to_all x1, starting transfers between devices, per_device(): received = lax.all_to_all(send, 'chan', 0, 0)  13.2 us
    pallas_call x1, Pallas kernels, per_device(): pl.pallas_call(model_kernel, grid=(4,), out_shape=shape(4, 2 * rows, n),...  8.61 us
    unnamed x16, local copies, waits for them, and re-layouts  4.98 us
    ppermute x3, starting transfers between devices, per_device(): lax.ppermute(spread[s], 'stn', ring(s))  4.82 us
    ppermute x3, starting transfers between devices, per_device(): lax.ppermute(solved, 'stn', ring(s))  4.01 us
    pallas_call x1, Pallas kernels, per_device(): pl.pallas_call(solve_kernel, out_shape=shape(8, n), in_specs=[whole] * 6...  3.99 us
    all_to_all x1, waiting for transfers between devices, per_device(): received = lax.all_to_all(send, 'chan', 0, 0)  3.16 us
  transfers between devices with their start and end apart: 7, of which 2 were waited for; matrix products, arithmetic and copies ran while one was open for 0% of the time, Pallas kernels for 39%

profile of v2, /device:TPU:1, one launch (start us, length us, event | category | flops | bytes accessed | tf_op | source)
XLA Modules:
  0.0 67.7 jit_solution(3618497708389741912)
XLA Ops:
  0.6 0.0 copy-start.2
  0.6 0.9 %copy-done.2 = s32[65536,1]{0,1:T(1,128)S(1)} copy-done((s32[65536,1]{0,1:T(1,128)S(1)}, s32[65536,1]{0,1:T(1,128)}, u32[]{:S(2)}) %copy-start.2) | copy-done | bytes 262168
  1.6 0.0 copy-start.3
  1.6 0.8 %copy-done.3 = f32[5,1024]{1,0:T(8,128)S(1)} copy-done((f32[5,1024]{1,0:T(8,128)S(1)}, f32[5,1024]{1,0:T(8,128)}, u32[]{:S(2)}) %copy-start.3) | copy-done | bytes 20504
  2.3 0.0 copy-start.4
  2.3 0.7 %copy-done.4 = f32[2,512]{1,0:T(2,128)S(1)} copy-done((f32[2,512]{1,0:T(2,128)S(1)}, f32[2,512]{1,0:T(2,128)}, u32[]{:S(2)}) %copy-start.4) | copy-done | bytes 4120
  3.0 0.0 copy-start.5
  3.0 0.7 %copy-done.5 = s32[512]{0:T(512)S(1)} copy-done((s32[512]{0:T(512)S(1)}, s32[512]{0:T(512)}, u32[]{:S(2)}) %copy-start.5) | copy-done | bytes 2072
  3.7 0.0 copy-start.6
  3.7 0.7 %copy-done.6 = s32[512]{0:T(512)S(1)} copy-done((s32[512]{0:T(512)S(1)}, s32[512]{0:T(512)}, u32[]{:S(2)}) %copy-start.6) | copy-done | bytes 2072
  4.4 1.7 %route.1 = (f32[64,1,160]{2,1,0:T(1,128)}, f32[8,512]{1,0:T(8,128)S(1)}) custom-call(s32[512,128]{1,0:T(8,128)S(1)} %bitcast.3, f32[5,1024]{1,0:T(8,128)S(1)} %copy-done.3, f32[2,512]{1,0:T(2,128)S(1)} %copy-done.4, s32[1,512]{1,0:T(1,128)S(1)} %bitcast.4, s32[1,512]{1,0:T(1,128)S(1)} %bitcast.5), custom_call_target="tpu_custom_call" | custom-call | tf_op jit(solution)/shard_map/route/pallas_call | solution.py:392
  6.1 13.2 %all-to-all-start = ((f32[64,1,160]{2,1,0:T(1,128)}), f32[64,1,160]{2,1,0:T(1,128)S(1)}, u32[]{:S(2)}, u32[]{:S(2)}) async-start(f32[64,1,160]{2,1,0:T(1,128)} %get-tuple-element.12), calls=%async_computation | async-start | bytes 131072 | tf_op jit(solution)/shard_map/all_to_all | solution.py:414
  19.2 0.0 copy-start
  19.3 1.2 %copy-done = bf16[2,4,128,512]{3,2,1,0:T(8,128)(2,1)S(1)} copy-done((bf16[2,4,128,512]{3,2,1,0:T(8,128)(2,1)S(1)}, bf16[2,4,128,512]{3,2,1,0:T(8,128)(2,1)}, u32[]{:S(2)}) %copy-start) | copy-done | bytes 1048600
  20.5 0.9 %spread.1 = (f32[2,128,512]{2,1,0:T(8,128)S(1)}, f32[2,128,512]{2,1,0:T(8,128)}, f32[2,128,512]{2,1,0:T(8,128)S(1)}, f32[2,128,512]{2,1,0:T(8,128)S(1)}) custom-call(bf16[2,4,128,512]{3,2,1,0:T(8,128)(2,1)S(1)} %copy-done), custom_call_target="tpu_custom_call" | custom-call | tf_op jit(solution)/shard_map/spread/pallas_call | solution.py:416
  21.4 1.2 %collective-permute-start = (f32[2,128,512]{2,1,0:T(8,128)}, f32[2,128,512]{2,1,0:T(8,128)S(1)}, u32[]{:S(2)}, u32[]{:S(2)}) collective-permute-start(f32[2,128,512]{2,1,0:T(8,128)} %get-tuple-element.18), channel_id=1, source_target_pairs={{0,1},{1,2},{2,3},{3,0},{4,5},{5,6},{6,7},{7,4},{8,9},{9,10},{10,1... | collective-permute-start | bytes 1572872 | tf_op jit(solution)/shard_map/ppermute | solution.py:424
  22.6 2.5 %collective-permute-start.1 = (f32[2,128,512]{2,1,0:T(8,128)S(1)}, f32[2,128,512]{2,1,0:T(8,128)S(1)}, u32[]{:S(2)}, u32[]{:S(2)}) collective-permute-start(f32[2,128,512]{2,1,0:T(8,128)S(1)} %get-tuple-element.19), channel_id=1, source_target_pairs={{0,2},{1,3},{2,0},{3,1},{4,6},{5,7},{6,4},{7,5},{8,10},{9,11},{10,... | collective-permute-start | bytes 1572872 | tf_op jit(solution)/shard_map/ppermute | solution.py:424
  25.0 1.2 %collective-permute-start.2 = (f32[2,128,512]{2,1,0:T(8,128)S(1)}, f32[2,128,512]{2,1,0:T(8,128)S(1)}, u32[]{:S(2)}, u32[]{:S(2)}) collective-permute-start(f32[2,128,512]{2,1,0:T(8,128)S(1)} %get-tuple-element.20), channel_id=1, source_target_pairs={{0,3},{1,0},{2,1},{3,2},{4,7},{5,4},{6,5},{7,6},{8,11},{9,8},{10,9... | collective-permute-start | bytes 1572872 | tf_op jit(solution)/shard_map/ppermute | solution.py:424
  26.2 3.2 %all-to-all-done.recv_ref = f32[64,1,160]{2,1,0:T(1,128)S(1)} async-done(((f32[64,1,160]{2,1,0:T(1,128)}), f32[64,1,160]{2,1,0:T(1,128)S(1)}, u32[]{:S(2)}, u32[]{:S(2)}) %all-to-all-start) | async-done | bytes 40992 | tf_op jit(solution)/shard_map/all_to_all | solution.py:414
  29.3 0.0 copy-start.7
  29.3 17.2 %phasor.1 = (bf16[8,4,512,512]{3,2,1,0:T(8,128)(2,1)}, bf16[8,4,128,512]{3,2,1,0:T(8,128)(2,1)S(1)}, f32[1024,512]{1,0:T(8,128)S(1)}) custom-call(f32[64,1,160]{2,1,0:T(1,128)S(1)} %all-to-all-done.recv_ref, f32[8,512]{1,0:T(8,128)S(1)} %get-tuple-element.13.place_ref.ok_ref), custom_call_target="tpu_custom_call" | custom-call | flops 10737418240 | bytes 22020096 | tf_op jit(solution)/shard_map/phasor/pallas_call | solution.py:426
  46.5 0.0 collective-permute-done.v1
  46.5 1.5 %collective-permute-done.1.v2 = f32[2,128,512]{2,1,0:T(8,128)S(1)} collective-permute-done((f32[2,128,512]{2,1,0:T(8,128)S(1)}, f32[2,128,512]{2,1,0:T(8,128)S(1)}, u32[]{:S(2)}, u32[]{:S(2)}) %collective-permute-start.1) | collective-permute-done | bytes 524320 | tf_op jit(solution)/shard_map/ppermute | solution.py:424
  48.0 0.0 collective-permute-done.2.v3
  48.0 0.0 copy-done.7
  48.0 4.0 %solve.1.g0 = f32[8,512]{1,0:T(8,128)S(1)} custom-call(f32[1024,512]{1,0:T(8,128)S(1)} %get-tuple-element.16.model_ref, f32[2,128,512]{2,1,0:T(8,128)S(1)} %get-tuple-element.17.v0, f32[2,128,512]{2,1,0:T(8,128)S(1)} %collective-permute-done.v1, f32[2,128,512]{2,1,0:T(8,128)S(1)} %collective-permute-done.1.v2, f32[2,128,512]{2,1,0:T(8,128)S(1)} %collective-permute-done.2.v3, ...), custom_call_target="tpu_custom_call" | custom-call | tf_op jit(solution)/shard_map/solve/pallas_call | solution.py:452
  52.0 1.0 %collective-permute-start.3 = (f32[8,512]{1,0:T(8,128)S(1)}, f32[8,512]{1,0:T(8,128)S(1)}, u32[]{:S(2)}, u32[]{:S(2)}) collective-permute-start(f32[8,512]{1,0:T(8,128)S(1)} %solve.1.g0), channel_id=1, source_target_pairs={{0,1},{1,2},{2,3},{3,0},{4,5},{5,6},{6,7},{7,4},{8,9},{9,10},{10,1... | collective-permute-start | bytes 49160 | tf_op jit(solution)/shard_map/ppermute | solution.py:461
  53.0 2.8 %collective-permute-start.4 = (f32[8,512]{1,0:T(8,128)S(1)}, f32[8,512]{1,0:T(8,128)S(1)}, u32[]{:S(2)}, u32[]{:S(2)}) collective-permute-start(f32[8,512]{1,0:T(8,128)S(1)} %solve.1.g0), channel_id=1, source_target_pairs={{0,2},{1,3},{2,0},{3,1},{4,6},{5,7},{6,4},{7,5},{8,10},{9,11},{10,... | collective-permute-start | bytes 49160 | tf_op jit(solution)/shard_map/ppermute | solution.py:461
  55.8 0.2 collective-permute-start.5
  56.0 0.0 copy-start.1
  56.0 8.6 %model.1.model_ref = f32[4,256,512]{2,1,0:T(8,128)S(1)} custom-call(bf16[8,4,512,512]{3,2,1,0:T(8,128)(2,1)} %get-tuple-element.14.right_ref, bf16[8,4,128,512]{3,2,1,0:T(8,128)(2,1)S(1)} %get-tuple-element.15.left_ref), custom_call_target="tpu_custom_call" | custom-call | flops 5368709120 | bytes 22020096 | tf_op jit(solution)/shard_map/model/pallas_call | solution.py:463
  64.7 0.0 collective-permute-done.3.g1
  64.7 0.0 collective-permute-done.4.g2
  64.7 0.0 collective-permute-done.5.g3
  64.7 0.0 copy-done.1
  64.7 3.0 %residual.1 = (f32[2,4,128]{2,1,0:T(4,128)}, bf16[2,4,128,512]{3,2,1,0:T(8,128)(2,1)}, f32[3,4]{1,0:T(4,128)}) custom-call(f32[4,256,512]{2,1,0:T(8,128)S(1)} %model.1.model_ref, bf16[2,4,128,512]{3,2,1,0:T(8,128)(2,1)S(1)} %copy-done.1, f32[8,512]{1,0:T(8,128)S(1)} %solve.1.g0, f32[8,512]{1,0:T(8,128)S(1)} %collective-permute-done.3.g1, ...), custom_call_target="tpu_custom_call" | custom-call | tf_op jit(solution)/shard_map/residual/pallas_call | solution.py:478
Async XLA Ops:
  0.6 1.0 %copy-start.2 = (s32[65536,1]{0,1:T(1,128)S(1)}, s32[65536,1]{0,1:T(1,128)}, u32[]{:S(2)}) copy-start(s32[65536,1]{0,1:T(1,128)} %param.10) | copy-start | bytes 786436
  1.6 0.8 %copy-start.3 = (f32[5,1024]{1,0:T(8,128)S(1)}, f32[5,1024]{1,0:T(8,128)}, u32[]{:S(2)}) copy-start(f32[5,1024]{1,0:T(8,128)} %cat_hbm.1) | copy-start | bytes 61444
  2.3 0.7 %copy-start.4 = (f32[2,512]{1,0:T(2,128)S(1)}, f32[2,512]{1,0:T(2,128)}, u32[]{:S(2)}) copy-start(f32[2,512]{1,0:T(2,128)} %st_hbm.1) | copy-start | bytes 12292
  3.0 0.7 %copy-start.5 = (s32[512]{0:T(512)S(1)}, s32[512]{0:T(512)}, u32[]{:S(2)}) copy-start(s32[512]{0:T(512)} %param.12) | copy-start | bytes 6148
  3.7 0.7 %copy-start.6 = (s32[512]{0:T(512)S(1)}, s32[512]{0:T(512)}, u32[]{:S(2)}) copy-start(s32[512]{0:T(512)} %param.13) | copy-start | bytes 6148
  6.1 23.3 %all-to-all-start = ((f32[64,1,160]{2,1,0:T(1,128)}), f32[64,1,160]{2,1,0:T(1,128)S(1)}, u32[]{:S(2)}, u32[]{:S(2)}) async-start(f32[64,1,160]{2,1,0:T(1,128)} %get-tuple-element.12), calls=%async_computation | async-start | bytes 131072 | tf_op jit(solution)/shard_map/all_to_all | solution.py:414
  19.2 1.2 %copy-start = (bf16[2,4,128,512]{3,2,1,0:T(8,128)(2,1)S(1)}, bf16[2,4,128,512]{3,2,1,0:T(8,128)(2,1)}, u32[]{:S(2)}) copy-start(bf16[2,4,128,512]{3,2,1,0:T(8,128)(2,1)} %vis_ref.3) | copy-start | bytes 3145732
  21.4 25.1 %collective-permute-start = (f32[2,128,512]{2,1,0:T(8,128)}, f32[2,128,512]{2,1,0:T(8,128)S(1)}, u32[]{:S(2)}, u32[]{:S(2)}) collective-permute-start(f32[2,128,512]{2,1,0:T(8,128)} %get-tuple-element.18), channel_id=1, source_target_pairs={{0,1},{1,2},{2,3},{3,0},{4,5},{5,6},{6,7},{7,4},{8,9},{9,10},{10,1... | collective-permute-start | bytes 1572872 | tf_op jit(solution)/shard_map/ppermute | solution.py:424
  22.6 25.5 %collective-permute-start.1 = (f32[2,128,512]{2,1,0:T(8,128)S(1)}, f32[2,128,512]{2,1,0:T(8,128)S(1)}, u32[]{:S(2)}, u32[]{:S(2)}) collective-permute-start(f32[2,128,512]{2,1,0:T(8,128)S(1)} %get-tuple-element.19), channel_id=1, source_target_pairs={{0,2},{1,3},{2,0},{3,1},{4,6},{5,7},{6,4},{7,5},{8,10},{9,11},{10,... | collective-permute-start | bytes 1572872 | tf_op jit(solution)/shard_map/ppermute | solution.py:424
  25.0 23.0 %collective-permute-start.2 = (f32[2,128,512]{2,1,0:T(8,128)S(1)}, f32[2,128,512]{2,1,0:T(8,128)S(1)}, u32[]{:S(2)}, u32[]{:S(2)}) collective-permute-start(f32[2,128,512]{2,1,0:T(8,128)S(1)} %get-tuple-element.20), channel_id=1, source_target_pairs={{0,3},{1,0},{2,1},{3,2},{4,7},{5,4},{6,5},{7,6},{8,11},{9,8},{10,9... | collective-permute-start | bytes 1572872 | tf_op jit(solution)/shard_map/ppermute | solution.py:424
  29.3 18.7 %copy-start.7 = (f32[4]{0:T(128)S(1)}, f32[4]{0:T(128)}, u32[]{:S(2)}) copy-start(f32[4]{0:T(128)} %cal_ref.3) | copy-start | bytes 52
  52.0 12.6 %collective-permute-start.3 = (f32[8,512]{1,0:T(8,128)S(1)}, f32[8,512]{1,0:T(8,128)S(1)}, u32[]{:S(2)}, u32[]{:S(2)}) collective-permute-start(f32[8,512]{1,0:T(8,128)S(1)} %solve.1.g0), channel_id=1, source_target_pairs={{0,1},{1,2},{2,3},{3,0},{4,5},{5,6},{6,7},{7,4},{8,9},{9,10},{10,1... | collective-permute-start | bytes 49160 | tf_op jit(solution)/shard_map/ppermute | solution.py:461
  53.0 11.6 %collective-permute-start.4 = (f32[8,512]{1,0:T(8,128)S(1)}, f32[8,512]{1,0:T(8,128)S(1)}, u32[]{:S(2)}, u32[]{:S(2)}) collective-permute-start(f32[8,512]{1,0:T(8,128)S(1)} %solve.1.g0), channel_id=1, source_target_pairs={{0,2},{1,3},{2,0},{3,1},{4,6},{5,7},{6,4},{7,5},{8,10},{9,11},{10,... | collective-permute-start | bytes 49160 | tf_op jit(solution)/shard_map/ppermute | solution.py:461
  55.8 8.9 %collective-permute-start.5 = (f32[8,512]{1,0:T(8,128)S(1)}, f32[8,512]{1,0:T(8,128)S(1)}, u32[]{:S(2)}, u32[]{:S(2)}) collective-permute-start(f32[8,512]{1,0:T(8,128)S(1)} %solve.1.g0), channel_id=1, source_target_pairs={{0,3},{1,0},{2,1},{3,2},{4,7},{5,4},{6,5},{7,6},{8,11},{9,8},{10,9... | collective-permute-start | bytes 49160 | tf_op jit(solution)/shard_map/ppermute | solution.py:461
  56.0 8.7 %copy-start.1 = (bf16[2,4,128,512]{3,2,1,0:T(8,128)(2,1)S(1)}, bf16[2,4,128,512]{3,2,1,0:T(8,128)(2,1)}, u32[]{:S(2)}) copy-start(bf16[2,4,128,512]{3,2,1,0:T(8,128)(2,1)} %vis_ref.3) | copy-start | bytes 3145732

commit v3 on v2

v3 whole, which is shorter than its diff:
```python
import jax
import jax.numpy as jnp
from jax import lax
from jax.experimental import pallas as pl
from jax.experimental.pallas import tpu as pltpu
from jax.sharding import PartitionSpec as P


ITERS = 3
CAP = 32
VMEM = pltpu.VMEM
F32 = jnp.float32
BF16 = jnp.bfloat16
NT = (((1,), (1,)), ((), ()))

SIN_HALF = (3.141582005383235, -5.167142124470761, 2.541892570102862, -0.5546189642693115)
COS_HALF = (
    0.999999953374577,
    -4.934792843915727,
    4.05841155956257,
    -1.3318775116821093,
    0.2196907395767838,
)
SIN_STEP = (1.9999932214850844, -0.33258196069982343)
COS_STEP = (1.9999999959214183, -0.9999979659209961, 0.08318303377955542)
ROUND = 12582912.0


def horner(coefficients, x):
    total = coefficients[-1]
    for c in coefficients[-2::-1]:
        total = total * x + c
    return total


def split3(x):
    high = x.astype(BF16).astype(F32)
    rest = x - high
    middle = rest.astype(BF16).astype(F32)
    return high, middle, rest - middle


def front_kernel(
    vis_hbm, assign_hbm, cat_hbm, st_hbm, order_hbm, flag_hbm, cal_hbm, *refs
):
    send_ref, place_ref, tiles = refs[0], refs[1], refs[2:6]
    vis, own, cat, st, order, flag, cal, sem = refs[6:]
    c = lax.axis_index("chan")
    k = lax.axis_index("stn")
    copies = [
        pltpu.make_async_copy(source, target, sem.at[i])
        for i, (source, target) in enumerate(
            (
                (st_hbm, st),
                (order_hbm, order),
                (flag_hbm, flag),
                (assign_hbm.at[pl.ds(pl.multiple_of(c * 8, 8), 8)], own),
                (cat_hbm, cat),
                (vis_hbm, vis),
                (cal_hbm, cal),
            )
        )
    ]
    for copy in copies:
        copy.start()
    n = order.shape[1]
    for copy in copies[:3] + copies[6:]:
        copy.wait()
    hot = (lax.broadcasted_iota(jnp.int32, (n, n), 0) == order[...]).astype(F32).astype(BF16)
    high, middle, low = split3(st[...])
    rows = jnp.concatenate([high, middle, low, flag[...].astype(F32), jnp.zeros((9, n), F32)], axis=0)
    placed = jnp.dot(rows.astype(BF16), hot, preferred_element_type=F32)
    middle_nu = 1.0 + (4.0 * c.astype(F32) + 1.5) * (1.0 / 512.0)
    place_ref[...] = jnp.zeros_like(place_ref)
    place_ref[0:1] = placed[6:7]
    for ch in range(4):
        place_ref[4 + ch : 5 + ch] = jnp.broadcast_to(cal[:, ch : ch + 1], (1, n))
    place_ref[1:2] = (placed[0:1] + placed[2:3] + placed[4:5]) * middle_nu
    place_ref[2:3] = (placed[1:2] + placed[3:4] + placed[5:6]) * middle_nu
    for copy in copies[3:5]:
        copy.wait()
    blocks = lax.broadcasted_iota(jnp.int32, (64, 128), 0)
    hits = [(blocks == own[t : t + 1]).astype(F32) for t in range(8)]
    stacked = jnp.concatenate(hits, axis=0).astype(BF16)
    upper = lax.broadcasted_iota(jnp.int32, (128, 128), 0) <= lax.broadcasted_iota(jnp.int32, (128, 128), 1)
    running = jnp.dot(stacked, upper.astype(F32).astype(BF16), preferred_element_type=F32)
    totals = jnp.dot(stacked, jnp.ones((128, 128), BF16), preferred_element_type=F32)
    before = jnp.full((64, 128), -1.0, F32)
    slot = lax.broadcasted_iota(jnp.int32, (CAP, 128), 0).astype(F32)
    pieces = split3(cat[...])
    left, right = [], []
    for t in range(8):
        part = slice(64 * t, 64 * t + 64)
        rank = jnp.sum(hits[t] * (running[part] + before), axis=0, keepdims=True)
        before = before + totals[part]
        chosen = slot == rank
        hit = hits[t].astype(BF16)
        for piece in pieces:
            left.append(hit)
            here = piece[:, 128 * t : 128 * t + 128]
            right.append(
                jnp.concatenate([jnp.where(chosen, here[f : f + 1], 0.0) for f in range(5)], axis=0).astype(BF16)
            )
    sent = lax.dot_general(
        jnp.concatenate(left, axis=1), jnp.concatenate(right, axis=1), NT, preferred_element_type=F32
    )
    send_ref[:, 0, :] = sent
    copies[5].wait()
    for s in range(4):
        tiles[s][...] = vis[:, lax.rem(k + s, 4)].astype(F32)


def spots_kernel(place_ref, spots_ref, out_ref):
    for axis in range(2):
        for b in range(spots_ref.shape[1] // 128):
            row = place_ref[1 + axis : 2 + axis, 128 * b : 128 * b + 128]
            spots_ref[axis, 128 * b : 128 * b + 128] = jnp.broadcast_to(row, (128, 128)).T
    out_ref[...] = place_ref[...]


def phasor_kernel(recv_ref, spots, place_ref, right_out, left_out, model_ref, parts, bright_rows, rights, lefts, wides, sems):
    c = lax.axis_index("chan")
    k = lax.axis_index("stn")
    n = model_ref.shape[1]
    quarter = n // 4
    width = 256
    pairs = right_out.shape[0] // 2
    tiles = width // 128
    base = 1.0 + 4.0 * c.astype(F32) * (1.0 / 512.0)
    middle_nu = 1.0 + (4.0 * c.astype(F32) + 1.5) * (1.0 / 512.0)
    step = jnp.full((8, width), 2.0 * jnp.pi / 1024.0, F32) / middle_nu

    got = recv_ref[:, 0, :]
    got = jnp.concatenate([got, jnp.zeros((64, 256 - got.shape[1]), F32)], axis=1)
    got = jnp.concatenate([got, jnp.zeros((64, 256), F32)], axis=0).T
    lane = lax.broadcasted_iota(jnp.int32, (16, 128), 1)
    rows = []
    for f in range(5):
        low, high = got[32 * f : 32 * f + 16], got[32 * f + 16 : 32 * f + 32]
        rows.append(jnp.where(lane < 64, low, pltpu.roll(high, 64, 1)))
    parts[0] = rows[0]
    parts[1] = rows[1]
    for ch in range(4):
        log_nu = jnp.log(jnp.full((16, 128), 1.0, F32) * (base + ch / 512.0))
        parts[2 + ch] = rows[2] * jnp.exp(log_nu * (rows[3] + rows[4] * log_nu))

    def out_copies(chunk, buffer):
        return (
            pltpu.make_async_copy(rights[buffer], right_out.at[chunk], sems.at[2 * buffer]),
            pltpu.make_async_copy(
                lefts[buffer].at[:, pl.ds(pl.multiple_of(k * quarter, quarter), quarter)],
                left_out.at[chunk],
                sems.at[2 * buffer + 1],
            ),
        )

    def phases(buffer, r0):
        right, left, wide = rights[buffer], lefts[buffer], wides[buffer]
        rows = slice(r0, r0 + 8)
        x = jnp.concatenate([spots[0, rows]] * tiles, axis=1)
        y = jnp.concatenate([spots[1, rows]] * tiles, axis=1)
        turns = wide[0] * x + wide[1] * y
        r = turns - ((turns + ROUND) - ROUND)
        t = r * r
        s = r * horner(SIN_HALF, t)
        h = horner(COS_HALF, t)
        half_cos = 0.5 - s * s
        half_sin = s * h
        e = turns * step
        e2 = e * e
        s2 = e * horner(SIN_STEP, e2)
        c2 = horner(COS_STEP, e2)
        twice = c2 * c2 - 2.0
        cc, ss = half_cos * c2, half_sin * s2
        sc, cs = half_sin * c2, half_cos * s2
        cos1, cos2 = cc + ss, cc - ss
        sin1, sin2 = sc - cs, sc + cs
        for ch, cosine, sine in (
            (1, cos1, sin1),
            (2, cos2, sin2),
            (0, twice * cos1 - cos2, twice * sin1 - sin2),
            (3, twice * cos2 - cos1, twice * sin2 - sin1),
        ):
            bright = wide[2 + ch]
            right[ch, rows, :width] = (bright * cosine).astype(BF16)
            right[ch, rows, width:] = (bright * sine).astype(BF16)
            left[ch, rows, :width] = cosine.astype(BF16)
            left[ch, rows, width:] = sine.astype(BF16)

    for f in range(2):
        (lefts, rights)[f][1][k] = jnp.zeros((n, 2 * width), BF16)

    def chunks(*totals):
        def matmul(other, turn, block):
            left, right = lefts[other], rights[other]
            columns = slice(turn * width, turn * width + width)
            if block == 0:
                for half in range(2):
                    pltpu.matmul_push_rhs(
                        right[k, half * width : half * width + width, columns], turn, half, transpose=True
                    )
            rows = slice(128 * (block % 4), 128 * (block % 4) + 128)
            if block < 4:
                lhs = left[k, rows, columns]
            else:
                lhs = left[k, rows, (1 - turn) * width : (2 - turn) * width]
                if turn == 1:
                    lhs = -lhs
            for half in range(2):
                pltpu.matmul_acc_lhs(totals[8 * half + block], lhs, turn if block == 0 else None)

        def pair(g, _):
            for sub in range(2):
                chunk = 2 * g + sub

                @pl.when(g > 0)
                def _():
                    for copy in out_copies(chunk - 2, sub):
                        copy.wait()

                for f in range(6):
                    for j in range(tiles):
                        row = parts[f, pl.ds(tiles * chunk + j, 1)]
                        wides[sub][f, :, 128 * j : 128 * j + 128] = jnp.broadcast_to(row, (8, 128))
                for turn in range(2):
                    for block in range(8):

                        def body(sub=sub, turn=turn, block=block):
                            matmul(1 - sub, turn, block)
                            for i in range(4):
                                phases(sub, 32 * (8 * turn + block) + 8 * i)

                        pl.when(g >= 0)(body)
                for copy in out_copies(chunk, sub):
                    copy.start()
            return 0

        lax.fori_loop(0, pairs, pair, 0)
        for turn in range(2):
            for block in range(8):
                matmul(1, turn, block)
        for sub in range(2):
            for copy in out_copies(2 * pairs - 2 + sub, sub):
                copy.wait()
        bright_rows[0:4] = place_ref[4:8, :128]
        bright = bright_rows[pl.ds(k, 1)]
        bright = jnp.concatenate([bright, bright], axis=1)
        off = lax.broadcasted_iota(jnp.int32, (128, 128), 0) != lax.broadcasted_iota(jnp.int32, (128, 128), 1)
        for block in range(8):
            rows = slice(128 * block, 128 * block + 128)
            for half in range(2):
                total = pltpu.matmul_pop(totals[8 * half + block])
                if block < 4:
                    total = total + bright
                for j in range(2):
                    part = total[:, 128 * j : 128 * j + 128]
                    column = 2 * half + j
                    if column == block % 4:
                        part = jnp.where(off, part, 0.0)
                    model_ref[rows, 128 * column : 128 * column + 128] = part

    pl.run_scoped(chunks, *[pltpu.ACC(half)((128, 256), F32) for half in range(2) for _ in range(8)])


def model_kernel(right_ref, left_ref, model_ref):
    chunks, half = left_ref.shape[0], left_ref.shape[3] // 2

    def channel(ch, _):
        lefts = []
        for q in range(chunks):
            left = left_ref[q, ch]
            cosine, sine = left[:, :half], left[:, half:]
            lefts.append(jnp.concatenate([left, jnp.concatenate([sine, -cosine], axis=1)], axis=0))
        model_ref[ch] = lax.dot_general(
            jnp.concatenate(lefts, axis=1),
            jnp.concatenate([right_ref[q, ch] for q in range(chunks)], axis=1),
            NT,
            preferred_element_type=F32,
        )
        return 0

    lax.fori_loop(0, 4, channel, 0)


def solve_kernel(model_ref, v0, v1, v2, v3, ok_ref, out_ref, a_re, a_im, b_ab, wide, part):
    k = lax.axis_index("stn")
    n = v0.shape[2]
    quarter = n // 4
    ok = ok_ref[0:1]

    def fold(x):
        return (x[:, :128] + x[:, 128:256]) + (x[:, 256:384] + x[:, 384:])

    def set_up(s, v):
        first = lax.rem(k + 4 - s, 4) * quarter

        def body(i, _):
            local = pl.multiple_of(8 * i, 8)
            r0 = pl.multiple_of(first + 8 * i, 8)
            mr = model_ref[pl.ds(r0, 8)]
            mi = model_ref[pl.ds(n + r0, 8)]
            vr = v[0, pl.ds(local, 8)]
            vi = v[1, pl.ds(local, 8)]
            ar = mr * vr + mi * vi
            ai = mr * vi - mi * vr
            b = mr * mr + mi * mi
            a_re[pl.ds(r0, 8)] = ar
            a_im[pl.ds(r0, 8)] = ai
            b_ab[pl.ds(r0, 8)] = b
            g = wide[0]
            part[0, pl.ds(r0, 8)] = fold(ar * g)
            part[1, pl.ds(r0, 8)] = fold(ai * g)
            part[2, pl.ds(r0, 8)] = fold(b * g)
            return 0

        lax.fori_loop(0, quarter // 8, body, 0, unroll=4)

    def sums():
        gr, gi, gg = wide[0], wide[1], wide[2]

        def body(i, _):
            r0 = pl.multiple_of(8 * i, 8)
            ar, ai = a_re[pl.ds(r0, 8)], a_im[pl.ds(r0, 8)]
            part[0, pl.ds(r0, 8)] = fold(ar * gr - ai * gi)
            part[1, pl.ds(r0, 8)] = fold(ar * gi + ai * gr)
            part[2, pl.ds(r0, 8)] = fold(b_ab[pl.ds(r0, 8)] * gg)
            return 0

        lax.fori_loop(0, n // 8, body, 0, unroll=4)

    def total(q):
        return jnp.concatenate(
            [jnp.sum(part[q, 128 * b : 128 * b + 128].T, axis=0, keepdims=True) for b in range(n // 128)], axis=1
        )

    g_re, g_im = jnp.ones((1, n), F32), jnp.zeros((1, n), F32)
    out_ref[...] = jnp.zeros_like(out_ref)
    for iteration in range(ITERS):
        wide[0] = jnp.broadcast_to(ok * g_re, (8, n))
        wide[1] = jnp.broadcast_to(ok * g_im, (8, n))
        wide[2] = jnp.broadcast_to(ok * (g_re * g_re + g_im * g_im), (8, n))
        if iteration == 0:
            for s, v in enumerate((v0, v1, v2, v3)):
                set_up(s, v)
        else:
            sums()
        below = total(2) * ok + 1e-6 + (1.0 - ok)
        new_re = total(0) * ok / below
        new_im = total(1) * ok / below
        if iteration % 2 == 1:
            new_re = 0.5 * (new_re + g_re)
            new_im = 0.5 * (new_im + g_im)
        moved = jnp.sum((new_re - g_re) ** 2 + (new_im - g_im) ** 2, axis=1, keepdims=True)
        size = jnp.sum(new_re * new_re + new_im * new_im, axis=1, keepdims=True)
        out_ref[2 + iteration : 3 + iteration] = jnp.broadcast_to(moved / (size + 1e-6), (1, n))
        g_re, g_im = new_re, new_im
    out_ref[0:1] = g_re
    out_ref[1:2] = g_im


def residual_kernel(model_ref, vis_ref, g0, g1, g2, g3, ok_ref, gains_ref, res_ref, change_ref, table, wide):
    k = lax.axis_index("stn")
    ch = pl.program_id(0)
    n = vis_ref.shape[3]
    quarter = n // 4
    lanes = pl.ds(pl.multiple_of(k * quarter, 128), quarter)

    @pl.when(ch == 0)
    def _():
        wide[0:4] = ok_ref[4:8, :128]
        for s, g in enumerate((g0, g1, g2, g3)):
            table[lax.rem(k + 4 - s, 4)] = g[...]
        lane = lax.broadcasted_iota(jnp.int32, (ITERS, 4), 1)
        history = jnp.zeros((ITERS, 4), F32)
        for q in range(4):
            gains_ref[0, q : q + 1] = table[q, 0:1, lanes]
            gains_ref[1, q : q + 1] = table[q, 1:2, lanes]
            history = jnp.where(lane == q, table[q, 2 : 2 + ITERS, 0:4], history)
        change_ref[...] = history

    bright = wide[pl.ds(ch, 1)]

    def column(row):
        return jnp.broadcast_to(row, (128, 128)).T

    gi_re = column(table[ch, 0:1, lanes])
    gi_im = column(table[ch, 1:2, lanes])
    ui = column(ok_ref[0:1, lanes])
    columns = lax.broadcasted_iota(jnp.int32, (16, 128), 1)
    sub = lax.broadcasted_iota(jnp.int32, (16, 128), 0)
    gj_re = [jnp.broadcast_to(table[ch, 0:1, 128 * b : 128 * b + 128], (16, 128)) for b in range(4)]
    gj_im = [jnp.broadcast_to(table[ch, 1:2, 128 * b : 128 * b + 128], (16, 128)) for b in range(4)]
    uj = [jnp.broadcast_to(ok_ref[0:1, 128 * b : 128 * b + 128], (16, 128)) for b in range(4)]
    for i in range(quarter // 16):
        rows = slice(16 * i, 16 * i + 16)
        a_re, a_im, a_ok = gi_re[rows], gi_im[rows], ui[rows]
        for b in range(4):
            at = slice(128 * b, 128 * b + 128)
            off = columns + 128 * b != sub + (k * quarter + 16 * i)
            e = jnp.where(off, a_ok * uj[b], 0.0)
            p_re = a_re * gj_re[b] + a_im * gj_im[b]
            p_im = a_im * gj_re[b] - a_re * gj_im[b]
            mr = model_ref[ch, rows, at] + bright
            mi = model_ref[ch, slice(quarter + 16 * i, quarter + 16 * i + 16), at]
            vr = vis_ref[0, ch, rows, at].astype(F32)
            vi = vis_ref[1, ch, rows, at].astype(F32)
            res_ref[0, 0, rows, at] = (e * (vr - (p_re * mr - p_im * mi))).astype(BF16)
            res_ref[1, 0, rows, at] = (e * (vi - (p_re * mi + p_im * mr))).astype(BF16)


def per_device(visibilities, calibrator, catalog, assignment, stations, input_order, station_flags):
    rows, n = visibilities.shape[2], visibilities.shape[3]
    sources = 64 * CAP
    chunks = sources // 256
    whole = pl.BlockSpec(memory_space=VMEM)
    hbm = pl.BlockSpec(memory_space=pltpu.HBM)
    small = pltpu.CompilerParams(vmem_limit_bytes=8 << 20)

    def shape(*dims, dtype=F32):
        return jax.ShapeDtypeStruct(dims, dtype)

    def ring(s):
        return [(i, (i + s) % 4) for i in range(4)]

    send, place, *own = pl.pallas_call(
        front_kernel,
        out_shape=[shape(64, 1, 5 * CAP), shape(8, n)] + [shape(2, rows, n)] * 4,
        in_specs=[hbm] * 7,
        out_specs=[whole] * 6,
        scratch_shapes=[
            VMEM(visibilities.shape, BF16),
            VMEM((8, 128), jnp.int32),
            VMEM(catalog.shape, F32),
            VMEM(stations.shape, F32),
            VMEM((1, n), jnp.int32),
            VMEM((1, n), jnp.int32),
            VMEM((1, 4), F32),
            pltpu.SemaphoreType.DMA((7,)),
        ],
        name="front",
    )(
        visibilities,
        assignment.reshape(-1, 128),
        catalog,
        stations,
        input_order.reshape(1, n),
        station_flags.reshape(1, n),
        calibrator.reshape(1, 4),
    )

    def turn(s):
        return lax.ppermute(own[s], "stn", ring(s))

    received = lax.all_to_all(send, "chan", 0, 0)
    tiles = [own[0], turn(1), turn(2), turn(3)]
    spots, place = pl.pallas_call(
        spots_kernel,
        out_shape=[shape(2, n, 128), shape(8, n)],
        in_specs=[whole],
        out_specs=[whole] * 2,
        compiler_params=small,
        name="spots",
    )(place)

    right, left, model_own = pl.pallas_call(
        phasor_kernel,
        out_shape=[
            shape(chunks, 4, n, 512, dtype=BF16),
            shape(chunks, 4, rows, 512, dtype=BF16),
            shape(2 * n, n),
        ],
        in_specs=[whole] * 3,
        out_specs=[hbm, hbm, whole],
        scratch_shapes=[
            VMEM((6, 16, 128), F32),
            VMEM((8, 128), F32),
            [VMEM((4, n, 512), BF16)] * 2,
            [VMEM((4, n, 512), BF16)] * 2,
            [VMEM((6, 8, 256), F32)] * 2,
            pltpu.SemaphoreType.DMA((4,)),
        ],
        compiler_params=pltpu.CompilerParams(vmem_limit_bytes=14 << 20),
        cost_estimate=pl.CostEstimate(flops=10 << 30, bytes_accessed=21 << 20, transcendentals=0),
        name="phasor",
    )(received, spots, place)

    solved = pl.pallas_call(
        solve_kernel,
        out_shape=shape(8, n),
        in_specs=[whole] * 6,
        out_specs=whole,
        scratch_shapes=[VMEM((n, n), F32)] * 3 + [VMEM((3, 8, n), F32), VMEM((3, n, 128), F32)],
        compiler_params=small,
        name="solve",
    )(model_own, *tiles, place)
    tables = [solved] + [lax.ppermute(solved, "stn", ring(s)) for s in (1, 2, 3)]

    model = pl.pallas_call(
        model_kernel,
        out_shape=shape(4, 2 * rows, n),
        in_specs=[whole] * 2,
        out_specs=whole,
        compiler_params=small,
        cost_estimate=pl.CostEstimate(flops=5 << 30, bytes_accessed=21 << 20, transcendentals=0),
        name="model",
    )(right, left)

    gains, residual, changes = pl.pallas_call(
        residual_kernel,
        grid=(4,),
        out_shape=[shape(2, 4, rows), shape(2, 4, rows, n, dtype=BF16), shape(ITERS, 4)],
        in_specs=[whole] * 7,
        out_specs=[
            pl.BlockSpec((2, 4, rows), lambda q: (0, 0, 0)),
            pl.BlockSpec((2, 1, rows, n), lambda q: (0, q, 0, 0)),
            pl.BlockSpec((ITERS, 4), lambda q: (0, 0)),
        ],
        scratch_shapes=[VMEM((4, 8, n), F32), VMEM((8, 128), F32)],
        compiler_params=small,
        name="residual",
    )(model, visibilities, *tables, place)
    return (gains, residual, changes)


def solution(mesh):
    placed = (P(None, "chan", "stn", None), P("chan"), P(None, "chan"), P(), P(), P(), P())

    return jax.shard_map(
        per_device,
        mesh=mesh,
        in_specs=placed,
        out_specs=(P(None, "chan", "stn"), P(None, "chan", "stn", None), P(None, "chan")),
        check_vma=False,
    )
```

time: 69 us -> 58.5 us (0.85)
  Pallas kernels: 35.3 us -> 27.2 us
  local copies, waits for them, and re-layouts: 4.98 us -> 0.72 us
  waiting for transfers between devices: 4.69 us -> 7.33 us
    pallas_call x5, Pallas kernels: 32.3 us -> 24.9 us  [the longest x1 13.6 us: per_device(): pl.pallas_call(phasor_kernel, out_shape=[shape(chunks, 4, n, 512, dtype=B...]
    unnamed x16 -> x6, local copies, waits for them, and re-layouts: 4.98 us -> 0.72 us
    ppermute x3, waiting for transfers between devices: 1.52 us -> 3.12 us  [turn(): return lax.ppermute(own[s], 'stn', ring(s))]
    all_to_all x1, waiting for transfers between devices: 3.16 us -> 4.21 us  [per_device(): received = lax.all_to_all(send, 'chan', 0, 0)]
  transfers between devices with their start and end apart: 7 -> 7, of which waited for: 2 -> 2; matrix products, arithmetic and copies ran while one was open for 0% -> 0% of each run, Pallas kernels for 39% -> 33%
where the time goes in v3:
time: 58.5 us; the launch traced here: 57.5 us
  Pallas kernels  27.2 us (46%)
  starting transfers between devices  21.5 us (37%)
  waiting for transfers between devices  7.33 us (13%)
  local copies, waits for them, and re-layouts  0.72 us (1%)
  between operations  0.72 us (1%)
    pallas_call x1, Pallas kernels, per_device(): pl.pallas_call(phasor_kernel, out_shape=[shape(chunks, 4, n, 512, dtype=B...  13.6 us
    all_to_all x1, starting transfers between devices, per_device(): received = lax.all_to_all(send, 'chan', 0, 0)  13.2 us
    pallas_call x1, Pallas kernels, per_device(): pl.pallas_call(model_kernel, out_shape=shape(4, 2 * rows, n), in_specs=[w...  5.09 us
    ppermute x3, starting transfers between devices, turn(): return lax.ppermute(own[s], 'stn', ring(s))  4.9 us
    all_to_all x1, waiting for transfers between devices, per_device(): received = lax.all_to_all(send, 'chan', 0, 0)  4.21 us
    ppermute x3, starting transfers between devices, per_device(): lax.ppermute(solved, 'stn', ring(s))  3.48 us
    pallas_call x1, Pallas kernels, per_device(): pl.pallas_call(front_kernel, out_shape=[shape(64, 1, 5 * CAP), shape(8, n...  3.46 us
    ppermute x3, waiting for transfers between devices, turn(): return lax.ppermute(own[s], 'stn', ring(s))  3.12 us
  transfers between devices with their start and end apart: 7, of which 2 were waited for; matrix products, arithmetic and copies ran while one was open for 0% of the time, Pallas kernels for 33%

profile of v3, /device:TPU:1, one launch (start us, length us, event | category | flops | bytes accessed | tf_op | source)
XLA Modules:
  0.0 57.5 jit_solution(7802296770052515914)
XLA Ops:
  0.6 3.5 %front.1 = (f32[64,1,160]{2,1,0:T(1,128)}, f32[8,512]{1,0:T(8,128)}, f32[2,128,512]{2,1,0:T(8,128)}, f32[2,128,512]{2,1,0:T(8,128)}, f32[2,128,512]{2,1,0:T(8,128)}, /*index=5*/f32[2,128,512]{2,1,0:T(8,128)}) custom-call(bf16[2,4,128,512]{3,2,1,0:T(8,128)(2,1)} %vis_ref.1, s32[512,128]{1,0:T(8,128)} %bitcast.4, f32[5,1024]{1,0:T(8,128)} %cat_hbm.1, ...), custom_call_target="tpu_custom_call" | custom-call | tf_op jit(solution)/shard_map/front/pallas_call | solution.py:425
  4.1 13.2 %all-to-all-start = ((f32[64,1,160]{2,1,0:T(1,128)}), f32[64,1,160]{2,1,0:T(1,128)S(1)}, u32[]{:S(2)}, u32[]{:S(2)}) async-start(f32[64,1,160]{2,1,0:T(1,128)} %get-tuple-element.14), calls=%async_computation | async-start | bytes 131072 | tf_op jit(solution)/shard_map/all_to_all | solution.py:454
  17.3 1.3 %collective-permute-start = (f32[2,128,512]{2,1,0:T(8,128)}, f32[2,128,512]{2,1,0:T(8,128)S(1)}, u32[]{:S(2)}, u32[]{:S(2)}) collective-permute-start(f32[2,128,512]{2,1,0:T(8,128)} %get-tuple-element.22), channel_id=1, source_target_pairs={{0,1},{1,2},{2,3},{3,0},{4,5},{5,6},{6,7},{7,4},{8,9},{9,10},{10,1... | collective-permute-start | bytes 1572872 | tf_op jit(solution)/shard_map/ppermute | solution.py:452
  18.6 2.4 %collective-permute-start.1 = (f32[2,128,512]{2,1,0:T(8,128)}, f32[2,128,512]{2,1,0:T(8,128)S(1)}, u32[]{:S(2)}, u32[]{:S(2)}) collective-permute-start(f32[2,128,512]{2,1,0:T(8,128)} %get-tuple-element.23), channel_id=1, source_target_pairs={{0,2},{1,3},{2,0},{3,1},{4,6},{5,7},{6,4},{7,5},{8,10},{9,11},{10,... | collective-permute-start | bytes 1572872 | tf_op jit(solution)/shard_map/ppermute | solution.py:452
  21.0 1.2 %collective-permute-start.2 = (f32[2,128,512]{2,1,0:T(8,128)}, f32[2,128,512]{2,1,0:T(8,128)S(1)}, u32[]{:S(2)}, u32[]{:S(2)}) collective-permute-start(f32[2,128,512]{2,1,0:T(8,128)} %get-tuple-element.24), channel_id=1, source_target_pairs={{0,3},{1,0},{2,1},{3,2},{4,7},{5,4},{6,5},{7,6},{8,11},{9,8},{10,9... | collective-permute-start | bytes 1572872 | tf_op jit(solution)/shard_map/ppermute | solution.py:452
  22.2 0.0 copy-start.2
  22.2 0.7 %copy-done.2 = f32[8,512]{1,0:T(8,128)S(1)} copy-done((f32[8,512]{1,0:T(8,128)S(1)}, f32[8,512]{1,0:T(8,128)}, u32[]{:S(2)}) %copy-start.2) | copy-done | bytes 16408
  22.9 0.2 spots.1
  23.1 4.2 %all-to-all-done.recv_ref = f32[64,1,160]{2,1,0:T(1,128)S(1)} async-done(((f32[64,1,160]{2,1,0:T(1,128)}), f32[64,1,160]{2,1,0:T(1,128)S(1)}, u32[]{:S(2)}, u32[]{:S(2)}) %all-to-all-start) | async-done | bytes 40992 | tf_op jit(solution)/shard_map/all_to_all | solution.py:454
  27.3 0.0 copy-start.1
  27.3 13.6 %phasor.1 = (bf16[8,4,512,512]{3,2,1,0:T(8,128)(2,1)S(1)}, bf16[8,4,128,512]{3,2,1,0:T(8,128)(2,1)S(1)}, f32[1024,512]{1,0:T(8,128)S(1)}) custom-call(f32[64,1,160]{2,1,0:T(1,128)S(1)} %all-to-all-done.recv_ref, f32[2,512,128]{2,1,0:T(8,128)S(1)} %get-tuple-element.16.spots, f32[8,512]{1,0:T(8,128)S(1)} %get-tuple-element.17.place_ref.ok_ref), custom_call_target="tpu_custom_call" | custom-call | flops 10737418240 | bytes 22020096 | tf_op jit(solution)/shard_map/phasor/pallas_call | solution.py:465
  40.9 0.0 collective-permute-done.v1
  40.9 3.1 %collective-permute-done.1.v2 = f32[2,128,512]{2,1,0:T(8,128)S(1)} collective-permute-done((f32[2,128,512]{2,1,0:T(8,128)}, f32[2,128,512]{2,1,0:T(8,128)S(1)}, u32[]{:S(2)}, u32[]{:S(2)}) %collective-permute-start.1) | collective-permute-done | bytes 524320 | tf_op jit(solution)/shard_map/ppermute | solution.py:452
  44.0 0.0 collective-permute-done.2.v3
  44.0 0.0 copy-done.1
  44.0 2.6 %solve.1.g0 = f32[8,512]{1,0:T(8,128)S(1)} custom-call(f32[1024,512]{1,0:T(8,128)S(1)} %get-tuple-element.20.model_ref, f32[2,128,512]{2,1,0:T(8,128)S(1)} %copy-done.1, f32[2,128,512]{2,1,0:T(8,128)S(1)} %collective-permute-done.v1, f32[2,128,512]{2,1,0:T(8,128)S(1)} %collective-permute-done.1.v2, f32[2,128,512]{2,1,0:T(8,128)S(1)} %collective-permute-done.2.v3, ...), custom_call_target="tpu_custom_call" | custom-call | tf_op jit(solution)/shard_map/solve/pallas_call | solution.py:487
  46.6 2.8 %collective-permute-start.5 = (f32[8,512]{1,0:T(8,128)S(1)}, f32[8,512]{1,0:T(8,128)S(1)}, u32[]{:S(2)}, u32[]{:S(2)}) collective-permute-start(f32[8,512]{1,0:T(8,128)S(1)} %solve.1.g0), channel_id=1, source_target_pairs={{0,3},{1,0},{2,1},{3,2},{4,7},{5,4},{6,5},{7,6},{8,11},{9,8},{10,9... | collective-permute-start | bytes 49160 | tf_op jit(solution)/shard_map/ppermute | solution.py:496
  49.4 0.2 collective-permute-start.4
  49.6 0.5 collective-permute-start.3
  50.1 0.0 copy-start
  50.1 5.1 %model.1.model_ref = f32[4,256,512]{2,1,0:T(8,128)S(1)} custom-call(bf16[8,4,512,512]{3,2,1,0:T(8,128)(2,1)S(1)} %get-tuple-element.18.right_ref, bf16[8,4,128,512]{3,2,1,0:T(8,128)(2,1)S(1)} %get-tuple-element.19.left_ref), custom_call_target="tpu_custom_call" | custom-call | flops 5368709120 | bytes 22020096 | tf_op jit(solution)/shard_map/model/pallas_call | solution.py:498
  55.2 0.0 collective-permute-done.5.g3
  55.2 0.0 collective-permute-done.4.g2
  55.2 0.0 collective-permute-done.3.g1
  55.2 0.0 copy-done
  55.2 2.3 %residual.1 = (f32[2,4,128]{2,1,0:T(4,128)}, bf16[2,4,128,512]{3,2,1,0:T(8,128)(2,1)}, f32[3,4]{1,0:T(4,128)}) custom-call(f32[4,256,512]{2,1,0:T(8,128)S(1)} %model.1.model_ref, bf16[2,4,128,512]{3,2,1,0:T(8,128)(2,1)S(1)} %copy-done, f32[8,512]{1,0:T(8,128)S(1)} %solve.1.g0, f32[8,512]{1,0:T(8,128)S(1)} %collective-permute-done.3.g1, ...), custom_call_target="tpu_custom_call" | custom-call | tf_op jit(solution)/shard_map/residual/pallas_call | solution.py:508
Async XLA Ops:
  4.1 23.2 %all-to-all-start = ((f32[64,1,160]{2,1,0:T(1,128)}), f32[64,1,160]{2,1,0:T(1,128)S(1)}, u32[]{:S(2)}, u32[]{:S(2)}) async-start(f32[64,1,160]{2,1,0:T(1,128)} %get-tuple-element.14), calls=%async_computation | async-start | bytes 131072 | tf_op jit(solution)/shard_map/all_to_all | solution.py:454
  17.3 23.6 %collective-permute-start = (f32[2,128,512]{2,1,0:T(8,128)}, f32[2,128,512]{2,1,0:T(8,128)S(1)}, u32[]{:S(2)}, u32[]{:S(2)}) collective-permute-start(f32[2,128,512]{2,1,0:T(8,128)} %get-tuple-element.22), channel_id=1, source_target_pairs={{0,1},{1,2},{2,3},{3,0},{4,5},{5,6},{6,7},{7,4},{8,9},{9,10},{10,1... | collective-permute-start | bytes 1572872 | tf_op jit(solution)/shard_map/ppermute | solution.py:452
  18.6 25.5 %collective-permute-start.1 = (f32[2,128,512]{2,1,0:T(8,128)}, f32[2,128,512]{2,1,0:T(8,128)S(1)}, u32[]{:S(2)}, u32[]{:S(2)}) collective-permute-start(f32[2,128,512]{2,1,0:T(8,128)} %get-tuple-element.23), channel_id=1, source_target_pairs={{0,2},{1,3},{2,0},{3,1},{4,6},{5,7},{6,4},{7,5},{8,10},{9,11},{10,... | collective-permute-start | bytes 1572872 | tf_op jit(solution)/shard_map/ppermute | solution.py:452
  21.0 23.0 %collective-permute-start.2 = (f32[2,128,512]{2,1,0:T(8,128)}, f32[2,128,512]{2,1,0:T(8,128)S(1)}, u32[]{:S(2)}, u32[]{:S(2)}) collective-permute-start(f32[2,128,512]{2,1,0:T(8,128)} %get-tuple-element.24), channel_id=1, source_target_pairs={{0,3},{1,0},{2,1},{3,2},{4,7},{5,4},{6,5},{7,6},{8,11},{9,8},{10,9... | collective-permute-start | bytes 1572872 | tf_op jit(solution)/shard_map/ppermute | solution.py:452
  22.2 0.7 %copy-start.2 = (f32[8,512]{1,0:T(8,128)S(1)}, f32[8,512]{1,0:T(8,128)}, u32[]{:S(2)}) copy-start(f32[8,512]{1,0:T(8,128)} %get-tuple-element.15.place_ref) | copy-start | bytes 49156
  27.3 16.7 %copy-start.1 = (f32[2,128,512]{2,1,0:T(8,128)S(1)}, f32[2,128,512]{2,1,0:T(8,128)}, u32[]{:S(2)}) copy-start(f32[2,128,512]{2,1,0:T(8,128)} %get-tuple-element.21.v0) | copy-start | bytes 1572868
  46.6 8.6 %collective-permute-start.5 = (f32[8,512]{1,0:T(8,128)S(1)}, f32[8,512]{1,0:T(8,128)S(1)}, u32[]{:S(2)}, u32[]{:S(2)}) collective-permute-start(f32[8,512]{1,0:T(8,128)S(1)} %solve.1.g0), channel_id=1, source_target_pairs={{0,3},{1,0},{2,1},{3,2},{4,7},{5,4},{6,5},{7,6},{8,11},{9,8},{10,9... | collective-permute-start | bytes 49160 | tf_op jit(solution)/shard_map/ppermute | solution.py:496
  49.4 5.8 %collective-permute-start.4 = (f32[8,512]{1,0:T(8,128)S(1)}, f32[8,512]{1,0:T(8,128)S(1)}, u32[]{:S(2)}, u32[]{:S(2)}) collective-permute-start(f32[8,512]{1,0:T(8,128)S(1)} %solve.1.g0), channel_id=1, source_target_pairs={{0,2},{1,3},{2,0},{3,1},{4,6},{5,7},{6,4},{7,5},{8,10},{9,11},{10,... | collective-permute-start | bytes 49160 | tf_op jit(solution)/shard_map/ppermute | solution.py:496
  49.6 5.6 %collective-permute-start.3 = (f32[8,512]{1,0:T(8,128)S(1)}, f32[8,512]{1,0:T(8,128)S(1)}, u32[]{:S(2)}, u32[]{:S(2)}) collective-permute-start(f32[8,512]{1,0:T(8,128)S(1)} %solve.1.g0), channel_id=1, source_target_pairs={{0,1},{1,2},{2,3},{3,0},{4,5},{5,6},{6,7},{7,4},{8,9},{9,10},{10,1... | collective-permute-start | bytes 49160 | tf_op jit(solution)/shard_map/ppermute | solution.py:496
  50.1 5.1 %copy-start = (bf16[2,4,128,512]{3,2,1,0:T(8,128)(2,1)S(1)}, bf16[2,4,128,512]{3,2,1,0:T(8,128)(2,1)}, u32[]{:S(2)}) copy-start(bf16[2,4,128,512]{3,2,1,0:T(8,128)(2,1)} %vis_ref.1) | copy-start | bytes 3145732

commit v4 on v3

--- a/solution.py
+++ b/solution.py
@@ -14,16 +14,9 @@
 NT = (((1,), (1,)), ((), ()))
 
 SIN_HALF = (3.141582005383235, -5.167142124470761, 2.541892570102862, -0.5546189642693115)
-COS_HALF = (
-    0.999999953374577,
-    -4.934792843915727,
-    4.05841155956257,
-    -1.3318775116821093,
-    0.2196907395767838,
-)
+COS_HALF = (0.9999932847330446, -4.93393699910271, 4.041270253370243, -1.2220835776975139)
 SIN_STEP = (1.9999932214850844, -0.33258196069982343)
-COS_STEP = (1.9999999959214183, -0.9999979659209961, 0.08318303377955542)
-ROUND = 12582912.0
+COS_STEP = (1.999986449379199, -0.9969952843589359)
 
 
 def horner(coefficients, x):
@@ -40,11 +33,17 @@
     return high, middle, rest - middle
 
 
+def spread_kernel(vis_ref, place_ref, *out_refs):
+    k = lax.axis_index("stn")
+    for s, out_ref in zip((1, 3, 0), out_refs):
+        out_ref[...] = vis_ref[:, lax.rem(k + s, 4)].astype(F32)
+    out_refs[3][...] = place_ref[...]
+
+
 def front_kernel(
     vis_hbm, assign_hbm, cat_hbm, st_hbm, order_hbm, flag_hbm, cal_hbm, *refs
 ):
-    send_ref, place_ref, tiles = refs[0], refs[1], refs[2:6]
-    vis, own, cat, st, order, flag, cal, sem = refs[6:]
+    send_ref, place_ref, far_hbm, vis, own, cat, st, order, flag, cal, sem, wide, out_sem = refs
     c = lax.axis_index("chan")
     k = lax.axis_index("stn")
     copies = [
@@ -56,7 +55,7 @@
                 (flag_hbm, flag),
                 (assign_hbm.at[pl.ds(pl.multiple_of(c * 8, 8), 8)], own),
                 (cat_hbm, cat),
-                (vis_hbm, vis),
+                (vis_hbm.at[:, lax.rem(k + 2, 4)], vis),
                 (cal_hbm, cal),
             )
         )
@@ -77,6 +76,10 @@
         place_ref[4 + ch : 5 + ch] = jnp.broadcast_to(cal[:, ch : ch + 1], (1, n))
     place_ref[1:2] = (placed[0:1] + placed[2:3] + placed[4:5]) * middle_nu
     place_ref[2:3] = (placed[1:2] + placed[3:4] + placed[5:6]) * middle_nu
+    copies[5].wait()
+    wide[...] = vis[...].astype(F32)
+    out = pltpu.make_async_copy(wide, far_hbm, out_sem)
+    out.start()
     for copy in copies[3:5]:
         copy.wait()
     blocks = lax.broadcasted_iota(jnp.int32, (64, 128), 0)
@@ -105,30 +108,24 @@
         jnp.concatenate(left, axis=1), jnp.concatenate(right, axis=1), NT, preferred_element_type=F32
     )
     send_ref[:, 0, :] = sent
-    copies[5].wait()
-    for s in range(4):
-        tiles[s][...] = vis[:, lax.rem(k + s, 4)].astype(F32)
-
-
-def spots_kernel(place_ref, spots_ref, out_ref):
-    for axis in range(2):
-        for b in range(spots_ref.shape[1] // 128):
-            row = place_ref[1 + axis : 2 + axis, 128 * b : 128 * b + 128]
-            spots_ref[axis, 128 * b : 128 * b + 128] = jnp.broadcast_to(row, (128, 128)).T
-    out_ref[...] = place_ref[...]
-
-
-def phasor_kernel(recv_ref, spots, place_ref, right_out, left_out, model_ref, parts, bright_rows, rights, lefts, wides, sems):
+    out.wait()
+
+
+def phasor_kernel(
+    recv_ref, place_ref, right_even, right_odd, left_out, model_ref, parts, spots, bright_rows, lefts, wides, sems
+):
+    rights = (right_even, right_odd)
     c = lax.axis_index("chan")
     k = lax.axis_index("stn")
     n = model_ref.shape[1]
     quarter = n // 4
     width = 256
-    pairs = right_out.shape[0] // 2
+    pairs = right_even.shape[0]
     tiles = width // 128
     base = 1.0 + 4.0 * c.astype(F32) * (1.0 / 512.0)
     middle_nu = 1.0 + (4.0 * c.astype(F32) + 1.5) * (1.0 / 512.0)
     step = jnp.full((8, width), 2.0 * jnp.pi / 1024.0, F32) / middle_nu
+    sin1_by, sin3_by, cos2_by = SIN_STEP[0] * step, SIN_STEP[1] * step * step * step, COS_STEP[1] * step * step
 
     got = recv_ref[:, 0, :]
     got = jnp.concatenate([got, jnp.zeros((64, 256 - got.shape[1]), F32)], axis=1)
@@ -144,33 +141,34 @@
         log_nu = jnp.log(jnp.full((16, 128), 1.0, F32) * (base + ch / 512.0))
         parts[2 + ch] = rows[2] * jnp.exp(log_nu * (rows[3] + rows[4] * log_nu))
 
-    def out_copies(chunk, buffer):
-        return (
-            pltpu.make_async_copy(rights[buffer], right_out.at[chunk], sems.at[2 * buffer]),
-            pltpu.make_async_copy(
-                lefts[buffer].at[:, pl.ds(pl.multiple_of(k * quarter, quarter), quarter)],
-                left_out.at[chunk],
-                sems.at[2 * buffer + 1],
-            ),
+    for axis in range(2):
+        for b in range(n // 128):
+            row = place_ref[1 + axis : 2 + axis, 128 * b : 128 * b + 128]
+            spots[axis, 128 * b : 128 * b + 128] = jnp.broadcast_to(row, (128, 128)).T
+
+    def out_copy(chunk, buffer):
+        return pltpu.make_async_copy(
+            lefts[buffer].at[:, pl.ds(pl.multiple_of(k * quarter, quarter), quarter)],
+            left_out.at[chunk],
+            sems.at[buffer],
         )
 
-    def phases(buffer, r0):
-        right, left, wide = rights[buffer], lefts[buffer], wides[buffer]
+    def phases(buffer, r0, g):
+        right, left, wide = rights[buffer].at[g], lefts[buffer], wides[buffer]
         rows = slice(r0, r0 + 8)
         x = jnp.concatenate([spots[0, rows]] * tiles, axis=1)
         y = jnp.concatenate([spots[1, rows]] * tiles, axis=1)
         turns = wide[0] * x + wide[1] * y
-        r = turns - ((turns + ROUND) - ROUND)
+        r = turns - jnp.round(turns)
         t = r * r
         s = r * horner(SIN_HALF, t)
         h = horner(COS_HALF, t)
         half_cos = 0.5 - s * s
         half_sin = s * h
-        e = turns * step
-        e2 = e * e
-        s2 = e * horner(SIN_STEP, e2)
-        c2 = horner(COS_STEP, e2)
-        twice = c2 * c2 - 2.0
+        square = turns * turns
+        s2 = turns * (sin1_by + sin3_by * square)
+        c2 = COS_STEP[0] + cos2_by * square
+        twice = 2.0 - s2 * s2
         cc, ss = half_cos * c2, half_sin * s2
         sc, cs = half_sin * c2, half_cos * s2
         cos1, cos2 = cc + ss, cc - ss
@@ -187,12 +185,12 @@
             left[ch, rows, :width] = cosine.astype(BF16)
             left[ch, rows, width:] = sine.astype(BF16)
 
-    for f in range(2):
-        (lefts, rights)[f][1][k] = jnp.zeros((n, 2 * width), BF16)
+    lefts[1][k] = jnp.zeros((n, 2 * width), BF16)
+    right_odd[pairs - 1, k] = jnp.zeros((n, 2 * width), BF16)
 
     def chunks(*totals):
-        def matmul(other, turn, block):
-            left, right = lefts[other], rights[other]
+        def matmul(other, turn, block, g):
+            left, right = lefts[other], rights[other].at[g]
             columns = slice(turn * width, turn * width + width)
             if block == 0:
                 for half in range(2):
@@ -215,8 +213,7 @@
 
                 @pl.when(g > 0)
                 def _():
-                    for copy in out_copies(chunk - 2, sub):
-                        copy.wait()
+                    out_copy(chunk - 2, sub).wait()
 
                 for f in range(6):
                     for j in range(tiles):
@@ -226,22 +223,20 @@
                     for block in range(8):
 
                         def body(sub=sub, turn=turn, block=block):
-                            matmul(1 - sub, turn, block)
+                            matmul(1 - sub, turn, block, g if sub else lax.rem(g + pairs - 1, pairs))
                             for i in range(4):
-                                phases(sub, 32 * (8 * turn + block) + 8 * i)
+                                phases(sub, 32 * (8 * turn + block) + 8 * i, g)
 
                         pl.when(g >= 0)(body)
-                for copy in out_copies(chunk, sub):
-                    copy.start()
+                out_copy(chunk, sub).start()
             return 0
 
         lax.fori_loop(0, pairs, pair, 0)
         for turn in range(2):
             for block in range(8):
-                matmul(1, turn, block)
+                matmul(1, turn, block, pairs - 1)
         for sub in range(2):
-            for copy in out_copies(2 * pairs - 2 + sub, sub):
-                copy.wait()
+            out_copy(2 * pairs - 2 + sub, sub).wait()
         bright_rows[0:4] = place_ref[4:8, :128]
         bright = bright_rows[pl.ds(k, 1)]
         bright = jnp.concatenate([bright, bright], axis=1)
@@ -262,24 +257,33 @@
     pl.run_scoped(chunks, *[pltpu.ACC(half)((128, 256), F32) for half in range(2) for _ in range(8)])
 
 
-def model_kernel(right_ref, left_ref, model_ref):
-    chunks, half = left_ref.shape[0], left_ref.shape[3] // 2
-
-    def channel(ch, _):
+def model_kernel(right_even, right_odd, left_ref, own_ref, place_ref, model_ref, wide):
+    k = lax.axis_index("stn")
+    chunks, rows, half = left_ref.shape[0], left_ref.shape[2], left_ref.shape[3] // 2
+    wide[0:4] = place_ref[4:8, :128]
+    first = pl.multiple_of(k * rows, rows)
+    model_ref[k, :rows] = own_ref[pl.ds(first, rows)]
+    model_ref[k, rows:] = own_ref[pl.ds(4 * rows + first, rows)]
+
+    def channel(i, _):
+        ch = lax.rem(k + 1 + i, 4)
         lefts = []
         for q in range(chunks):
             left = left_ref[q, ch]
             cosine, sine = left[:, :half], left[:, half:]
             lefts.append(jnp.concatenate([left, jnp.concatenate([sine, -cosine], axis=1)], axis=0))
-        model_ref[ch] = lax.dot_general(
+        total = lax.dot_general(
             jnp.concatenate(lefts, axis=1),
-            jnp.concatenate([right_ref[q, ch] for q in range(chunks)], axis=1),
+            jnp.concatenate([(right_even, right_odd)[q % 2][q // 2, ch] for q in range(chunks)], axis=1),
             NT,
             preferred_element_type=F32,
         )
+        bright = jnp.concatenate([wide[pl.ds(ch, 1)]] * 4, axis=1)
+        model_ref[ch, :rows] = total[:rows] + bright
+        model_ref[ch, rows:] = total[rows:]
         return 0
 
-    lax.fori_loop(0, 4, channel, 0)
+    lax.fori_loop(0, 3, channel, 0)
 
 
 def solve_kernel(model_ref, v0, v1, v2, v3, ok_ref, out_ref, a_re, a_im, b_ab, wide, part):
@@ -358,7 +362,7 @@
     out_ref[1:2] = g_im
 
 
-def residual_kernel(model_ref, vis_ref, g0, g1, g2, g3, ok_ref, gains_ref, res_ref, change_ref, table, wide):
+def residual_kernel(model_ref, vis_ref, g0, g1, g2, g3, ok_ref, gains_ref, res_ref, change_ref, table):
     k = lax.axis_index("stn")
     ch = pl.program_id(0)
     n = vis_ref.shape[3]
@@ -367,7 +371,6 @@
 
     @pl.when(ch == 0)
     def _():
-        wide[0:4] = ok_ref[4:8, :128]
         for s, g in enumerate((g0, g1, g2, g3)):
             table[lax.rem(k + 4 - s, 4)] = g[...]
         lane = lax.broadcasted_iota(jnp.int32, (ITERS, 4), 1)
@@ -377,8 +380,6 @@
             gains_ref[1, q : q + 1] = table[q, 1:2, lanes]
             history = jnp.where(lane == q, table[q, 2 : 2 + ITERS, 0:4], history)
         change_ref[...] = history
-
-    bright = wide[pl.ds(ch, 1)]
 
     def column(row):
         return jnp.broadcast_to(row, (128, 128)).T
@@ -400,7 +401,7 @@
             e = jnp.where(off, a_ok * uj[b], 0.0)
             p_re = a_re * gj_re[b] + a_im * gj_im[b]
             p_im = a_im * gj_re[b] - a_re * gj_im[b]
-            mr = model_ref[ch, rows, at] + bright
+            mr = model_ref[ch, rows, at]
             mi = model_ref[ch, slice(quarter + 16 * i, quarter + 16 * i + 16), at]
             vr = vis_ref[0, ch, rows, at].astype(F32)
             vi = vis_ref[1, ch, rows, at].astype(F32)
@@ -414,7 +415,7 @@
     chunks = sources // 256
     whole = pl.BlockSpec(memory_space=VMEM)
     hbm = pl.BlockSpec(memory_space=pltpu.HBM)
-    small = pltpu.CompilerParams(vmem_limit_bytes=8 << 20)
+    small = pltpu.CompilerParams(vmem_limit_bytes=6 << 20)
 
     def shape(*dims, dtype=F32):
         return jax.ShapeDtypeStruct(dims, dtype)
@@ -422,13 +423,13 @@
     def ring(s):
         return [(i, (i + s) % 4) for i in range(4)]
 
-    send, place, *own = pl.pallas_call(
+    send, place, far = pl.pallas_call(
         front_kernel,
-        out_shape=[shape(64, 1, 5 * CAP), shape(8, n)] + [shape(2, rows, n)] * 4,
+        out_shape=[shape(64, 1, 5 * CAP), shape(8, n), shape(2, rows, n)],
         in_specs=[hbm] * 7,
-        out_specs=[whole] * 6,
+        out_specs=[whole] * 2 + [hbm],
         scratch_shapes=[
-            VMEM(visibilities.shape, BF16),
+            VMEM((2, rows, n), BF16),
             VMEM((8, 128), jnp.int32),
             VMEM(catalog.shape, F32),
             VMEM(stations.shape, F32),
@@ -436,6 +437,8 @@
             VMEM((1, n), jnp.int32),
             VMEM((1, 4), F32),
             pltpu.SemaphoreType.DMA((7,)),
+            VMEM((2, rows, n), F32),
+            pltpu.SemaphoreType.DMA,
         ],
         name="front",
     )(
@@ -448,41 +451,44 @@
         calibrator.reshape(1, 4),
     )
 
-    def turn(s):
-        return lax.ppermute(own[s], "stn", ring(s))
+    ahead, behind, own, place = pl.pallas_call(
+        spread_kernel,
+        out_shape=[shape(2, rows, n)] * 3 + [shape(8, n)],
+        in_specs=[whole] * 2,
+        out_specs=[whole] * 4,
+        compiler_params=small,
+        cost_estimate=pl.CostEstimate(flops=1 << 20, bytes_accessed=2 << 20, transcendentals=0),
+        name="spread",
+    )(visibilities, place)
+
+    def turn(tile, s):
+        return lax.ppermute(tile, "stn", ring(s))
 
     received = lax.all_to_all(send, "chan", 0, 0)
-    tiles = [own[0], turn(1), turn(2), turn(3)]
-    spots, place = pl.pallas_call(
-        spots_kernel,
-        out_shape=[shape(2, n, 128), shape(8, n)],
-        in_specs=[whole],
-        out_specs=[whole] * 2,
-        compiler_params=small,
-        name="spots",
-    )(place)
-
-    right, left, model_own = pl.pallas_call(
+    tiles = [own, turn(ahead, 1), turn(far, 2), turn(behind, 3)]
+
+    right_even, right_odd, left, model_own = pl.pallas_call(
         phasor_kernel,
         out_shape=[
-            shape(chunks, 4, n, 512, dtype=BF16),
+            shape(chunks // 2, 4, n, 512, dtype=BF16),
+            shape(chunks // 2, 4, n, 512, dtype=BF16),
             shape(chunks, 4, rows, 512, dtype=BF16),
             shape(2 * n, n),
         ],
-        in_specs=[whole] * 3,
-        out_specs=[hbm, hbm, whole],
+        in_specs=[whole] * 2,
+        out_specs=[whole, whole, hbm, whole],
         scratch_shapes=[
             VMEM((6, 16, 128), F32),
+            VMEM((2, n, 128), F32),
             VMEM((8, 128), F32),
             [VMEM((4, n, 512), BF16)] * 2,
-            [VMEM((4, n, 512), BF16)] * 2,
             [VMEM((6, 8, 256), F32)] * 2,
-            pltpu.SemaphoreType.DMA((4,)),
+            pltpu.SemaphoreType.DMA((2,)),
         ],
-        compiler_params=pltpu.CompilerParams(vmem_limit_bytes=14 << 20),
+        compiler_params=pltpu.CompilerParams(vmem_limit_bytes=8 << 20),
         cost_estimate=pl.CostEstimate(flops=10 << 30, bytes_accessed=21 << 20, transcendentals=0),
         name="phasor",
-    )(received, spots, place)
+    )(received, place)
 
     solved = pl.pallas_call(
         solve_kernel,
@@ -498,12 +504,13 @@
     model = pl.pallas_call(
         model_kernel,
         out_shape=shape(4, 2 * rows, n),
-        in_specs=[whole] * 2,
+        in_specs=[whole] * 5,
         out_specs=whole,
+        scratch_shapes=[VMEM((8, 128), F32)],
         compiler_params=small,
-        cost_estimate=pl.CostEstimate(flops=5 << 30, bytes_accessed=21 << 20, transcendentals=0),
+        cost_estimate=pl.CostEstimate(flops=4 << 30, bytes_accessed=21 << 20, transcendentals=0),
         name="model",
-    )(right, left)
+    )(right_even, right_odd, left, model_own, place)
 
     gains, residual, changes = pl.pallas_call(
         residual_kernel,
@@ -515,7 +522,7 @@
             pl.BlockSpec((2, 1, rows, n), lambda q: (0, q, 0, 0)),
             pl.BlockSpec((ITERS, 4), lambda q: (0, 0)),
         ],
-        scratch_shapes=[VMEM((4, 8, n), F32), VMEM((8, 128), F32)],
+        scratch_shapes=[VMEM((4, 8, n), F32)],
         compiler_params=small,
         name="residual",
     )(model, visibilities, *tables, place)

time: 58.5 us -> 56.1 us (0.959)
  Pallas kernels: 27.2 us -> 22.8 us
  local copies, waits for them, and re-layouts: 0.72 us -> 1.94 us
  starting transfers between devices: 21.5 us -> 22.4 us
    pallas_call x2, Pallas kernels: 13.8 us -> 11.5 us  [the longest x1 11.4 us: per_device(): pl.pallas_call(phasor_kernel, out_shape=[shape(chunks // 2, 4, n, 512, dt...]
    ppermute x3, waiting for transfers between devices: 3.12 us -> 5.36 us  [turn(): return lax.ppermute(tile, 'stn', ring(s))]
    all_to_all x1, waiting for transfers between devices: 4.21 us -> 2.45 us  [per_device(): received = lax.all_to_all(send, 'chan', 0, 0)]
    pallas_call x1, Pallas kernels: 5.09 us -> 3.86 us  [per_device(): pl.pallas_call(model_kernel, out_shape=shape(4, 2 * rows, n), in_specs=[w...]
    unnamed x6, local copies, waits for them, and re-layouts: 0.72 us -> 1.94 us
    pallas_call x1, Pallas kernels: 3.46 us -> 2.57 us  [per_device(): pl.pallas_call(front_kernel, out_shape=[shape(64, 1, 5 * CAP), shape(8, n...]
    ppermute x3, starting transfers between devices: 4.9 us -> 5.58 us  [turn(): return lax.ppermute(tile, 'stn', ring(s))]
  transfers between devices with their start and end apart: 7 -> 7, of which waited for: 2 -> 2; matrix products, arithmetic and copies ran while one was open for 0% -> 0% of each run, Pallas kernels for 33% -> 28%
where the time goes in v4:
time: 56.1 us; the launch traced here: 55.7 us
  Pallas kernels  22.8 us (41%)
  starting transfers between devices  22.4 us (40%)
  waiting for transfers between devices  7.82 us (14%)
  local copies, waits for them, and re-layouts  1.94 us (3%)
  between operations  0.71 us (1%)
    all_to_all x1, starting transfers between devices, per_device(): received = lax.all_to_all(send, 'chan', 0, 0)  13.2 us
    pallas_call x1, Pallas kernels, per_device(): pl.pallas_call(phasor_kernel, out_shape=[shape(chunks // 2, 4, n, 512, dt...  11.4 us
    ppermute x3, starting transfers between devices, turn(): return lax.ppermute(tile, 'stn', ring(s))  5.58 us
    ppermute x3, waiting for transfers between devices, turn(): return lax.ppermute(tile, 'stn', ring(s))  5.36 us
    pallas_call x1, Pallas kernels, per_device(): pl.pallas_call(model_kernel, out_shape=shape(4, 2 * rows, n), in_specs=[w...  3.86 us
    ppermute x3, starting transfers between devices, per_device(): lax.ppermute(solved, 'stn', ring(s))  3.63 us
    pallas_call x1, Pallas kernels, per_device(): pl.pallas_call(front_kernel, out_shape=[shape(64, 1, 5 * CAP), shape(8, n...  2.57 us
    pallas_call x1, Pallas kernels, per_device(): pl.pallas_call(solve_kernel, out_shape=shape(8, n), in_specs=[whole] * 6,...  2.56 us
  transfers between devices with their start and end apart: 7, of which 2 were waited for; matrix products, arithmetic and copies ran while one was open for 0% of the time, Pallas kernels for 28%

profile of v4, /device:TPU:1, one launch (start us, length us, event | category | flops | bytes accessed | tf_op | source)
XLA Modules:
  0.0 55.7 jit_solution(7301126832287442516)
XLA Ops:
  0.6 2.6 %front.1 = (f32[64,1,160]{2,1,0:T(1,128)}, f32[8,512]{1,0:T(8,128)}, f32[2,128,512]{2,1,0:T(8,128)}) custom-call(bf16[2,4,128,512]{3,2,1,0:T(8,128)(2,1)} %vis_ref.3, s32[512,128]{1,0:T(8,128)} %bitcast.4, f32[5,1024]{1,0:T(8,128)} %cat_hbm.1, f32[2,512]{1,0:T(2,128)} %st_hbm.1, s32[1,512]{1,0:T(1,128)} %bitcast.5, s32[1,512]{1,0:T(1,128)} %bitcast.6, ...), custom_call_target="tpu_custom_call" | custom-call | tf_op jit(solution)/shard_map/front/pallas_call | solution.py:426
  3.2 13.2 %all-to-all-start = ((f32[64,1,160]{2,1,0:T(1,128)}), f32[64,1,160]{2,1,0:T(1,128)S(1)}, u32[]{:S(2)}, u32[]{:S(2)}) async-start(f32[64,1,160]{2,1,0:T(1,128)} %get-tuple-element.14), calls=%async_computation | async-start | bytes 131072 | tf_op jit(solution)/shard_map/all_to_all | solution.py:467
  16.4 2.8 %collective-permute-start.1 = (f32[2,128,512]{2,1,0:T(8,128)}, f32[2,128,512]{2,1,0:T(8,128)S(1)}, u32[]{:S(2)}, u32[]{:S(2)}) collective-permute-start(f32[2,128,512]{2,1,0:T(8,128)} %get-tuple-element.23), channel_id=1, source_target_pairs={{0,2},{1,3},{2,0},{3,1},{4,6},{5,7},{6,4},{7,5},{8,10},{9,11},{10,... | collective-permute-start | bytes 1572872 | tf_op jit(solution)/shard_map/ppermute | solution.py:465
  19.2 0.0 copy-start
  19.2 1.2 %copy-done = bf16[2,4,128,512]{3,2,1,0:T(8,128)(2,1)S(1)} copy-done((bf16[2,4,128,512]{3,2,1,0:T(8,128)(2,1)S(1)}, bf16[2,4,128,512]{3,2,1,0:T(8,128)(2,1)}, u32[]{:S(2)}) %copy-start) | copy-done | bytes 1048600
  20.4 0.0 copy-start.2
  20.4 0.7 %copy-done.2 = f32[8,512]{1,0:T(8,128)S(1)} copy-done((f32[8,512]{1,0:T(8,128)S(1)}, f32[8,512]{1,0:T(8,128)}, u32[]{:S(2)}) %copy-start.2) | copy-done | bytes 16408
  21.1 0.1 spread.1
  21.3 0.4 collective-permute-start
  21.6 2.4 %collective-permute-start.2 = (f32[2,128,512]{2,1,0:T(8,128)S(1)}, f32[2,128,512]{2,1,0:T(8,128)S(1)}, u32[]{:S(2)}, u32[]{:S(2)}) collective-permute-start(f32[2,128,512]{2,1,0:T(8,128)S(1)} %get-tuple-element.24), channel_id=1, source_target_pairs={{0,3},{1,0},{2,1},{3,2},{4,7},{5,4},{6,5},{7,6},{8,11},{9,8},{10,9... | collective-permute-start | bytes 1572872 | tf_op jit(solution)/shard_map/ppermute | solution.py:465
  24.0 2.5 %all-to-all-done.recv_ref = f32[64,1,160]{2,1,0:T(1,128)S(1)} async-done(((f32[64,1,160]{2,1,0:T(1,128)}), f32[64,1,160]{2,1,0:T(1,128)S(1)}, u32[]{:S(2)}, u32[]{:S(2)}) %all-to-all-start) | async-done | bytes 40992 | tf_op jit(solution)/shard_map/all_to_all | solution.py:467
  26.5 11.4 %phasor.1 = (bf16[4,4,512,512]{3,2,1,0:T(8,128)(2,1)S(1)}, bf16[4,4,512,512]{3,2,1,0:T(8,128)(2,1)S(1)}, bf16[8,4,128,512]{3,2,1,0:T(8,128)(2,1)S(1)}, f32[1024,512]{1,0:T(8,128)S(1)}) custom-call(f32[64,1,160]{2,1,0:T(1,128)S(1)} %all-to-all-done.recv_ref, f32[8,512]{1,0:T(8,128)S(1)} %get-tuple-element.16.place_ref.ok_ref), custom_call_target="tpu_custom_call" | custom-call | flops 10737418240 | bytes 22020096 | tf_op jit(solution)/shard_map/phasor/pallas_call | solution.py:470
  37.9 0.0 collective-permute-done.1.v2
  37.9 5.4 %collective-permute-done.v1 = f32[2,128,512]{2,1,0:T(8,128)S(1)} collective-permute-done((f32[2,128,512]{2,1,0:T(8,128)S(1)}, f32[2,128,512]{2,1,0:T(8,128)S(1)}, u32[]{:S(2)}, u32[]{:S(2)}) %collective-permute-start) | collective-permute-done | bytes 524320 | tf_op jit(solution)/shard_map/ppermute | solution.py:465
  43.3 0.0 collective-permute-done.2.v3
  43.3 2.6 %solve.1.g0 = f32[8,512]{1,0:T(8,128)S(1)} custom-call(f32[1024,512]{1,0:T(8,128)S(1)} %get-tuple-element.20.own_ref.model_ref, f32[2,128,512]{2,1,0:T(8,128)S(1)} %get-tuple-element.21.v0, f32[2,128,512]{2,1,0:T(8,128)S(1)} %collective-permute-done.v1, f32[2,128,512]{2,1,0:T(8,128)S(1)} %collective-permute-done.1.v2, ...), custom_call_target="tpu_custom_call" | custom-call | tf_op jit(solution)/shard_map/solve/pallas_call | solution.py:493
  45.8 2.5 %collective-permute-start.5 = (f32[8,512]{1,0:T(8,128)S(1)}, f32[8,512]{1,0:T(8,128)S(1)}, u32[]{:S(2)}, u32[]{:S(2)}) collective-permute-start(f32[8,512]{1,0:T(8,128)S(1)} %solve.1.g0), channel_id=1, source_target_pairs={{0,3},{1,0},{2,1},{3,2},{4,7},{5,4},{6,5},{7,6},{8,11},{9,8},{10,9... | collective-permute-start | bytes 49160 | tf_op jit(solution)/shard_map/ppermute | solution.py:502
  48.3 0.5 collective-permute-start.4
  48.8 0.6 %collective-permute-start.3 = (f32[8,512]{1,0:T(8,128)S(1)}, f32[8,512]{1,0:T(8,128)S(1)}, u32[]{:S(2)}, u32[]{:S(2)}) collective-permute-start(f32[8,512]{1,0:T(8,128)S(1)} %solve.1.g0), channel_id=1, source_target_pairs={{0,1},{1,2},{2,3},{3,0},{4,5},{5,6},{6,7},{7,4},{8,9},{9,10},{10,1... | collective-permute-start | bytes 49160 | tf_op jit(solution)/shard_map/ppermute | solution.py:502
  49.4 0.0 copy-start.1
  49.4 3.9 %model.1.model_ref = f32[4,256,512]{2,1,0:T(8,128)S(1)} custom-call(bf16[4,4,512,512]{3,2,1,0:T(8,128)(2,1)S(1)} %get-tuple-element.17.right_even, bf16[4,4,512,512]{3,2,1,0:T(8,128)(2,1)S(1)} %get-tuple-element.18.right_odd, bf16[8,4,128,512]{3,2,1,0:T(8,128)(2,1)S(1)} %get-tuple-element.19.left_ref, f32[1024,512]{1,0:T(8,128)S(1)} %get-tuple-element.20.own_ref.model_ref, ...), custom_call_target="tpu_custom_call" | custom-call | flops 4294967296 | bytes 22020096 | tf_op jit(solution)/shard_map/model/pallas_call | solution.py:504
  53.3 0.0 collective-permute-done.5.g3
  53.3 0.0 collective-permute-done.4.g2
  53.3 0.0 collective-permute-done.3.g1
  53.3 0.0 copy-done.1
  53.3 2.3 %residual.1 = (f32[2,4,128]{2,1,0:T(4,128)}, bf16[2,4,128,512]{3,2,1,0:T(8,128)(2,1)}, f32[3,4]{1,0:T(4,128)}) custom-call(f32[4,256,512]{2,1,0:T(8,128)S(1)} %model.1.model_ref, bf16[2,4,128,512]{3,2,1,0:T(8,128)(2,1)S(1)} %copy-done.1, f32[8,512]{1,0:T(8,128)S(1)} %solve.1.g0, f32[8,512]{1,0:T(8,128)S(1)} %collective-permute-done.3.g1, ...), custom_call_target="tpu_custom_call" | custom-call | tf_op jit(solution)/shard_map/residual/pallas_call | solution.py:515
Async XLA Ops:
  3.2 23.3 %all-to-all-start = ((f32[64,1,160]{2,1,0:T(1,128)}), f32[64,1,160]{2,1,0:T(1,128)S(1)}, u32[]{:S(2)}, u32[]{:S(2)}) async-start(f32[64,1,160]{2,1,0:T(1,128)} %get-tuple-element.14), calls=%async_computation | async-start | bytes 131072 | tf_op jit(solution)/shard_map/all_to_all | solution.py:467
  16.4 21.5 %collective-permute-start.1 = (f32[2,128,512]{2,1,0:T(8,128)}, f32[2,128,512]{2,1,0:T(8,128)S(1)}, u32[]{:S(2)}, u32[]{:S(2)}) collective-permute-start(f32[2,128,512]{2,1,0:T(8,128)} %get-tuple-element.23), channel_id=1, source_target_pairs={{0,2},{1,3},{2,0},{3,1},{4,6},{5,7},{6,4},{7,5},{8,10},{9,11},{10,... | collective-permute-start | bytes 1572872 | tf_op jit(solution)/shard_map/ppermute | solution.py:465
  19.2 1.2 %copy-start = (bf16[2,4,128,512]{3,2,1,0:T(8,128)(2,1)S(1)}, bf16[2,4,128,512]{3,2,1,0:T(8,128)(2,1)}, u32[]{:S(2)}) copy-start(bf16[2,4,128,512]{3,2,1,0:T(8,128)(2,1)} %vis_ref.3) | copy-start | bytes 3145732
  20.4 0.7 %copy-start.2 = (f32[8,512]{1,0:T(8,128)S(1)}, f32[8,512]{1,0:T(8,128)}, u32[]{:S(2)}) copy-start(f32[8,512]{1,0:T(8,128)} %get-tuple-element.15.place_ref) | copy-start | bytes 49156
  21.3 22.0 %collective-permute-start = (f32[2,128,512]{2,1,0:T(8,128)S(1)}, f32[2,128,512]{2,1,0:T(8,128)S(1)}, u32[]{:S(2)}, u32[]{:S(2)}) collective-permute-start(f32[2,128,512]{2,1,0:T(8,128)S(1)} %get-tuple-element.22), channel_id=1, source_target_pairs={{0,1},{1,2},{2,3},{3,0},{4,5},{5,6},{6,7},{7,4},{8,9},{9,10},{10,1... | collective-permute-start | bytes 1572872 | tf_op jit(solution)/shard_map/ppermute | solution.py:465
  21.6 21.6 %collective-permute-start.2 = (f32[2,128,512]{2,1,0:T(8,128)S(1)}, f32[2,128,512]{2,1,0:T(8,128)S(1)}, u32[]{:S(2)}, u32[]{:S(2)}) collective-permute-start(f32[2,128,512]{2,1,0:T(8,128)S(1)} %get-tuple-element.24), channel_id=1, source_target_pairs={{0,3},{1,0},{2,1},{3,2},{4,7},{5,4},{6,5},{7,6},{8,11},{9,8},{10,9... | collective-permute-start | bytes 1572872 | tf_op jit(solution)/shard_map/ppermute | solution.py:465
  45.8 7.5 %collective-permute-start.5 = (f32[8,512]{1,0:T(8,128)S(1)}, f32[8,512]{1,0:T(8,128)S(1)}, u32[]{:S(2)}, u32[]{:S(2)}) collective-permute-start(f32[8,512]{1,0:T(8,128)S(1)} %solve.1.g0), channel_id=1, source_target_pairs={{0,3},{1,0},{2,1},{3,2},{4,7},{5,4},{6,5},{7,6},{8,11},{9,8},{10,9... | collective-permute-start | bytes 49160 | tf_op jit(solution)/shard_map/ppermute | solution.py:502
  48.3 5.0 %collective-permute-start.4 = (f32[8,512]{1,0:T(8,128)S(1)}, f32[8,512]{1,0:T(8,128)S(1)}, u32[]{:S(2)}, u32[]{:S(2)}) collective-permute-start(f32[8,512]{1,0:T(8,128)S(1)} %solve.1.g0), channel_id=1, source_target_pairs={{0,2},{1,3},{2,0},{3,1},{4,6},{5,7},{6,4},{7,5},{8,10},{9,11},{10,... | collective-permute-start | bytes 49160 | tf_op jit(solution)/shard_map/ppermute | solution.py:502
  48.8 4.5 %collective-permute-start.3 = (f32[8,512]{1,0:T(8,128)S(1)}, f32[8,512]{1,0:T(8,128)S(1)}, u32[]{:S(2)}, u32[]{:S(2)}) collective-permute-start(f32[8,512]{1,0:T(8,128)S(1)} %solve.1.g0), channel_id=1, source_target_pairs={{0,1},{1,2},{2,3},{3,0},{4,5},{5,6},{6,7},{7,4},{8,9},{9,10},{10,1... | collective-permute-start | bytes 49160 | tf_op jit(solution)/shard_map/ppermute | solution.py:502
  49.4 3.9 %copy-start.1 = (bf16[2,4,128,512]{3,2,1,0:T(8,128)(2,1)S(1)}, bf16[2,4,128,512]{3,2,1,0:T(8,128)(2,1)}, u32[]{:S(2)}) copy-start(bf16[2,4,128,512]{3,2,1,0:T(8,128)(2,1)} %vis_ref.3) | copy-start | bytes 3145732

commit v5 on v4

--- a/solution.py
+++ b/solution.py
@@ -35,15 +35,15 @@
 
 def spread_kernel(vis_ref, place_ref, *out_refs):
     k = lax.axis_index("stn")
-    for s, out_ref in zip((1, 3, 0), out_refs):
+    for s, out_ref in zip((2, 0), out_refs):
         out_ref[...] = vis_ref[:, lax.rem(k + s, 4)].astype(F32)
-    out_refs[3][...] = place_ref[...]
+    out_refs[2][...] = place_ref[...]
 
 
 def front_kernel(
     vis_hbm, assign_hbm, cat_hbm, st_hbm, order_hbm, flag_hbm, cal_hbm, *refs
 ):
-    send_ref, place_ref, far_hbm, vis, own, cat, st, order, flag, cal, sem, wide, out_sem = refs
+    send_hbm, place_ref, ahead_hbm, behind_hbm, vis, own, cat, st, order, flag, cal, sem, wide, send, out_sem = refs
     c = lax.axis_index("chan")
     k = lax.axis_index("stn")
     copies = [
@@ -55,31 +55,21 @@
                 (flag_hbm, flag),
                 (assign_hbm.at[pl.ds(pl.multiple_of(c * 8, 8), 8)], own),
                 (cat_hbm, cat),
-                (vis_hbm.at[:, lax.rem(k + 2, 4)], vis),
+                (vis_hbm.at[:, lax.rem(k + 1, 4)], vis.at[0]),
                 (cal_hbm, cal),
+                (vis_hbm.at[:, lax.rem(k + 3, 4)], vis.at[1]),
             )
         )
     ]
-    for copy in copies:
-        copy.start()
+    for i in (5, 7, 3, 4, 0, 1, 2, 6):
+        copies[i].start()
     n = order.shape[1]
-    for copy in copies[:3] + copies[6:]:
-        copy.wait()
-    hot = (lax.broadcasted_iota(jnp.int32, (n, n), 0) == order[...]).astype(F32).astype(BF16)
-    high, middle, low = split3(st[...])
-    rows = jnp.concatenate([high, middle, low, flag[...].astype(F32), jnp.zeros((9, n), F32)], axis=0)
-    placed = jnp.dot(rows.astype(BF16), hot, preferred_element_type=F32)
-    middle_nu = 1.0 + (4.0 * c.astype(F32) + 1.5) * (1.0 / 512.0)
-    place_ref[...] = jnp.zeros_like(place_ref)
-    place_ref[0:1] = placed[6:7]
-    for ch in range(4):
-        place_ref[4 + ch : 5 + ch] = jnp.broadcast_to(cal[:, ch : ch + 1], (1, n))
-    place_ref[1:2] = (placed[0:1] + placed[2:3] + placed[4:5]) * middle_nu
-    place_ref[2:3] = (placed[1:2] + placed[3:4] + placed[5:6]) * middle_nu
-    copies[5].wait()
-    wide[...] = vis[...].astype(F32)
-    out = pltpu.make_async_copy(wide, far_hbm, out_sem)
-    out.start()
+    outs = []
+    for i, tile_hbm in enumerate((ahead_hbm, behind_hbm)):
+        copies[5 + 2 * i].wait()
+        wide[i] = vis[i].astype(F32)
+        outs.append(pltpu.make_async_copy(wide.at[i], tile_hbm, out_sem.at[i]))
+        outs[-1].start()
     for copy in copies[3:5]:
         copy.wait()
     blocks = lax.broadcasted_iota(jnp.int32, (64, 128), 0)
@@ -107,8 +97,25 @@
     sent = lax.dot_general(
         jnp.concatenate(left, axis=1), jnp.concatenate(right, axis=1), NT, preferred_element_type=F32
     )
-    send_ref[:, 0, :] = sent
-    out.wait()
+    send[:, 0, :] = sent
+    sending = pltpu.make_async_copy(send, send_hbm, out_sem.at[2])
+    sending.start()
+    for copy in copies[:3] + copies[6:7]:
+        copy.wait()
+    hot = (lax.broadcasted_iota(jnp.int32, (n, n), 0) == order[...]).astype(F32).astype(BF16)
+    high, middle, low = split3(st[...])
+    rows = jnp.concatenate([high, middle, low, flag[...].astype(F32), jnp.zeros((9, n), F32)], axis=0)
+    placed = jnp.dot(rows.astype(BF16), hot, preferred_element_type=F32)
+    middle_nu = 1.0 + (4.0 * c.astype(F32) + 1.5) * (1.0 / 512.0)
+    place_ref[...] = jnp.zeros_like(place_ref)
+    place_ref[0:1] = placed[6:7]
+    for ch in range(4):
+        place_ref[4 + ch : 5 + ch] = jnp.broadcast_to(cal[:, ch : ch + 1], (1, n))
+    place_ref[1:2] = (placed[0:1] + placed[2:3] + placed[4:5]) * middle_nu
+    place_ref[2:3] = (placed[1:2] + placed[3:4] + placed[5:6]) * middle_nu
+    for out in outs:
+        out.wait()
+    sending.wait()
 
 
 def phasor_kernel(
@@ -423,22 +430,23 @@
     def ring(s):
         return [(i, (i + s) % 4) for i in range(4)]
 
-    send, place, far = pl.pallas_call(
+    send, place, ahead, behind = pl.pallas_call(
         front_kernel,
-        out_shape=[shape(64, 1, 5 * CAP), shape(8, n), shape(2, rows, n)],
+        out_shape=[shape(64, 1, 5 * CAP), shape(8, n)] + [shape(2, rows, n)] * 2,
         in_specs=[hbm] * 7,
-        out_specs=[whole] * 2 + [hbm],
+        out_specs=[hbm, whole, hbm, hbm],
         scratch_shapes=[
-            VMEM((2, rows, n), BF16),
+            VMEM((2, 2, rows, n), BF16),
             VMEM((8, 128), jnp.int32),
             VMEM(catalog.shape, F32),
             VMEM(stations.shape, F32),
             VMEM((1, n), jnp.int32),
             VMEM((1, n), jnp.int32),
             VMEM((1, 4), F32),
-            pltpu.SemaphoreType.DMA((7,)),
-            VMEM((2, rows, n), F32),
-            pltpu.SemaphoreType.DMA,
+            pltpu.SemaphoreType.DMA((8,)),
+            VMEM((2, 2, rows, n), F32),
+            VMEM((64, 1, 5 * CAP), F32),
+            pltpu.SemaphoreType.DMA((3,)),
         ],
         name="front",
     )(
@@ -451,11 +459,11 @@
         calibrator.reshape(1, 4),
     )
 
-    ahead, behind, own, place = pl.pallas_call(
+    far, own, place = pl.pallas_call(
         spread_kernel,
-        out_shape=[shape(2, rows, n)] * 3 + [shape(8, n)],
+        out_shape=[shape(2, rows, n)] * 2 + [shape(8, n)],
         in_specs=[whole] * 2,
-        out_specs=[whole] * 4,
+        out_specs=[whole] * 3,
         compiler_params=small,
         cost_estimate=pl.CostEstimate(flops=1 << 20, bytes_accessed=2 << 20, transcendentals=0),
         name="spread",

time: 56.1 us -> 56.8 us (1.012)
  the two profiles are of different devices: /device:TPU:1 before, /device:TPU:8 now
where the time goes in v5:
time: 56.8 us; the launch traced here: 56.6 us
  Pallas kernels  23.4 us (41%)
  starting transfers between devices  20.5 us (36%)
  waiting for transfers between devices  10.1 us (18%)
  local copies, waits for them, and re-layouts  1.94 us (3%)
  between operations  0.69 us (1%)
    all_to_all x1, starting transfers between devices, per_device(): received = lax.all_to_all(send, 'chan', 0, 0)  12.1 us
    pallas_call x1, Pallas kernels, per_device(): pl.pallas_call(phasor_kernel, out_shape=[shape(chunks // 2, 4, n, 512, dt...  11.4 us
    ppermute x3, waiting for transfers between devices, turn(): return lax.ppermute(tile, 'stn', ring(s))  7.3 us
    ppermute x3, starting transfers between devices, turn(): return lax.ppermute(tile, 'stn', ring(s))  5.21 us
    pallas_call x1, Pallas kernels, per_device(): pl.pallas_call(model_kernel, out_shape=shape(4, 2 * rows, n), in_specs=[w...  3.86 us
    ppermute x3, starting transfers between devices, per_device(): lax.ppermute(solved, 'stn', ring(s))  3.22 us
    pallas_call x1, Pallas kernels, per_device(): pl.pallas_call(front_kernel, out_shape=[shape(64, 1, 5 * CAP), shape(8, n...  3.17 us
    pallas_call x1, Pallas kernels, per_device(): pl.pallas_call(solve_kernel, out_shape=shape(8, n), in_specs=[whole] * 6,...  2.55 us
  transfers between devices with their start and end apart: 7, of which 5 were waited for; matrix products, arithmetic and copies ran while one was open for 0% of the time, Pallas kernels for 27%

profile of v5, /device:TPU:8, one launch (start us, length us, event | category | flops | bytes accessed | tf_op | source)
XLA Modules:
  0.0 56.6 jit_solution(5697857272888690081)
XLA Ops:
  0.6 3.2 %front.1 = (f32[64,1,160]{2,1,0:T(1,128)}, f32[8,512]{1,0:T(8,128)}, f32[2,128,512]{2,1,0:T(8,128)}, f32[2,128,512]{2,1,0:T(8,128)}) custom-call(bf16[2,4,128,512]{3,2,1,0:T(8,128)(2,1)} %vis_ref.3, s32[512,128]{1,0:T(8,128)} %bitcast.4, f32[5,1024]{1,0:T(8,128)} %cat_hbm.1, f32[2,512]{1,0:T(2,128)} %st_hbm.1, s32[1,512]{1,0:T(1,128)} %bitcast.5, ...), custom_call_target="tpu_custom_call" | custom-call | tf_op jit(solution)/shard_map/front/pallas_call | solution.py:433
  3.8 12.1 %all-to-all-start = ((f32[64,1,160]{2,1,0:T(1,128)}), f32[64,1,160]{2,1,0:T(1,128)S(1)}, u32[]{:S(2)}, u32[]{:S(2)}) async-start(f32[64,1,160]{2,1,0:T(1,128)} %get-tuple-element.14), calls=%async_computation | async-start | bytes 131072 | tf_op jit(solution)/shard_map/all_to_all | solution.py:475
  15.9 1.6 %collective-permute-start = (f32[2,128,512]{2,1,0:T(8,128)}, f32[2,128,512]{2,1,0:T(8,128)S(1)}, u32[]{:S(2)}, u32[]{:S(2)}) collective-permute-start(f32[2,128,512]{2,1,0:T(8,128)} %get-tuple-element.22), channel_id=1, source_target_pairs={{0,1},{1,2},{2,3},{3,0},{4,5},{5,6},{6,7},{7,4},{8,9},{9,10},{10,1... | collective-permute-start | bytes 1572872 | tf_op jit(solution)/shard_map/ppermute | solution.py:473
  17.5 1.7 %collective-permute-start.2 = (f32[2,128,512]{2,1,0:T(8,128)}, f32[2,128,512]{2,1,0:T(8,128)S(1)}, u32[]{:S(2)}, u32[]{:S(2)}) collective-permute-start(f32[2,128,512]{2,1,0:T(8,128)} %get-tuple-element.24), channel_id=1, source_target_pairs={{0,3},{1,0},{2,1},{3,2},{4,7},{5,4},{6,5},{7,6},{8,11},{9,8},{10,9... | collective-permute-start | bytes 1572872 | tf_op jit(solution)/shard_map/ppermute | solution.py:473
  19.2 0.0 copy-start
  19.2 1.2 %copy-done = bf16[2,4,128,512]{3,2,1,0:T(8,128)(2,1)S(1)} copy-done((bf16[2,4,128,512]{3,2,1,0:T(8,128)(2,1)S(1)}, bf16[2,4,128,512]{3,2,1,0:T(8,128)(2,1)}, u32[]{:S(2)}) %copy-start) | copy-done | bytes 1048600
  20.5 0.0 copy-start.2
  20.5 0.7 %copy-done.2 = f32[8,512]{1,0:T(8,128)S(1)} copy-done((f32[8,512]{1,0:T(8,128)S(1)}, f32[8,512]{1,0:T(8,128)}, u32[]{:S(2)}) %copy-start.2) | copy-done | bytes 16408
  21.2 0.1 spread.1
  21.3 1.9 %collective-permute-start.1 = (f32[2,128,512]{2,1,0:T(8,128)S(1)}, f32[2,128,512]{2,1,0:T(8,128)S(1)}, u32[]{:S(2)}, u32[]{:S(2)}) collective-permute-start(f32[2,128,512]{2,1,0:T(8,128)S(1)} %get-tuple-element.23), channel_id=1, source_target_pairs={{0,2},{1,3},{2,0},{3,1},{4,6},{5,7},{6,4},{7,5},{8,10},{9,11},{10,... | collective-permute-start | bytes 1572872 | tf_op jit(solution)/shard_map/ppermute | solution.py:473
  23.2 1.7 %all-to-all-done.recv_ref = f32[64,1,160]{2,1,0:T(1,128)S(1)} async-done(((f32[64,1,160]{2,1,0:T(1,128)}), f32[64,1,160]{2,1,0:T(1,128)S(1)}, u32[]{:S(2)}, u32[]{:S(2)}) %all-to-all-start) | async-done | bytes 40992 | tf_op jit(solution)/shard_map/all_to_all | solution.py:475
  24.9 11.4 %phasor.1 = (bf16[4,4,512,512]{3,2,1,0:T(8,128)(2,1)S(1)}, bf16[4,4,512,512]{3,2,1,0:T(8,128)(2,1)S(1)}, bf16[8,4,128,512]{3,2,1,0:T(8,128)(2,1)S(1)}, f32[1024,512]{1,0:T(8,128)S(1)}) custom-call(f32[64,1,160]{2,1,0:T(1,128)S(1)} %all-to-all-done.recv_ref, f32[8,512]{1,0:T(8,128)S(1)} %get-tuple-element.16.place_ref.ok_ref), custom_call_target="tpu_custom_call" | custom-call | flops 10737418240 | bytes 22020096 | tf_op jit(solution)/shard_map/phasor/pallas_call | solution.py:478
  36.3 0.0 collective-permute-done.v1
  36.3 5.7 %collective-permute-done.2.v3 = f32[2,128,512]{2,1,0:T(8,128)S(1)} collective-permute-done((f32[2,128,512]{2,1,0:T(8,128)}, f32[2,128,512]{2,1,0:T(8,128)S(1)}, u32[]{:S(2)}, u32[]{:S(2)}) %collective-permute-start.2) | collective-permute-done | bytes 524320 | tf_op jit(solution)/shard_map/ppermute | solution.py:473
  42.0 1.6 %collective-permute-done.1.v2 = f32[2,128,512]{2,1,0:T(8,128)S(1)} collective-permute-done((f32[2,128,512]{2,1,0:T(8,128)S(1)}, f32[2,128,512]{2,1,0:T(8,128)S(1)}, u32[]{:S(2)}, u32[]{:S(2)}) %collective-permute-start.1) | collective-permute-done | bytes 524320 | tf_op jit(solution)/shard_map/ppermute | solution.py:473
  43.6 2.6 %solve.1.g0 = f32[8,512]{1,0:T(8,128)S(1)} custom-call(f32[1024,512]{1,0:T(8,128)S(1)} %get-tuple-element.20.own_ref.model_ref, f32[2,128,512]{2,1,0:T(8,128)S(1)} %get-tuple-element.21.v0, f32[2,128,512]{2,1,0:T(8,128)S(1)} %collective-permute-done.v1, f32[2,128,512]{2,1,0:T(8,128)S(1)} %collective-permute-done.1.v2, ...), custom_call_target="tpu_custom_call" | custom-call | tf_op jit(solution)/shard_map/solve/pallas_call | solution.py:501
  46.1 2.0 %collective-permute-start.5 = (f32[8,512]{1,0:T(8,128)S(1)}, f32[8,512]{1,0:T(8,128)S(1)}, u32[]{:S(2)}, u32[]{:S(2)}) collective-permute-start(f32[8,512]{1,0:T(8,128)S(1)} %solve.1.g0), channel_id=1, source_target_pairs={{0,3},{1,0},{2,1},{3,2},{4,7},{5,4},{6,5},{7,6},{8,11},{9,8},{10,9... | collective-permute-start | bytes 49160 | tf_op jit(solution)/shard_map/ppermute | solution.py:510
  48.1 1.2 %collective-permute-start.4 = (f32[8,512]{1,0:T(8,128)S(1)}, f32[8,512]{1,0:T(8,128)S(1)}, u32[]{:S(2)}, u32[]{:S(2)}) collective-permute-start(f32[8,512]{1,0:T(8,128)S(1)} %solve.1.g0), channel_id=1, source_target_pairs={{0,2},{1,3},{2,0},{3,1},{4,6},{5,7},{6,4},{7,5},{8,10},{9,11},{10,... | collective-permute-start | bytes 49160 | tf_op jit(solution)/shard_map/ppermute | solution.py:510
  49.4 0.0 collective-permute-start.3
  49.4 0.0 copy-start.1
  49.4 3.9 %model.1.model_ref = f32[4,256,512]{2,1,0:T(8,128)S(1)} custom-call(bf16[4,4,512,512]{3,2,1,0:T(8,128)(2,1)S(1)} %get-tuple-element.17.right_even, bf16[4,4,512,512]{3,2,1,0:T(8,128)(2,1)S(1)} %get-tuple-element.18.right_odd, bf16[8,4,128,512]{3,2,1,0:T(8,128)(2,1)S(1)} %get-tuple-element.19.left_ref, f32[1024,512]{1,0:T(8,128)S(1)} %get-tuple-element.20.own_ref.model_ref, ...), custom_call_target="tpu_custom_call" | custom-call | flops 4294967296 | bytes 22020096 | tf_op jit(solution)/shard_map/model/pallas_call | solution.py:512
  53.2 0.0 collective-permute-done.5.g3
  53.2 0.1 collective-permute-done.4.g2
  53.4 0.9 %collective-permute-done.3.g1 = f32[8,512]{1,0:T(8,128)S(1)} collective-permute-done((f32[8,512]{1,0:T(8,128)S(1)}, f32[8,512]{1,0:T(8,128)S(1)}, u32[]{:S(2)}, u32[]{:S(2)}) %collective-permute-start.3) | collective-permute-done | bytes 16416 | tf_op jit(solution)/shard_map/ppermute | solution.py:510
  54.3 0.0 copy-done.1
  54.3 2.3 %residual.1 = (f32[2,4,128]{2,1,0:T(4,128)}, bf16[2,4,128,512]{3,2,1,0:T(8,128)(2,1)}, f32[3,4]{1,0:T(4,128)}) custom-call(f32[4,256,512]{2,1,0:T(8,128)S(1)} %model.1.model_ref, bf16[2,4,128,512]{3,2,1,0:T(8,128)(2,1)S(1)} %copy-done.1, f32[8,512]{1,0:T(8,128)S(1)} %solve.1.g0, f32[8,512]{1,0:T(8,128)S(1)} %collective-permute-done.3.g1, ...), custom_call_target="tpu_custom_call" | custom-call | tf_op jit(solution)/shard_map/residual/pallas_call | solution.py:523
Async XLA Ops:
  3.8 21.0 %all-to-all-start = ((f32[64,1,160]{2,1,0:T(1,128)}), f32[64,1,160]{2,1,0:T(1,128)S(1)}, u32[]{:S(2)}, u32[]{:S(2)}) async-start(f32[64,1,160]{2,1,0:T(1,128)} %get-tuple-element.14), calls=%async_computation | async-start | bytes 131072 | tf_op jit(solution)/shard_map/all_to_all | solution.py:475
  15.9 20.4 %collective-permute-start = (f32[2,128,512]{2,1,0:T(8,128)}, f32[2,128,512]{2,1,0:T(8,128)S(1)}, u32[]{:S(2)}, u32[]{:S(2)}) collective-permute-start(f32[2,128,512]{2,1,0:T(8,128)} %get-tuple-element.22), channel_id=1, source_target_pairs={{0,1},{1,2},{2,3},{3,0},{4,5},{5,6},{6,7},{7,4},{8,9},{9,10},{10,1... | collective-permute-start | bytes 1572872 | tf_op jit(solution)/shard_map/ppermute | solution.py:473
  17.5 24.5 %collective-permute-start.2 = (f32[2,128,512]{2,1,0:T(8,128)}, f32[2,128,512]{2,1,0:T(8,128)S(1)}, u32[]{:S(2)}, u32[]{:S(2)}) collective-permute-start(f32[2,128,512]{2,1,0:T(8,128)} %get-tuple-element.24), channel_id=1, source_target_pairs={{0,3},{1,0},{2,1},{3,2},{4,7},{5,4},{6,5},{7,6},{8,11},{9,8},{10,9... | collective-permute-start | bytes 1572872 | tf_op jit(solution)/shard_map/ppermute | solution.py:473
  19.2 1.2 %copy-start = (bf16[2,4,128,512]{3,2,1,0:T(8,128)(2,1)S(1)}, bf16[2,4,128,512]{3,2,1,0:T(8,128)(2,1)}, u32[]{:S(2)}) copy-start(bf16[2,4,128,512]{3,2,1,0:T(8,128)(2,1)} %vis_ref.3) | copy-start | bytes 3145732
  20.5 0.7 %copy-start.2 = (f32[8,512]{1,0:T(8,128)S(1)}, f32[8,512]{1,0:T(8,128)}, u32[]{:S(2)}) copy-start(f32[8,512]{1,0:T(8,128)} %get-tuple-element.15.place_ref) | copy-start | bytes 49156
  21.3 22.3 %collective-permute-start.1 = (f32[2,128,512]{2,1,0:T(8,128)S(1)}, f32[2,128,512]{2,1,0:T(8,128)S(1)}, u32[]{:S(2)}, u32[]{:S(2)}) collective-permute-start(f32[2,128,512]{2,1,0:T(8,128)S(1)} %get-tuple-element.23), channel_id=1, source_target_pairs={{0,2},{1,3},{2,0},{3,1},{4,6},{5,7},{6,4},{7,5},{8,10},{9,11},{10,... | collective-permute-start | bytes 1572872 | tf_op jit(solution)/shard_map/ppermute | solution.py:473
  46.1 7.1 %collective-permute-start.5 = (f32[8,512]{1,0:T(8,128)S(1)}, f32[8,512]{1,0:T(8,128)S(1)}, u32[]{:S(2)}, u32[]{:S(2)}) collective-permute-start(f32[8,512]{1,0:T(8,128)S(1)} %solve.1.g0), channel_id=1, source_target_pairs={{0,3},{1,0},{2,1},{3,2},{4,7},{5,4},{6,5},{7,6},{8,11},{9,8},{10,9... | collective-permute-start | bytes 49160 | tf_op jit(solution)/shard_map/ppermute | solution.py:510
  48.1 5.2 %collective-permute-start.4 = (f32[8,512]{1,0:T(8,128)S(1)}, f32[8,512]{1,0:T(8,128)S(1)}, u32[]{:S(2)}, u32[]{:S(2)}) collective-permute-start(f32[8,512]{1,0:T(8,128)S(1)} %solve.1.g0), channel_id=1, source_target_pairs={{0,2},{1,3},{2,0},{3,1},{4,6},{5,7},{6,4},{7,5},{8,10},{9,11},{10,... | collective-permute-start | bytes 49160 | tf_op jit(solution)/shard_map/ppermute | solution.py:510
  49.4 4.9 %collective-permute-start.3 = (f32[8,512]{1,0:T(8,128)S(1)}, f32[8,512]{1,0:T(8,128)S(1)}, u32[]{:S(2)}, u32[]{:S(2)}) collective-permute-start(f32[8,512]{1,0:T(8,128)S(1)} %solve.1.g0), channel_id=1, source_target_pairs={{0,1},{1,2},{2,3},{3,0},{4,5},{5,6},{6,7},{7,4},{8,9},{9,10},{10,1... | collective-permute-start | bytes 49160 | tf_op jit(solution)/shard_map/ppermute | solution.py:510
  49.4 4.9 %copy-start.1 = (bf16[2,4,128,512]{3,2,1,0:T(8,128)(2,1)S(1)}, bf16[2,4,128,512]{3,2,1,0:T(8,128)(2,1)}, u32[]{:S(2)}) copy-start(bf16[2,4,128,512]{3,2,1,0:T(8,128)(2,1)} %vis_ref.3) | copy-start | bytes 3145732

commit v6 on v4

--- a/solution.py
+++ b/solution.py
@@ -1,3 +1,5 @@
+import functools
+
 import jax
 import jax.numpy as jnp
 from jax import lax
@@ -43,7 +45,7 @@
 def front_kernel(
     vis_hbm, assign_hbm, cat_hbm, st_hbm, order_hbm, flag_hbm, cal_hbm, *refs
 ):
-    send_ref, place_ref, far_hbm, vis, own, cat, st, order, flag, cal, sem, wide, out_sem = refs
+    send_hbm, place_ref, far_hbm, vis, own, cat, st, order, flag, cal, sem, wide, send, out_sem = refs
     c = lax.axis_index("chan")
     k = lax.axis_index("stn")
     copies = [
@@ -60,25 +62,12 @@
             )
         )
     ]
-    for copy in copies:
-        copy.start()
+    for i in (5, 3, 4, 0, 1, 2, 6):
+        copies[i].start()
     n = order.shape[1]
-    for copy in copies[:3] + copies[6:]:
-        copy.wait()
-    hot = (lax.broadcasted_iota(jnp.int32, (n, n), 0) == order[...]).astype(F32).astype(BF16)
-    high, middle, low = split3(st[...])
-    rows = jnp.concatenate([high, middle, low, flag[...].astype(F32), jnp.zeros((9, n), F32)], axis=0)
-    placed = jnp.dot(rows.astype(BF16), hot, preferred_element_type=F32)
-    middle_nu = 1.0 + (4.0 * c.astype(F32) + 1.5) * (1.0 / 512.0)
-    place_ref[...] = jnp.zeros_like(place_ref)
-    place_ref[0:1] = placed[6:7]
-    for ch in range(4):
-        place_ref[4 + ch : 5 + ch] = jnp.broadcast_to(cal[:, ch : ch + 1], (1, n))
-    place_ref[1:2] = (placed[0:1] + placed[2:3] + placed[4:5]) * middle_nu
-    place_ref[2:3] = (placed[1:2] + placed[3:4] + placed[5:6]) * middle_nu
     copies[5].wait()
     wide[...] = vis[...].astype(F32)
-    out = pltpu.make_async_copy(wide, far_hbm, out_sem)
+    out = pltpu.make_async_copy(wide, far_hbm, out_sem.at[0])
     out.start()
     for copy in copies[3:5]:
         copy.wait()
@@ -107,8 +96,24 @@
     sent = lax.dot_general(
         jnp.concatenate(left, axis=1), jnp.concatenate(right, axis=1), NT, preferred_element_type=F32
     )
-    send_ref[:, 0, :] = sent
+    send[:, 0, :] = sent
+    sending = pltpu.make_async_copy(send, send_hbm, out_sem.at[1])
+    sending.start()
+    for copy in copies[:3] + copies[6:]:
+        copy.wait()
+    hot = (lax.broadcasted_iota(jnp.int32, (n, n), 0) == order[...]).astype(F32).astype(BF16)
+    high, middle, low = split3(st[...])
+    rows = jnp.concatenate([high, middle, low, flag[...].astype(F32), jnp.zeros((9, n), F32)], axis=0)
+    placed = jnp.dot(rows.astype(BF16), hot, preferred_element_type=F32)
+    middle_nu = 1.0 + (4.0 * c.astype(F32) + 1.5) * (1.0 / 512.0)
+    place_ref[...] = jnp.zeros_like(place_ref)
+    place_ref[0:1] = placed[6:7]
+    for ch in range(4):
+        place_ref[4 + ch : 5 + ch] = jnp.broadcast_to(cal[:, ch : ch + 1], (1, n))
+    place_ref[1:2] = (placed[0:1] + placed[2:3] + placed[4:5]) * middle_nu
+    place_ref[2:3] = (placed[1:2] + placed[3:4] + placed[5:6]) * middle_nu
     out.wait()
+    sending.wait()
 
 
 def phasor_kernel(
@@ -153,7 +158,7 @@
             sems.at[buffer],
         )
 
-    def phases(buffer, r0, g):
+    def phases(buffer, r0, g, channel):
         right, left, wide = rights[buffer].at[g], lefts[buffer], wides[buffer]
         rows = slice(r0, r0 + 8)
         x = jnp.concatenate([spots[0, rows]] * tiles, axis=1)
@@ -182,32 +187,33 @@
             bright = wide[2 + ch]
             right[ch, rows, :width] = (bright * cosine).astype(BF16)
             right[ch, rows, width:] = (bright * sine).astype(BF16)
-            left[ch, rows, :width] = cosine.astype(BF16)
-            left[ch, rows, width:] = sine.astype(BF16)
+            if ch == channel or r0 // quarter == channel:
+                left[ch, rows, :width] = cosine.astype(BF16)
+                left[ch, rows, width:] = sine.astype(BF16)
 
     lefts[1][k] = jnp.zeros((n, 2 * width), BF16)
     right_odd[pairs - 1, k] = jnp.zeros((n, 2 * width), BF16)
 
     def chunks(*totals):
-        def matmul(other, turn, block, g):
+        def matmul(other, turn, block, g, own):
             left, right = lefts[other], rights[other].at[g]
             columns = slice(turn * width, turn * width + width)
             if block == 0:
                 for half in range(2):
                     pltpu.matmul_push_rhs(
-                        right[k, half * width : half * width + width, columns], turn, half, transpose=True
+                        right[own, half * width : half * width + width, columns], turn, half, transpose=True
                     )
             rows = slice(128 * (block % 4), 128 * (block % 4) + 128)
             if block < 4:
-                lhs = left[k, rows, columns]
+                lhs = left[own, rows, columns]
             else:
-                lhs = left[k, rows, (1 - turn) * width : (2 - turn) * width]
+                lhs = left[own, rows, (1 - turn) * width : (2 - turn) * width]
                 if turn == 1:
                     lhs = -lhs
             for half in range(2):
                 pltpu.matmul_acc_lhs(totals[8 * half + block], lhs, turn if block == 0 else None)
 
-        def pair(g, _):
+        def pair(channel, g, _):
             for sub in range(2):
                 chunk = 2 * g + sub
 
@@ -223,18 +229,23 @@
                     for block in range(8):
 
                         def body(sub=sub, turn=turn, block=block):
-                            matmul(1 - sub, turn, block, g if sub else lax.rem(g + pairs - 1, pairs))
+                            matmul(1 - sub, turn, block, g if sub else lax.rem(g + pairs - 1, pairs), channel)
                             for i in range(4):
-                                phases(sub, 32 * (8 * turn + block) + 8 * i, g)
+                                phases(sub, 32 * (8 * turn + block) + 8 * i, g, channel)
 
                         pl.when(g >= 0)(body)
                 out_copy(chunk, sub).start()
             return 0
 
-        lax.fori_loop(0, pairs, pair, 0)
+        for channel in range(4):
+
+            @pl.when(k == channel)
+            def _():
+                lax.fori_loop(0, pairs, functools.partial(pair, channel), 0)
+
         for turn in range(2):
             for block in range(8):
-                matmul(1, turn, block, pairs - 1)
+                matmul(1, turn, block, pairs - 1, k)
         for sub in range(2):
             out_copy(2 * pairs - 2 + sub, sub).wait()
         bright_rows[0:4] = place_ref[4:8, :128]
@@ -427,7 +438,7 @@
         front_kernel,
         out_shape=[shape(64, 1, 5 * CAP), shape(8, n), shape(2, rows, n)],
         in_specs=[hbm] * 7,
-        out_specs=[whole] * 2 + [hbm],
+        out_specs=[hbm, whole, hbm],
         scratch_shapes=[
             VMEM((2, rows, n), BF16),
             VMEM((8, 128), jnp.int32),
@@ -438,7 +449,8 @@
             VMEM((1, 4), F32),
             pltpu.SemaphoreType.DMA((7,)),
             VMEM((2, rows, n), F32),
-            pltpu.SemaphoreType.DMA,
+            VMEM((64, 1, 5 * CAP), F32),
+            pltpu.SemaphoreType.DMA((2,)),
         ],
         name="front",
     )(

time: 56.1 us -> 56.6 us (level)
  transfers between devices with their start and end apart: 7 -> 7, of which waited for: 2 -> 2; matrix products, arithmetic and copies ran while one was open for 0% -> 0% of each run, Pallas kernels for 28% -> 27%
where the time goes in v6:
time: 56.6 us; the launch traced here: 56.2 us
  Pallas kernels  23.1 us (41%)
  starting transfers between devices  22.4 us (40%)
  waiting for transfers between devices  8.07 us (14%)
  local copies, waits for them, and re-layouts  1.94 us (3%)
  between operations  0.71 us (1%)
    all_to_all x1, starting transfers between devices, per_device(): received = lax.all_to_all(send, 'chan', 0, 0)  13.2 us
    pallas_call x1, Pallas kernels, per_device(): pl.pallas_call(phasor_kernel, out_shape=[shape(chunks // 2, 4, n, 512, dt...  11.2 us
    ppermute x3, waiting for transfers between devices, turn(): return lax.ppermute(tile, 'stn', ring(s))  5.61 us
    ppermute x3, starting transfers between devices, turn(): return lax.ppermute(tile, 'stn', ring(s))  5.58 us
    pallas_call x1, Pallas kernels, per_device(): pl.pallas_call(model_kernel, out_shape=shape(4, 2 * rows, n), in_specs=[w...  3.86 us
    ppermute x3, starting transfers between devices, per_device(): lax.ppermute(solved, 'stn', ring(s))  3.62 us
    pallas_call x1, Pallas kernels, per_device(): pl.pallas_call(front_kernel, out_shape=[shape(64, 1, 5 * CAP), shape(8, n...  3.08 us
    pallas_call x1, Pallas kernels, per_device(): pl.pallas_call(solve_kernel, out_shape=shape(8, n), in_specs=[whole] * 6,...  2.56 us
  transfers between devices with their start and end apart: 7, of which 2 were waited for; matrix products, arithmetic and copies ran while one was open for 0% of the time, Pallas kernels for 27%

profile of v6, /device:TPU:1, one launch (start us, length us, event | category | flops | bytes accessed | tf_op | source)
XLA Modules:
  0.0 56.2 jit_solution(6567095789250303384)
XLA Ops:
  0.6 3.1 %front.1 = (f32[64,1,160]{2,1,0:T(1,128)}, f32[8,512]{1,0:T(8,128)}, f32[2,128,512]{2,1,0:T(8,128)}) custom-call(bf16[2,4,128,512]{3,2,1,0:T(8,128)(2,1)} %vis_ref.3, s32[512,128]{1,0:T(8,128)} %bitcast.4, f32[5,1024]{1,0:T(8,128)} %cat_hbm.1, f32[2,512]{1,0:T(2,128)} %st_hbm.1, s32[1,512]{1,0:T(1,128)} %bitcast.5, s32[1,512]{1,0:T(1,128)} %bitcast.6, ...), custom_call_target="tpu_custom_call" | custom-call | tf_op jit(solution)/shard_map/front/pallas_call | solution.py:437
  3.7 13.2 %all-to-all-start = ((f32[64,1,160]{2,1,0:T(1,128)}), f32[64,1,160]{2,1,0:T(1,128)S(1)}, u32[]{:S(2)}, u32[]{:S(2)}) async-start(f32[64,1,160]{2,1,0:T(1,128)} %get-tuple-element.14), calls=%async_computation | async-start | bytes 131072 | tf_op jit(solution)/shard_map/all_to_all | solution.py:479
  16.9 2.8 %collective-permute-start.1 = (f32[2,128,512]{2,1,0:T(8,128)}, f32[2,128,512]{2,1,0:T(8,128)S(1)}, u32[]{:S(2)}, u32[]{:S(2)}) collective-permute-start(f32[2,128,512]{2,1,0:T(8,128)} %get-tuple-element.23), channel_id=1, source_target_pairs={{0,2},{1,3},{2,0},{3,1},{4,6},{5,7},{6,4},{7,5},{8,10},{9,11},{10,... | collective-permute-start | bytes 1572872 | tf_op jit(solution)/shard_map/ppermute | solution.py:477
  19.7 0.0 copy-start
  19.7 1.2 %copy-done = bf16[2,4,128,512]{3,2,1,0:T(8,128)(2,1)S(1)} copy-done((bf16[2,4,128,512]{3,2,1,0:T(8,128)(2,1)S(1)}, bf16[2,4,128,512]{3,2,1,0:T(8,128)(2,1)}, u32[]{:S(2)}) %copy-start) | copy-done | bytes 1048600
  20.9 0.0 copy-start.2
  20.9 0.7 %copy-done.2 = f32[8,512]{1,0:T(8,128)S(1)} copy-done((f32[8,512]{1,0:T(8,128)S(1)}, f32[8,512]{1,0:T(8,128)}, u32[]{:S(2)}) %copy-start.2) | copy-done | bytes 16408
  21.7 0.1 spread.1
  21.8 0.4 collective-permute-start
  22.2 2.4 %collective-permute-start.2 = (f32[2,128,512]{2,1,0:T(8,128)S(1)}, f32[2,128,512]{2,1,0:T(8,128)S(1)}, u32[]{:S(2)}, u32[]{:S(2)}) collective-permute-start(f32[2,128,512]{2,1,0:T(8,128)S(1)} %get-tuple-element.24), channel_id=1, source_target_pairs={{0,3},{1,0},{2,1},{3,2},{4,7},{5,4},{6,5},{7,6},{8,11},{9,8},{10,9... | collective-permute-start | bytes 1572872 | tf_op jit(solution)/shard_map/ppermute | solution.py:477
  24.5 2.5 %all-to-all-done.recv_ref = f32[64,1,160]{2,1,0:T(1,128)S(1)} async-done(((f32[64,1,160]{2,1,0:T(1,128)}), f32[64,1,160]{2,1,0:T(1,128)S(1)}, u32[]{:S(2)}, u32[]{:S(2)}) %all-to-all-start) | async-done | bytes 40992 | tf_op jit(solution)/shard_map/all_to_all | solution.py:479
  27.0 11.2 %phasor.1 = (bf16[4,4,512,512]{3,2,1,0:T(8,128)(2,1)S(1)}, bf16[4,4,512,512]{3,2,1,0:T(8,128)(2,1)S(1)}, bf16[8,4,128,512]{3,2,1,0:T(8,128)(2,1)S(1)}, f32[1024,512]{1,0:T(8,128)S(1)}) custom-call(f32[64,1,160]{2,1,0:T(1,128)S(1)} %all-to-all-done.recv_ref, f32[8,512]{1,0:T(8,128)S(1)} %get-tuple-element.16.place_ref.ok_ref), custom_call_target="tpu_custom_call" | custom-call | flops 10737418240 | bytes 22020096 | tf_op jit(solution)/shard_map/phasor/pallas_call | solution.py:482
  38.2 0.0 collective-permute-done.1.v2
  38.2 5.6 %collective-permute-done.v1 = f32[2,128,512]{2,1,0:T(8,128)S(1)} collective-permute-done((f32[2,128,512]{2,1,0:T(8,128)S(1)}, f32[2,128,512]{2,1,0:T(8,128)S(1)}, u32[]{:S(2)}, u32[]{:S(2)}) %collective-permute-start) | collective-permute-done | bytes 524320 | tf_op jit(solution)/shard_map/ppermute | solution.py:477
  43.8 0.0 collective-permute-done.2.v3
  43.8 2.6 %solve.1.g0 = f32[8,512]{1,0:T(8,128)S(1)} custom-call(f32[1024,512]{1,0:T(8,128)S(1)} %get-tuple-element.20.own_ref.model_ref, f32[2,128,512]{2,1,0:T(8,128)S(1)} %get-tuple-element.21.v0, f32[2,128,512]{2,1,0:T(8,128)S(1)} %collective-permute-done.v1, f32[2,128,512]{2,1,0:T(8,128)S(1)} %collective-permute-done.1.v2, ...), custom_call_target="tpu_custom_call" | custom-call | tf_op jit(solution)/shard_map/solve/pallas_call | solution.py:505
  46.3 2.5 %collective-permute-start.5 = (f32[8,512]{1,0:T(8,128)S(1)}, f32[8,512]{1,0:T(8,128)S(1)}, u32[]{:S(2)}, u32[]{:S(2)}) collective-permute-start(f32[8,512]{1,0:T(8,128)S(1)} %solve.1.g0), channel_id=1, source_target_pairs={{0,3},{1,0},{2,1},{3,2},{4,7},{5,4},{6,5},{7,6},{8,11},{9,8},{10,9... | collective-permute-start | bytes 49160 | tf_op jit(solution)/shard_map/ppermute | solution.py:514
  48.8 0.5 collective-permute-start.4
  49.3 0.6 %collective-permute-start.3 = (f32[8,512]{1,0:T(8,128)S(1)}, f32[8,512]{1,0:T(8,128)S(1)}, u32[]{:S(2)}, u32[]{:S(2)}) collective-permute-start(f32[8,512]{1,0:T(8,128)S(1)} %solve.1.g0), channel_id=1, source_target_pairs={{0,1},{1,2},{2,3},{3,0},{4,5},{5,6},{6,7},{7,4},{8,9},{9,10},{10,1... | collective-permute-start | bytes 49160 | tf_op jit(solution)/shard_map/ppermute | solution.py:514
  50.0 0.0 copy-start.1
  50.0 3.9 %model.1.model_ref = f32[4,256,512]{2,1,0:T(8,128)S(1)} custom-call(bf16[4,4,512,512]{3,2,1,0:T(8,128)(2,1)S(1)} %get-tuple-element.17.right_even, bf16[4,4,512,512]{3,2,1,0:T(8,128)(2,1)S(1)} %get-tuple-element.18.right_odd, bf16[8,4,128,512]{3,2,1,0:T(8,128)(2,1)S(1)} %get-tuple-element.19.left_ref, f32[1024,512]{1,0:T(8,128)S(1)} %get-tuple-element.20.own_ref.model_ref, ...), custom_call_target="tpu_custom_call" | custom-call | flops 4294967296 | bytes 22020096 | tf_op jit(solution)/shard_map/model/pallas_call | solution.py:516
  53.8 0.0 collective-permute-done.5.g3
  53.8 0.0 collective-permute-done.4.g2
  53.8 0.0 collective-permute-done.3.g1
  53.9 0.0 copy-done.1
  53.9 2.3 %residual.1 = (f32[2,4,128]{2,1,0:T(4,128)}, bf16[2,4,128,512]{3,2,1,0:T(8,128)(2,1)}, f32[3,4]{1,0:T(4,128)}) custom-call(f32[4,256,512]{2,1,0:T(8,128)S(1)} %model.1.model_ref, bf16[2,4,128,512]{3,2,1,0:T(8,128)(2,1)S(1)} %copy-done.1, f32[8,512]{1,0:T(8,128)S(1)} %solve.1.g0, f32[8,512]{1,0:T(8,128)S(1)} %collective-permute-done.3.g1, ...), custom_call_target="tpu_custom_call" | custom-call | tf_op jit(solution)/shard_map/residual/pallas_call | solution.py:527
Async XLA Ops:
  3.7 23.3 %all-to-all-start = ((f32[64,1,160]{2,1,0:T(1,128)}), f32[64,1,160]{2,1,0:T(1,128)S(1)}, u32[]{:S(2)}, u32[]{:S(2)}) async-start(f32[64,1,160]{2,1,0:T(1,128)} %get-tuple-element.14), calls=%async_computation | async-start | bytes 131072 | tf_op jit(solution)/shard_map/all_to_all | solution.py:479
  16.9 21.3 %collective-permute-start.1 = (f32[2,128,512]{2,1,0:T(8,128)}, f32[2,128,512]{2,1,0:T(8,128)S(1)}, u32[]{:S(2)}, u32[]{:S(2)}) collective-permute-start(f32[2,128,512]{2,1,0:T(8,128)} %get-tuple-element.23), channel_id=1, source_target_pairs={{0,2},{1,3},{2,0},{3,1},{4,6},{5,7},{6,4},{7,5},{8,10},{9,11},{10,... | collective-permute-start | bytes 1572872 | tf_op jit(solution)/shard_map/ppermute | solution.py:477
  19.7 1.2 %copy-start = (bf16[2,4,128,512]{3,2,1,0:T(8,128)(2,1)S(1)}, bf16[2,4,128,512]{3,2,1,0:T(8,128)(2,1)}, u32[]{:S(2)}) copy-start(bf16[2,4,128,512]{3,2,1,0:T(8,128)(2,1)} %vis_ref.3) | copy-start | bytes 3145732
  20.9 0.7 %copy-start.2 = (f32[8,512]{1,0:T(8,128)S(1)}, f32[8,512]{1,0:T(8,128)}, u32[]{:S(2)}) copy-start(f32[8,512]{1,0:T(8,128)} %get-tuple-element.15.place_ref) | copy-start | bytes 49156
  21.8 22.0 %collective-permute-start = (f32[2,128,512]{2,1,0:T(8,128)S(1)}, f32[2,128,512]{2,1,0:T(8,128)S(1)}, u32[]{:S(2)}, u32[]{:S(2)}) collective-permute-start(f32[2,128,512]{2,1,0:T(8,128)S(1)} %get-tuple-element.22), channel_id=1, source_target_pairs={{0,1},{1,2},{2,3},{3,0},{4,5},{5,6},{6,7},{7,4},{8,9},{9,10},{10,1... | collective-permute-start | bytes 1572872 | tf_op jit(solution)/shard_map/ppermute | solution.py:477
  22.2 21.6 %collective-permute-start.2 = (f32[2,128,512]{2,1,0:T(8,128)S(1)}, f32[2,128,512]{2,1,0:T(8,128)S(1)}, u32[]{:S(2)}, u32[]{:S(2)}) collective-permute-start(f32[2,128,512]{2,1,0:T(8,128)S(1)} %get-tuple-element.24), channel_id=1, source_target_pairs={{0,3},{1,0},{2,1},{3,2},{4,7},{5,4},{6,5},{7,6},{8,11},{9,8},{10,9... | collective-permute-start | bytes 1572872 | tf_op jit(solution)/shard_map/ppermute | solution.py:477
  46.3 7.5 %collective-permute-start.5 = (f32[8,512]{1,0:T(8,128)S(1)}, f32[8,512]{1,0:T(8,128)S(1)}, u32[]{:S(2)}, u32[]{:S(2)}) collective-permute-start(f32[8,512]{1,0:T(8,128)S(1)} %solve.1.g0), channel_id=1, source_target_pairs={{0,3},{1,0},{2,1},{3,2},{4,7},{5,4},{6,5},{7,6},{8,11},{9,8},{10,9... | collective-permute-start | bytes 49160 | tf_op jit(solution)/shard_map/ppermute | solution.py:514
  48.8 5.0 %collective-permute-start.4 = (f32[8,512]{1,0:T(8,128)S(1)}, f32[8,512]{1,0:T(8,128)S(1)}, u32[]{:S(2)}, u32[]{:S(2)}) collective-permute-start(f32[8,512]{1,0:T(8,128)S(1)} %solve.1.g0), channel_id=1, source_target_pairs={{0,2},{1,3},{2,0},{3,1},{4,6},{5,7},{6,4},{7,5},{8,10},{9,11},{10,... | collective-permute-start | bytes 49160 | tf_op jit(solution)/shard_map/ppermute | solution.py:514
  49.3 4.5 %collective-permute-start.3 = (f32[8,512]{1,0:T(8,128)S(1)}, f32[8,512]{1,0:T(8,128)S(1)}, u32[]{:S(2)}, u32[]{:S(2)}) collective-permute-start(f32[8,512]{1,0:T(8,128)S(1)} %solve.1.g0), channel_id=1, source_target_pairs={{0,1},{1,2},{2,3},{3,0},{4,5},{5,6},{6,7},{7,4},{8,9},{9,10},{10,1... | collective-permute-start | bytes 49160 | tf_op jit(solution)/shard_map/ppermute | solution.py:514
  50.0 3.9 %copy-start.1 = (bf16[2,4,128,512]{3,2,1,0:T(8,128)(2,1)S(1)}, bf16[2,4,128,512]{3,2,1,0:T(8,128)(2,1)}, u32[]{:S(2)}) copy-start(bf16[2,4,128,512]{3,2,1,0:T(8,128)(2,1)} %vis_ref.3) | copy-start | bytes 3145732

commit v7 on v4

--- a/solution.py
+++ b/solution.py
@@ -1,3 +1,5 @@
+import functools
+
 import jax
 import jax.numpy as jnp
 from jax import lax
@@ -153,7 +155,7 @@
             sems.at[buffer],
         )
 
-    def phases(buffer, r0, g):
+    def phases(buffer, r0, g, channel):
         right, left, wide = rights[buffer].at[g], lefts[buffer], wides[buffer]
         rows = slice(r0, r0 + 8)
         x = jnp.concatenate([spots[0, rows]] * tiles, axis=1)
@@ -182,32 +184,33 @@
             bright = wide[2 + ch]
             right[ch, rows, :width] = (bright * cosine).astype(BF16)
             right[ch, rows, width:] = (bright * sine).astype(BF16)
-            left[ch, rows, :width] = cosine.astype(BF16)
-            left[ch, rows, width:] = sine.astype(BF16)
+            if ch == channel or r0 // quarter == channel:
+                left[ch, rows, :width] = cosine.astype(BF16)
+                left[ch, rows, width:] = sine.astype(BF16)
 
     lefts[1][k] = jnp.zeros((n, 2 * width), BF16)
     right_odd[pairs - 1, k] = jnp.zeros((n, 2 * width), BF16)
 
     def chunks(*totals):
-        def matmul(other, turn, block, g):
+        def matmul(other, turn, block, g, own):
             left, right = lefts[other], rights[other].at[g]
             columns = slice(turn * width, turn * width + width)
             if block == 0:
                 for half in range(2):
                     pltpu.matmul_push_rhs(
-                        right[k, half * width : half * width + width, columns], turn, half, transpose=True
+                        right[own, half * width : half * width + width, columns], turn, half, transpose=True
                     )
             rows = slice(128 * (block % 4), 128 * (block % 4) + 128)
             if block < 4:
-                lhs = left[k, rows, columns]
+                lhs = left[own, rows, columns]
             else:
-                lhs = left[k, rows, (1 - turn) * width : (2 - turn) * width]
+                lhs = left[own, rows, (1 - turn) * width : (2 - turn) * width]
                 if turn == 1:
                     lhs = -lhs
             for half in range(2):
                 pltpu.matmul_acc_lhs(totals[8 * half + block], lhs, turn if block == 0 else None)
 
-        def pair(g, _):
+        def pair(channel, g, _):
             for sub in range(2):
                 chunk = 2 * g + sub
 
@@ -223,18 +226,23 @@
                     for block in range(8):
 
                         def body(sub=sub, turn=turn, block=block):
-                            matmul(1 - sub, turn, block, g if sub else lax.rem(g + pairs - 1, pairs))
+                            matmul(1 - sub, turn, block, g if sub else lax.rem(g + pairs - 1, pairs), channel)
                             for i in range(4):
-                                phases(sub, 32 * (8 * turn + block) + 8 * i, g)
+                                phases(sub, 32 * (8 * turn + block) + 8 * i, g, channel)
 
                         pl.when(g >= 0)(body)
                 out_copy(chunk, sub).start()
             return 0
 
-        lax.fori_loop(0, pairs, pair, 0)
+        for channel in range(4):
+
+            @pl.when(k == channel)
+            def _():
+                lax.fori_loop(0, pairs, functools.partial(pair, channel), 0)
+
         for turn in range(2):
             for block in range(8):
-                matmul(1, turn, block, pairs - 1)
+                matmul(1, turn, block, pairs - 1, k)
         for sub in range(2):
             out_copy(2 * pairs - 2 + sub, sub).wait()
         bright_rows[0:4] = place_ref[4:8, :128]
@@ -499,7 +507,9 @@
         compiler_params=small,
         name="solve",
     )(model_own, *tiles, place)
-    tables = [solved] + [lax.ppermute(solved, "stn", ring(s)) for s in (1, 2, 3)]
+    tables = [solved]
+    for s in (1, 2, 3):
+        tables.append(lax.ppermute(solved, "stn", ring(s)))
 
     model = pl.pallas_call(
         model_kernel,

time: 56.1 us -> 56.1 us (level)
  transfers between devices with their start and end apart: 7 -> 7, of which waited for: 2 -> 2; matrix products, arithmetic and copies ran while one was open for 0% -> 0% of each run, Pallas kernels for 28% -> 27%
where the time goes in v7:
time: 56.1 us; the launch traced here: 55.7 us
  Pallas kernels  22.6 us (40%)
  starting transfers between devices  22.4 us (40%)
  waiting for transfers between devices  8.06 us (14%)
  local copies, waits for them, and re-layouts  1.94 us (3%)
  between operations  0.71 us (1%)
    all_to_all x1, starting transfers between devices, per_device(): received = lax.all_to_all(send, 'chan', 0, 0)  13.2 us
    pallas_call x1, Pallas kernels, per_device(): pl.pallas_call(phasor_kernel, out_shape=[shape(chunks // 2, 4, n, 512, dt...  11.2 us
    ppermute x3, waiting for transfers between devices, turn(): return lax.ppermute(tile, 'stn', ring(s))  5.6 us
    ppermute x3, starting transfers between devices, turn(): return lax.ppermute(tile, 'stn', ring(s))  5.58 us
    pallas_call x1, Pallas kernels, per_device(): pl.pallas_call(model_kernel, out_shape=shape(4, 2 * rows, n), in_specs=[w...  3.86 us
    ppermute x3, starting transfers between devices, per_device(): tables.append(lax.ppermute(solved, 'stn', ring(s)))  3.63 us
    pallas_call x1, Pallas kernels, per_device(): pl.pallas_call(front_kernel, out_shape=[shape(64, 1, 5 * CAP), shape(8, n...  2.57 us
    pallas_call x1, Pallas kernels, per_device(): pl.pallas_call(solve_kernel, out_shape=shape(8, n), in_specs=[whole] * 6,...  2.56 us
  transfers between devices with their start and end apart: 7, of which 2 were waited for; matrix products, arithmetic and copies ran while one was open for 0% of the time, Pallas kernels for 27%

profile of v7, /device:TPU:1, one launch (start us, length us, event | category | flops | bytes accessed | tf_op | source)
XLA Modules:
  0.0 55.7 jit_solution(13140046156085863963)
XLA Ops:
  0.6 2.6 %front.1 = (f32[64,1,160]{2,1,0:T(1,128)}, f32[8,512]{1,0:T(8,128)}, f32[2,128,512]{2,1,0:T(8,128)}) custom-call(bf16[2,4,128,512]{3,2,1,0:T(8,128)(2,1)} %vis_ref.3, s32[512,128]{1,0:T(8,128)} %bitcast.4, f32[5,1024]{1,0:T(8,128)} %cat_hbm.1, f32[2,512]{1,0:T(2,128)} %st_hbm.1, s32[1,512]{1,0:T(1,128)} %bitcast.5, s32[1,512]{1,0:T(1,128)} %bitcast.6, ...), custom_call_target="tpu_custom_call" | custom-call | tf_op jit(solution)/shard_map/front/pallas_call | solution.py:434
  3.2 13.2 %all-to-all-start = ((f32[64,1,160]{2,1,0:T(1,128)}), f32[64,1,160]{2,1,0:T(1,128)S(1)}, u32[]{:S(2)}, u32[]{:S(2)}) async-start(f32[64,1,160]{2,1,0:T(1,128)} %get-tuple-element.14), calls=%async_computation | async-start | bytes 131072 | tf_op jit(solution)/shard_map/all_to_all | solution.py:475
  16.4 2.8 %collective-permute-start.1 = (f32[2,128,512]{2,1,0:T(8,128)}, f32[2,128,512]{2,1,0:T(8,128)S(1)}, u32[]{:S(2)}, u32[]{:S(2)}) collective-permute-start(f32[2,128,512]{2,1,0:T(8,128)} %get-tuple-element.23), channel_id=1, source_target_pairs={{0,2},{1,3},{2,0},{3,1},{4,6},{5,7},{6,4},{7,5},{8,10},{9,11},{10,... | collective-permute-start | bytes 1572872 | tf_op jit(solution)/shard_map/ppermute | solution.py:473
  19.2 0.0 copy-start
  19.2 1.2 %copy-done = bf16[2,4,128,512]{3,2,1,0:T(8,128)(2,1)S(1)} copy-done((bf16[2,4,128,512]{3,2,1,0:T(8,128)(2,1)S(1)}, bf16[2,4,128,512]{3,2,1,0:T(8,128)(2,1)}, u32[]{:S(2)}) %copy-start) | copy-done | bytes 1048600
  20.4 0.0 copy-start.2
  20.4 0.7 %copy-done.2 = f32[8,512]{1,0:T(8,128)S(1)} copy-done((f32[8,512]{1,0:T(8,128)S(1)}, f32[8,512]{1,0:T(8,128)}, u32[]{:S(2)}) %copy-start.2) | copy-done | bytes 16408
  21.1 0.1 spread.1
  21.3 0.4 collective-permute-start
  21.6 2.4 %collective-permute-start.2 = (f32[2,128,512]{2,1,0:T(8,128)S(1)}, f32[2,128,512]{2,1,0:T(8,128)S(1)}, u32[]{:S(2)}, u32[]{:S(2)}) collective-permute-start(f32[2,128,512]{2,1,0:T(8,128)S(1)} %get-tuple-element.24), channel_id=1, source_target_pairs={{0,3},{1,0},{2,1},{3,2},{4,7},{5,4},{6,5},{7,6},{8,11},{9,8},{10,9... | collective-permute-start | bytes 1572872 | tf_op jit(solution)/shard_map/ppermute | solution.py:473
  24.0 2.5 %all-to-all-done.recv_ref = f32[64,1,160]{2,1,0:T(1,128)S(1)} async-done(((f32[64,1,160]{2,1,0:T(1,128)}), f32[64,1,160]{2,1,0:T(1,128)S(1)}, u32[]{:S(2)}, u32[]{:S(2)}) %all-to-all-start) | async-done | bytes 40992 | tf_op jit(solution)/shard_map/all_to_all | solution.py:475
  26.5 11.2 %phasor.1 = (bf16[4,4,512,512]{3,2,1,0:T(8,128)(2,1)S(1)}, bf16[4,4,512,512]{3,2,1,0:T(8,128)(2,1)S(1)}, bf16[8,4,128,512]{3,2,1,0:T(8,128)(2,1)S(1)}, f32[1024,512]{1,0:T(8,128)S(1)}) custom-call(f32[64,1,160]{2,1,0:T(1,128)S(1)} %all-to-all-done.recv_ref, f32[8,512]{1,0:T(8,128)S(1)} %get-tuple-element.16.place_ref.ok_ref), custom_call_target="tpu_custom_call" | custom-call | flops 10737418240 | bytes 22020096 | tf_op jit(solution)/shard_map/phasor/pallas_call | solution.py:478
  37.7 0.0 collective-permute-done.1.v2
  37.7 5.6 %collective-permute-done.v1 = f32[2,128,512]{2,1,0:T(8,128)S(1)} collective-permute-done((f32[2,128,512]{2,1,0:T(8,128)S(1)}, f32[2,128,512]{2,1,0:T(8,128)S(1)}, u32[]{:S(2)}, u32[]{:S(2)}) %collective-permute-start) | collective-permute-done | bytes 524320 | tf_op jit(solution)/shard_map/ppermute | solution.py:473
  43.3 0.0 collective-permute-done.2.v3
  43.3 2.6 %solve.1.g0 = f32[8,512]{1,0:T(8,128)S(1)} custom-call(f32[1024,512]{1,0:T(8,128)S(1)} %get-tuple-element.20.own_ref.model_ref, f32[2,128,512]{2,1,0:T(8,128)S(1)} %get-tuple-element.21.v0, f32[2,128,512]{2,1,0:T(8,128)S(1)} %collective-permute-done.v1, f32[2,128,512]{2,1,0:T(8,128)S(1)} %collective-permute-done.1.v2, ...), custom_call_target="tpu_custom_call" | custom-call | tf_op jit(solution)/shard_map/solve/pallas_call | solution.py:501
  45.8 2.5 %collective-permute-start.5 = (f32[8,512]{1,0:T(8,128)S(1)}, f32[8,512]{1,0:T(8,128)S(1)}, u32[]{:S(2)}, u32[]{:S(2)}) collective-permute-start(f32[8,512]{1,0:T(8,128)S(1)} %solve.1.g0), channel_id=1, source_target_pairs={{0,3},{1,0},{2,1},{3,2},{4,7},{5,4},{6,5},{7,6},{8,11},{9,8},{10,9... | collective-permute-start | bytes 49160 | tf_op jit(solution)/shard_map/ppermute | solution.py:512
  48.3 0.5 collective-permute-start.4
  48.8 0.6 %collective-permute-start.3 = (f32[8,512]{1,0:T(8,128)S(1)}, f32[8,512]{1,0:T(8,128)S(1)}, u32[]{:S(2)}, u32[]{:S(2)}) collective-permute-start(f32[8,512]{1,0:T(8,128)S(1)} %solve.1.g0), channel_id=1, source_target_pairs={{0,1},{1,2},{2,3},{3,0},{4,5},{5,6},{6,7},{7,4},{8,9},{9,10},{10,1... | collective-permute-start | bytes 49160 | tf_op jit(solution)/shard_map/ppermute | solution.py:512
  49.4 0.0 copy-start.1
  49.4 3.9 %model.1.model_ref = f32[4,256,512]{2,1,0:T(8,128)S(1)} custom-call(bf16[4,4,512,512]{3,2,1,0:T(8,128)(2,1)S(1)} %get-tuple-element.17.right_even, bf16[4,4,512,512]{3,2,1,0:T(8,128)(2,1)S(1)} %get-tuple-element.18.right_odd, bf16[8,4,128,512]{3,2,1,0:T(8,128)(2,1)S(1)} %get-tuple-element.19.left_ref, f32[1024,512]{1,0:T(8,128)S(1)} %get-tuple-element.20.own_ref.model_ref, ...), custom_call_target="tpu_custom_call" | custom-call | flops 4294967296 | bytes 22020096 | tf_op jit(solution)/shard_map/model/pallas_call | solution.py:514
  53.3 0.0 collective-permute-done.5.g3
  53.3 0.0 collective-permute-done.4.g2
  53.3 0.0 collective-permute-done.3.g1
  53.3 0.0 copy-done.1
  53.4 2.3 %residual.1 = (f32[2,4,128]{2,1,0:T(4,128)}, bf16[2,4,128,512]{3,2,1,0:T(8,128)(2,1)}, f32[3,4]{1,0:T(4,128)}) custom-call(f32[4,256,512]{2,1,0:T(8,128)S(1)} %model.1.model_ref, bf16[2,4,128,512]{3,2,1,0:T(8,128)(2,1)S(1)} %copy-done.1, f32[8,512]{1,0:T(8,128)S(1)} %solve.1.g0, f32[8,512]{1,0:T(8,128)S(1)} %collective-permute-done.3.g1, ...), custom_call_target="tpu_custom_call" | custom-call | tf_op jit(solution)/shard_map/residual/pallas_call | solution.py:525
Async XLA Ops:
  3.2 23.3 %all-to-all-start = ((f32[64,1,160]{2,1,0:T(1,128)}), f32[64,1,160]{2,1,0:T(1,128)S(1)}, u32[]{:S(2)}, u32[]{:S(2)}) async-start(f32[64,1,160]{2,1,0:T(1,128)} %get-tuple-element.14), calls=%async_computation | async-start | bytes 131072 | tf_op jit(solution)/shard_map/all_to_all | solution.py:475
  16.4 21.3 %collective-permute-start.1 = (f32[2,128,512]{2,1,0:T(8,128)}, f32[2,128,512]{2,1,0:T(8,128)S(1)}, u32[]{:S(2)}, u32[]{:S(2)}) collective-permute-start(f32[2,128,512]{2,1,0:T(8,128)} %get-tuple-element.23), channel_id=1, source_target_pairs={{0,2},{1,3},{2,0},{3,1},{4,6},{5,7},{6,4},{7,5},{8,10},{9,11},{10,... | collective-permute-start | bytes 1572872 | tf_op jit(solution)/shard_map/ppermute | solution.py:473
  19.2 1.2 %copy-start = (bf16[2,4,128,512]{3,2,1,0:T(8,128)(2,1)S(1)}, bf16[2,4,128,512]{3,2,1,0:T(8,128)(2,1)}, u32[]{:S(2)}) copy-start(bf16[2,4,128,512]{3,2,1,0:T(8,128)(2,1)} %vis_ref.3) | copy-start | bytes 3145732
  20.4 0.7 %copy-start.2 = (f32[8,512]{1,0:T(8,128)S(1)}, f32[8,512]{1,0:T(8,128)}, u32[]{:S(2)}) copy-start(f32[8,512]{1,0:T(8,128)} %get-tuple-element.15.place_ref) | copy-start | bytes 49156
  21.3 22.0 %collective-permute-start = (f32[2,128,512]{2,1,0:T(8,128)S(1)}, f32[2,128,512]{2,1,0:T(8,128)S(1)}, u32[]{:S(2)}, u32[]{:S(2)}) collective-permute-start(f32[2,128,512]{2,1,0:T(8,128)S(1)} %get-tuple-element.22), channel_id=1, source_target_pairs={{0,1},{1,2},{2,3},{3,0},{4,5},{5,6},{6,7},{7,4},{8,9},{9,10},{10,1... | collective-permute-start | bytes 1572872 | tf_op jit(solution)/shard_map/ppermute | solution.py:473
  21.6 21.6 %collective-permute-start.2 = (f32[2,128,512]{2,1,0:T(8,128)S(1)}, f32[2,128,512]{2,1,0:T(8,128)S(1)}, u32[]{:S(2)}, u32[]{:S(2)}) collective-permute-start(f32[2,128,512]{2,1,0:T(8,128)S(1)} %get-tuple-element.24), channel_id=1, source_target_pairs={{0,3},{1,0},{2,1},{3,2},{4,7},{5,4},{6,5},{7,6},{8,11},{9,8},{10,9... | collective-permute-start | bytes 1572872 | tf_op jit(solution)/shard_map/ppermute | solution.py:473
  45.8 7.5 %collective-permute-start.5 = (f32[8,512]{1,0:T(8,128)S(1)}, f32[8,512]{1,0:T(8,128)S(1)}, u32[]{:S(2)}, u32[]{:S(2)}) collective-permute-start(f32[8,512]{1,0:T(8,128)S(1)} %solve.1.g0), channel_id=1, source_target_pairs={{0,3},{1,0},{2,1},{3,2},{4,7},{5,4},{6,5},{7,6},{8,11},{9,8},{10,9... | collective-permute-start | bytes 49160 | tf_op jit(solution)/shard_map/ppermute | solution.py:512
  48.3 5.0 %collective-permute-start.4 = (f32[8,512]{1,0:T(8,128)S(1)}, f32[8,512]{1,0:T(8,128)S(1)}, u32[]{:S(2)}, u32[]{:S(2)}) collective-permute-start(f32[8,512]{1,0:T(8,128)S(1)} %solve.1.g0), channel_id=1, source_target_pairs={{0,2},{1,3},{2,0},{3,1},{4,6},{5,7},{6,4},{7,5},{8,10},{9,11},{10,... | collective-permute-start | bytes 49160 | tf_op jit(solution)/shard_map/ppermute | solution.py:512
  48.8 4.5 %collective-permute-start.3 = (f32[8,512]{1,0:T(8,128)S(1)}, f32[8,512]{1,0:T(8,128)S(1)}, u32[]{:S(2)}, u32[]{:S(2)}) collective-permute-start(f32[8,512]{1,0:T(8,128)S(1)} %solve.1.g0), channel_id=1, source_target_pairs={{0,1},{1,2},{2,3},{3,0},{4,5},{5,6},{6,7},{7,4},{8,9},{9,10},{10,1... | collective-permute-start | bytes 49160 | tf_op jit(solution)/shard_map/ppermute | solution.py:512
  49.4 3.9 %copy-start.1 = (bf16[2,4,128,512]{3,2,1,0:T(8,128)(2,1)S(1)}, bf16[2,4,128,512]{3,2,1,0:T(8,128)(2,1)}, u32[]{:S(2)}) copy-start(bf16[2,4,128,512]{3,2,1,0:T(8,128)(2,1)} %vis_ref.3) | copy-start | bytes 3145732
